TPU v7x, 32 devices: a whole 2x2x4 slice. The times are simulated.
32 devices in a mesh: groups: 2 (over x), seq: 16 (over z, y, core).
Axes of the slice: x: 2, y: 2, z: 4, core: 2. Of those that a mesh axis runs over, the one named last changes fastest.
Arguments:
- proj: bfloat16 [4096, 12288], P(('groups', 'seq')), parts along dimension 0, may hold values from -6 to 6
- short_weight: float32 [7, 12288], replicated, may hold values from -2 to 2
- residues: float32 [16, 4096], replicated, may hold values from -10 to 10
- rates: float32 [16, 4096], replicated, may hold values from 0.00024414062 to 0.05
- skip: float32 [4096], replicated, may hold values from -0.75 to 0.75
- grad_out: bfloat16 [4096, 4096], P(('groups', 'seq')), parts along dimension 0, may hold values from -0.3125 to 0.3125
Outputs:
- gated_output: bfloat16 [4096, 4096], P(('groups', 'seq')), parts along dimension 0
- filter_grad: float32 [4096, 4096], P(('groups', 'seq')), parts along dimension 0
There are 2 independent parts, one for each index of `groups`. A program takes and returns all parts, laid end to end along the dimension named above; an argument that names none is the same for every part. Nothing has to cross between parts.
All inputs are finite; a program needn't handle non-finite values.
Results may differ from a plain program's by a relative error of at most 0.0085.
Values may be sent and summed in bfloat16 or wider, within the bound.
No kernel may reach another device: no remote copies, remote signals or barrier semaphores. Data moves between devices by JAX's collectives and lax.ppermute only.
A program may use at most 128 MiB of HBM per device.

v0:
```python
import math

import jax
import jax.numpy as jnp
from jax import lax
from jax.sharding import PartitionSpec as P

HIGH_PRECISION = lax.Precision.HIGH


def make_tables(devices, rows):
    length = devices * rows
    halves = jnp.arange(2, dtype=jnp.int32)
    coarse = jnp.arange(devices, dtype=jnp.int32)
    fine_pos = jnp.arange(rows, dtype=jnp.int32)
    outer_turn = (
        coarse[None, None, :] * (2 * coarse[None, :, None] + halves[:, None, None]) % (2 * devices)
    )
    outer_angle = -math.pi / devices * outer_turn.astype(jnp.float32)
    twist_turn = (
        fine_pos[None, None, :] * (2 * coarse[None, :, None] + halves[:, None, None]) % (2 * length)
    )
    twist_angle = -math.pi / length * twist_turn.astype(jnp.float32)
    inner_turn = fine_pos[:, None] * fine_pos[None, :] % rows
    inner_angle = -2.0 * math.pi / rows * inner_turn.astype(jnp.float32)
    outer_stack = jnp.stack([jnp.cos(outer_angle), jnp.sin(outer_angle)])
    inverse_outer = outer_stack * (0.5 / length)
    inner_cos = jnp.cos(inner_angle)
    inner_sin = jnp.sin(inner_angle)
    forward_inner = jnp.stack(
        [jnp.stack([inner_cos, -inner_sin]), jnp.stack([inner_sin, inner_cos])]
    )
    inverse_inner = jnp.stack(
        [jnp.stack([inner_cos, inner_sin]), jnp.stack([-inner_sin, inner_cos])]
    )
    return (
        outer_stack,
        inverse_outer,
        jnp.cos(twist_angle)[:, None],
        jnp.sin(twist_angle)[:, None],
        forward_inner,
        inverse_inner,
    )


def forward_transform(signal, tables):
    outer_stack, inverse_outer, twist_re, twist_im, forward_inner, inverse_inner = tables
    first = jnp.einsum(
        "rbkp,cpj->rbckj", outer_stack, signal.astype(jnp.float32), precision=HIGH_PRECISION
    )
    turned = jnp.stack(
        [first[0] * twist_re - first[1] * twist_im, first[0] * twist_im + first[1] * twist_re]
    )
    return jnp.einsum("rsmj,sbckj->rbckm", forward_inner, turned, precision=HIGH_PRECISION)


def inverse_transform(spectrum, tables):
    outer_stack, inverse_outer, twist_re, twist_im, forward_inner, inverse_inner = tables
    back = jnp.einsum("rsjm,sbckm->rbckj", inverse_inner, spectrum, precision=HIGH_PRECISION)
    turned = jnp.stack(
        [back[0] * twist_re + back[1] * twist_im, back[1] * twist_re - back[0] * twist_im]
    )
    return jnp.einsum("rbkp,rbckj->cpj", inverse_outer, turned, precision=HIGH_PRECISION)


def filter_spectrum(residue_local, rate_local, skip_local, devices, rows):
    length = devices * rows
    halves = jnp.arange(2, dtype=jnp.int32)[:, None, None, None]
    coarse = jnp.arange(devices, dtype=jnp.int32)[None, None, :, None]
    fine_pos = jnp.arange(rows, dtype=jnp.int32)[None, None, None, :]
    frequency = 2 * (coarse + devices * fine_pos) + halves
    half_angle = math.pi / (2 * length) * frequency.astype(jnp.float32)
    sine_half = jnp.sin(half_angle)
    sine_sq = sine_half * sine_half
    sine_full = 2.0 * sine_half * jnp.cos(half_angle)
    parity_sign = (1 - 2 * halves).astype(jnp.float32)
    local_width = residue_local.shape[1]
    kernel_re = jnp.zeros((2, local_width, devices, rows), jnp.float32)
    kernel_im = jnp.zeros((2, local_width, devices, rows), jnp.float32)
    for mode_index in range(residue_local.shape[0]):
        rate_row = rate_local[mode_index][None, :, None, None]
        amplitude = residue_local[mode_index][None, :, None, None] * jnp.sqrt(rate_row)
        decay_factor = jnp.exp(-rate_row)
        decay_gap = -jnp.expm1(-rate_row)
        tail_factor = jnp.exp(-rate_row * length)
        denominator = decay_gap * decay_gap + 4.0 * decay_factor * sine_sq
        weighting = amplitude * (1.0 - tail_factor * parity_sign) / denominator
        kernel_re = kernel_re + weighting * (decay_gap + 2.0 * decay_factor * sine_sq)
        kernel_im = kernel_im - weighting * decay_factor * sine_full
    kernel_re = kernel_re + skip_local[None, :, None, None]
    return (kernel_re, kernel_im)


def times_kernel(spectrum, kernel_re, kernel_im):
    return jnp.stack(
        [
            spectrum[0] * kernel_re - spectrum[1] * kernel_im,
            spectrum[0] * kernel_im + spectrum[1] * kernel_re,
        ]
    )


def on_device(proj, short_weight, residues, rates, skip, grad_out):
    devices = lax.axis_size("seq")
    rows = proj.shape[0]
    channels = grad_out.shape[1]
    local_width = channels // devices
    length = devices * rows
    tap_count = short_weight.shape[0]
    first_channel = lax.axis_index("seq") * local_width
    residue_local = lax.dynamic_slice_in_dim(residues, first_channel, local_width, 1)
    rate_local = lax.dynamic_slice_in_dim(rates, first_channel, local_width, 1)
    skip_local = lax.dynamic_slice_in_dim(skip, first_channel, local_width, 0)
    tables = make_tables(devices, rows)
    kernel_re, kernel_im = filter_spectrum(residue_local, rate_local, skip_local, devices, rows)
    arranged = proj.T.reshape(3, devices, local_width, 1, rows)
    streams = lax.all_to_all(arranged, "seq", split_axis=1, concat_axis=3, tiled=True).reshape(
        3, local_width, length
    )
    weight_local = lax.dynamic_slice_in_dim(
        short_weight.reshape(tap_count, 3, channels), first_channel, local_width, 2
    )
    padded = jnp.pad(streams, ((0, 0), (0, 0), (tap_count - 1, 0)))
    filtered = jnp.zeros((3, local_width, length), jnp.float32)
    for tap_index in range(tap_count):
        offset = tap_count - 1 - tap_index
        filtered = filtered + weight_local[tap_index][:, :, None] * padded[
            :, :, offset : offset + length
        ].astype(jnp.float32)
    query_part = filtered[0].reshape(local_width, devices, rows)
    mixed = (filtered[1] * filtered[2]).astype(jnp.bfloat16).reshape(local_width, devices, rows)
    cot_arranged = grad_out.T.reshape(devices, local_width, 1, rows)
    cotangent = lax.all_to_all(
        cot_arranged, "seq", split_axis=0, concat_axis=2, tiled=True
    ).reshape(local_width, devices, rows)
    mixed_spec = forward_transform(mixed, tables)
    conv = inverse_transform(times_kernel(mixed_spec, kernel_re, kernel_im), tables).astype(
        jnp.bfloat16
    )
    gated = (query_part * conv.astype(jnp.float32)).astype(jnp.bfloat16)
    gated_rows = lax.all_to_all(
        gated.reshape(1, local_width, devices, rows), "seq", split_axis=2, concat_axis=0, tiled=True
    )
    gated_output = gated_rows.reshape(channels, rows).T
    scaled = (query_part * cotangent.astype(jnp.float32)).astype(jnp.bfloat16)
    scaled_spec = forward_transform(scaled, tables)
    lag_spec = jnp.stack(
        [
            mixed_spec[0] * scaled_spec[0] + mixed_spec[1] * scaled_spec[1],
            mixed_spec[0] * scaled_spec[1] - mixed_spec[1] * scaled_spec[0],
        ]
    )
    lagged = inverse_transform(lag_spec, tables)
    lagged_rows = lax.all_to_all(
        lagged.reshape(1, local_width, devices, rows),
        "seq",
        split_axis=2,
        concat_axis=0,
        tiled=True,
    )
    filter_grad = lagged_rows.reshape(channels, rows).T
    return (gated_output, filter_grad)


def solution(mesh):
    return jax.shard_map(
        on_device,
        mesh=mesh,
        in_specs=(P(("groups", "seq"), None), P(), P(), P(), P(), P(("groups", "seq"), None)),
        out_specs=(P(("groups", "seq"), None), P(("groups", "seq"), None)),
        check_vma=False,
    )
```

profile of v0, /device:TPU:13, one launch (start us, length us, event | category | flops | bytes accessed | tf_op | source)
XLA Modules:
  0.0 335.2 jit_solution(8176572068506548456)
XLA Ops:
  0.6 3.5 %copy.85 = bf16[128,12288]{0,1:T(8,128)(2,1)S(1)} copy(bf16[128,12288]{1,0:T(8,128)(2,1)} %param.6) | data formatting | bytes 6291456 | tf_op args[0]
  4.1 1.9 copy.86
  6.0 6.7 %all-to-all-start = ((bf16[3,16,256,1,128]{4,2,3,0,1:T(8,128)(2,1)}), bf16[3,16,256,1,128]{4,2,3,0,1:T(8,128)(2,1)S(1)}, u32[]{:S(2)}, u32[]{:S(2)}) async-start(bf16[3,16,256,1,128]{4,2,3,0,1:T(8,128)(2,1)} %copy.86), calls=%async_computation | async-start | bytes 6291456 | tf_op jit(solution)/shard_map/all_to_all | solution.py:117
  12.6 0.9 fusion.59
  13.6 0.9 fusion.63
  14.5 1.0 reshape.2530
  15.5 2.3 copy.95
  18.4 1.4 dynamic-slice_bitcast_fusion.6
  19.8 1.9 exponential-minus-one_negate_fusion.15
  21.7 0.6 exponential-minus-one_negate_fusion
  22.3 0.6 broadcast_multiply_fusion
  23.5 1.3 dynamic_slice.15
  24.9 1.7 fusion.48
  26.6 0.6 exponential-minus-one_negate_fusion.2
  27.2 0.6 broadcast_multiply_fusion.2
  28.3 0.6 exponential-minus-one_negate_fusion.4
  29.0 0.6 broadcast_multiply_fusion.4
  30.1 0.6 exponential-minus-one_negate_fusion.6
  30.8 0.6 broadcast_multiply_fusion.6
  31.9 0.6 exponential-minus-one_negate_fusion.8
  32.5 0.6 broadcast_multiply_fusion.8
  33.1 0.6 broadcast_multiply_fusion.9
  33.7 0.6 exponential-minus-one_negate_fusion.10
  34.9 0.6 broadcast_multiply_fusion.11
  35.5 0.6 exponential-minus-one_negate_fusion.12
  37.8 0.6 broadcast_multiply_fusion.14
  38.5 0.7 subtract_multiply_fusion.6
  39.2 1.4 fusion.83
  40.6 1.4 fusion.81
  42.0 1.4 subtract_multiply_fusion.15
  43.5 0.7 fusion.73
  44.2 38.4 %all-to-all-done = bf16[3,16,256,1,128]{4,2,3,0,1:T(8,128)(2,1)S(1)} async-done(((bf16[3,16,256,1,128]{4,2,3,0,1:T(8,128)(2,1)}), bf16[3,16,256,1,128]{4,2,3,0,1:T(8,128)(2,1)S(1)}, u32[]{:S(2)}, u32[]{:S(2)}) %all-to-all-start) | async-done | bytes 3145760 | tf_op jit(solution)/shard_map/all_to_all | solution.py:117
  82.5 1.6 copy-done.3
  84.2 5.1 %all-to-all-start.2 = ((bf16[16,256,1,128]{3,1,2,0:T(8,128)(2,1)}), bf16[16,256,1,128]{3,1,2,0:T(8,128)(2,1)}, u32[]{:S(2)}, u32[]{:S(2)}) async-start(bf16[16,256,1,128]{3,1,2,0:T(8,128)(2,1)} %bitcast.245), calls=%async_computation.2 | async-start | bytes 2097152 | tf_op jit(solution)/shard_map/all_to_all | solution.py:133
  89.3 3.2 copy.87
  92.5 6.4 %multiply_add_fusion = f32[3,256,2048]{1,2,0:T(8,128)S(1)} fusion(bf16[3,256,2048]{1,2,0:T(8,128)(2,1)S(1)} %bitcast.240, f32[3,256]{1,0:T(4,128)} %get-tuple-element.78, f32[3,256]{1,0:T(4,128)} %get-tuple-element.73, f32[3,256]{1,0:T(4,128)} %get-tuple-element.74, f32[3,256]{1,0:T(4,128)} %get-tuple-element.75, f32[3,256]{1,0:T(4,128)} %get-tuple-element.76, ...), kind=kLoop, calls=%fused_computation.20 | loop fusion | flops 31457280 | bytes 9458688 | tf_op jit(solution)/shard_map/add | solution.py:127
  98.8 1.6 fusion.28
  100.5 2.2 copy.121
  102.7 1.8 copy.105
  104.5 6.9 %convolution_bitcast_fusion.1 = f32[2,2,256,16,128]{4,3,1,0,2:T(8,128)} fusion(bf16[256,16,128,1,1]{2,1,4,3,0:T(8,128)(2,1)} %copy.105, f32[1,2,16,16]{3,2,1,0:T(8,128)} %get-tuple-element.221, f32[1,2,16,16]{3,2,1,0:T(8,128)S(1)} %get-tuple-element.220), kind=kOutput, calls=%fused_computation.54 | convolution fusion | flops 201327616 | bytes 9441280 | tf_op jit(solution)/shard_map/rbkp,cpj->rbckj/dot_general | solution.py:48
  111.4 2.7 all-to-all-done.2
  114.1 3.7 %convolution_bitcast_fusion = f32[2,2,256,16,128]{4,3,1,0,2:T(8,128)S(1)} fusion(f32[256,16,128]{2,1,0:T(8,128)S(1)} %copy.121, bf16[16,256,1,128]{3,1,2,0:T(8,128)(2,1)} %all-to-all-done.2, f32[1,2,16,16]{3,2,1,0:T(8,128)S(1)} %copy-done.5, f32[1,2,16,16]{3,2,1,0:T(8,128)S(1)} %get-tuple-element.220), kind=kOutput, calls=%fused_computation.53 | convolution fusion | flops 202900480 | bytes 11538432 | tf_op jit(solution)/shard_map/rbkp,cpj->rbckj/dot_general | solution.py:48
  117.8 7.0 %multiply_subtract_fusion.2 = (f32[1,2,256,16,128]{4,3,1,0,2:T(8,128)}, f32[1,2,256,16,128]{4,3,1,0,2:T(8,128)}, f32[1,2,256,16,128]{4,3,1,0,2:T(8,128)}, f32[1,2,256,16,128]{4,3,1,0,2:T(8,128)}) fusion(f32[2,2,256,16,128]{4,3,1,0,2:T(8,128)S(1)} %convolution_bitcast_fusion, f32[2,16,128]{2,1,0:T(8,128)S(1)} %copy-done.9, f32[2,16,128]{2,1,0:T(8,128)S(1)} %copy-done.8, ...), kind=kLoop, calls=%fused_computation.26 | loop fusion | flops 12582912 | bytes 33587200 | tf_op jit(solution)/shard_map/sub | solution.py:52
  124.8 6.9 %maximum_bitcast_fusion = (f32[2,2,256,16,128,1]{4,3,1,0,2,5:T(8,128)S(1)}, f32[2,2,256,16,128,1]{4,3,1,0,2,5:T(8,128)S(1)}) fusion(f32[1,2,256,16,128]{4,3,1,0,2:T(8,128)} %get-tuple-element.137, f32[1,2,256,16,128]{4,3,1,0,2:T(8,128)} %get-tuple-element.138, f32[1,2,256,16,128]{4,3,1,0,2:T(8,128)} %get-tuple-element.49, ...), kind=kLoop, calls=%fused_computation | loop fusion | flops 4194304 | bytes 33554432 | tf_op jit(solution)/shard_map/stack | solution.py:51
  131.8 9.5 %fusion.25 = f32[2,2,256,16,128]{4,2,0,3,1:T(8,128)} fusion(f32[2,2,256,16,128,1]{4,3,1,0,2,5:T(8,128)S(1)} %get-tuple-element.260, f32[1,2,128,128]{3,2,1,0:T(8,128)S(1)} %get-tuple-element.130, f32[1,2,128,128]{3,2,1,0:T(8,128)S(1)} %copy-done.4), kind=kOutput, calls=%fused_computation.56 | convolution fusion | flops 3221291008 | bytes 17039360 | tf_op jit(solution)/shard_map/rsmj,sbckj->rbckm/dot_general | solution.py:54
  141.3 7.9 %fusion.22 = f32[2,2,256,16,128]{4,2,0,3,1:T(8,128)S(1)} fusion(f32[2,2,256,16,128,1]{4,3,1,0,2,5:T(8,128)S(1)} %get-tuple-element.259, f32[1,2,128,128]{3,2,1,0:T(8,128)S(1)} %get-tuple-element.130, f32[1,2,128,128]{3,2,1,0:T(8,128)S(1)} %copy-done.4), kind=kOutput, calls=%fused_computation.55 | convolution fusion | flops 3221291008 | bytes 17039360 | tf_op jit(solution)/shard_map/rsmj,sbckj->rbckm/dot_general | solution.py:54
  149.6 4.2 %multiply_add_fusion.2 = (f32[1,2,256,16,128]{4,2,0,3,1:T(8,128)}, f32[1,2,256,16,128]{4,2,0,3,1:T(8,128)}) fusion(f32[2,2,256,16,128]{4,2,0,3,1:T(8,128)S(1)} %copy-done, f32[2,2,256,16,128]{4,2,0,3,1:T(8,128)S(1)} %fusion.22), kind=kLoop, calls=%fused_computation.24 | loop fusion | flops 6291456 | bytes 25165824 | tf_op jit(solution)/shard_map/add | solution.py:149
  154.2 36.7 %multiply_subtract_fusion.4 = (f32[1,2,256,16,128]{4,2,0,3,1:T(8,128)S(1)}, f32[1,2,256,16,128]{4,2,0,3,1:T(8,128)S(1)}) fusion(f32[2,2,256,16,128]{4,2,0,3,1:T(8,128)S(1)} %fusion.22, f32[256]{0:T(256)S(1)} %bitcast.251, f32[256]{0:T(256)S(1)} %copy-done.61, f32[256]{0:T(256)} %bitcast.299, f32[2,256]{1,0:T(2,128)S(1)} %copy-done.18, f32[256]{0:T(256)S(1)} %bitcast.254, ...), kind=kLoop, calls=%fused_computation.30 | loop fusion | flops 170917888 | bytes 16925696 | tf_op jit(solution)/shard_map/sub | solution.py:97
  190.9 20.0 %multiply_add_fusion.5 = f32[1,2,256,16,128]{4,2,0,3,1:T(8,128)S(1)} fusion(f32[1,2,256,16,128]{4,2,0,3,1:T(8,128)S(1)} %get-tuple-element.13, f32[2,2,256,16,128]{4,2,0,3,1:T(8,128)S(1)} %fusion.22, f32[256]{0:T(256)S(1)} %bitcast.252, f32[256]{0:T(256)S(1)} %copy-done.61, f32[256]{0:T(256)} %bitcast.300, f32[2,256]{1,0:T(2,128)S(1)} %copy-done.18, ...), kind=kLoop, calls=%fused_computation.29 | loop fusion | flops 103809024 | bytes 16891904 | tf_op jit(solution)/shard_map/add | solution.py:98
  210.9 4.0 %maximum_bitcast_fusion.3 = f32[2,2,256,16,128,1]{4,2,0,3,1,5:T(8,128)S(1)} fusion(f32[1,2,256,16,128]{4,2,0,3,1:T(8,128)} %get-tuple-element.45, f32[1,2,256,16,128]{4,2,0,3,1:T(8,128)} %get-tuple-element.44), kind=kLoop, calls=%fused_computation.7 | loop fusion | flops 2097152 | bytes 16777216 | tf_op jit(solution)/shard_map/stack | solution.py:147
  214.9 3.9 %maximum_bitcast_fusion.1 = f32[2,2,256,16,128,1]{4,2,0,3,1,5:T(8,128)} fusion(f32[1,2,256,16,128]{4,2,0,3,1:T(8,128)S(1)} %multiply_add_fusion.5, f32[1,2,256,16,128]{4,2,0,3,1:T(8,128)S(1)} %get-tuple-element.12), kind=kLoop, calls=%fused_computation.1 | loop fusion | flops 2097152 | bytes 16777216 | tf_op jit(solution)/shard_map/stack | solution.py:95
  218.8 9.0 %fusion.19 = f32[2,2,256,16,128]{4,3,1,0,2:T(8,128)S(1)} fusion(f32[2,2,256,16,128,1]{4,2,0,3,1,5:T(8,128)S(1)} %maximum_bitcast_fusion.3, f32[1,2,128,128]{3,2,1,0:T(8,128)S(1)} %get-tuple-element.134, f32[1,2,128,128]{3,2,1,0:T(8,128)S(1)} %get-tuple-element.129), kind=kOutput, calls=%fused_computation.52 | convolution fusion | flops 3221291008 | bytes 17039360 | tf_op jit(solution)/shard_map/rsjm,sbckm->rbckj/dot_general | solution.py:59
  227.9 9.2 %fusion.16 = f32[2,2,256,16,128]{4,3,1,0,2:T(8,128)S(1)} fusion(f32[2,2,256,16,128,1]{4,2,0,3,1,5:T(8,128)S(1)} %copy-done.2, f32[1,2,128,128]{3,2,1,0:T(8,128)S(1)} %get-tuple-element.134, f32[1,2,128,128]{3,2,1,0:T(8,128)S(1)} %get-tuple-element.129), kind=kOutput, calls=%fused_computation.51 | convolution fusion | flops 3221291008 | bytes 17039360 | tf_op jit(solution)/shard_map/rsjm,sbckm->rbckj/dot_general | solution.py:59
  237.1 7.0 %multiply_add_fusion.1 = (f32[1,2,256,16,128]{4,3,1,0,2:T(8,128)}, f32[1,2,256,16,128]{4,3,1,0,2:T(8,128)}, f32[1,2,256,16,128]{4,3,1,0,2:T(8,128)}, f32[1,2,256,16,128]{4,3,1,0,2:T(8,128)}) fusion(f32[2,2,256,16,128]{4,3,1,0,2:T(8,128)S(1)} %fusion.19, f32[2,16,128]{2,1,0:T(8,128)S(1)} %copy-done.9, f32[2,16,128]{2,1,0:T(8,128)S(1)} %copy-done.8, ...), kind=kLoop, calls=%fused_computation.22 | loop fusion | flops 12582912 | bytes 33587200 | tf_op jit(solution)/shard_map/add | solution.py:61
  244.1 5.6 %fusion.38 = bf16[1,256,16,128]{3,2,1,0:T(8,128)(2,1)S(1)} fusion(f32[256,16,128]{2,1,0:T(8,128)S(1)} %copy.121, f32[1,2,256,16,128]{4,3,1,0,2:T(8,128)} %get-tuple-element.135, f32[1,2,256,16,128]{4,3,1,0,2:T(8,128)} %get-tuple-element.136, f32[1,2,16,16]{3,2,1,0:T(8,128)S(1)} %copy-done.5, f32[1,2,16,16]{3,2,1,0:T(8,128)S(1)} %get-tuple-element.220), kind=kOutput, calls=%fused_computation.69 | convolution fusion | flops 205522944 | bytes 11538432 | tf_op jit(solution)/shard_map/rbkp,rbckj->cpj/dot_general | solution.py:63
  249.7 1.2 copy.94
  250.9 5.2 %all-to-all-start.1 = ((bf16[1,256,16,128]{3,1,0,2:T(8,128)(2,1)}), bf16[1,256,16,128]{3,1,0,2:T(8,128)(2,1)S(1)}, u32[]{:S(2)}, u32[]{:S(2)}) async-start(bf16[1,256,16,128]{3,1,0,2:T(8,128)(2,1)} %copy.94), calls=%async_computation.1 | async-start | bytes 2097152 | tf_op jit(solution)/shard_map/all_to_all | solution.py:141
  256.1 4.7 %fusion.31 = f32[1,256,16,128]{3,2,1,0:T(8,128)S(1)} fusion(f32[1,2,256,16,128]{4,3,1,0,2:T(8,128)} %get-tuple-element.47, f32[1,2,256,16,128]{4,3,1,0,2:T(8,128)} %get-tuple-element.46, f32[1,2,16,16]{3,2,1,0:T(8,128)S(1)} %copy-done.6, f32[1,2,16,16]{3,2,1,0:T(8,128)S(1)} %get-tuple-element.220), kind=kOutput, calls=%fused_computation.68 | convolution fusion | flops 203425792 | bytes 10489856 | tf_op jit(solution)/shard_map/rbkp,rbckj->cpj/dot_general | solution.py:63
  260.8 2.0 copy.102
  262.8 18.1 %all-to-all-done.1 = bf16[1,256,16,128]{3,1,0,2:T(8,128)(2,1)S(1)} async-done(((bf16[1,256,16,128]{3,1,0,2:T(8,128)(2,1)}), bf16[1,256,16,128]{3,1,0,2:T(8,128)(2,1)S(1)}, u32[]{:S(2)}, u32[]{:S(2)}) %all-to-all-start.1) | async-done | bytes 1048608 | tf_op jit(solution)/shard_map/all_to_all | solution.py:141
  280.9 4.8 %all-to-all-start.3 = ((f32[1,256,16,128]{3,1,0,2:T(8,128)}), f32[1,256,16,128]{3,1,0,2:T(8,128)S(1)}, u32[]{:S(2)}, u32[]{:S(2)}) async-start(f32[1,256,16,128]{3,1,0,2:T(8,128)} %copy.102), calls=%async_computation.3 | async-start | bytes 4194304 | tf_op jit(solution)/shard_map/all_to_all | solution.py:154
  285.7 1.3 copy.103
  287.0 46.1 %all-to-all-done.3 = f32[1,256,16,128]{3,1,0,2:T(8,128)S(1)} async-done(((f32[1,256,16,128]{3,1,0,2:T(8,128)}), f32[1,256,16,128]{3,1,0,2:T(8,128)S(1)}, u32[]{:S(2)}, u32[]{:S(2)}) %all-to-all-start.3) | async-done | bytes 2097184 | tf_op jit(solution)/shard_map/all_to_all | solution.py:154
  333.1 1.8 copy.104
  (146 shorter events, 5.4 us)
Async XLA Ops:
  6.0 8.5 %copy-start.7 = (f32[7,12288]{1,0:T(8,128)S(1)}, f32[7,12288]{1,0:T(8,128)}, u32[]{:S(2)}) copy-start(f32[7,12288]{1,0:T(8,128)} %param.7) | copy-start | bytes 1032196
  6.0 76.5 %all-to-all-start = ((bf16[3,16,256,1,128]{4,2,3,0,1:T(8,128)(2,1)}), bf16[3,16,256,1,128]{4,2,3,0,1:T(8,128)(2,1)S(1)}, u32[]{:S(2)}, u32[]{:S(2)}) async-start(bf16[3,16,256,1,128]{4,2,3,0,1:T(8,128)(2,1)} %copy.86), calls=%async_computation | async-start | bytes 6291456 | tf_op jit(solution)/shard_map/all_to_all | solution.py:117
  14.5 24.0 %copy-start.66 = (f32[2]{0:T(128)}, f32[2]{0:T(128)S(1)}, u32[]{:S(2)}) copy-start(f32[2]{0:T(128)S(1)} %subtract_convert_fusion) | copy-start | bytes 28
  21.7 21.7 %copy-start.28 = (f32[1,256]{1,0:T(1,128)}, f32[1,256]{1,0:T(1,128)S(1)}, u32[]{:S(2)}) copy-start(f32[1,256]{1,0:T(1,128)S(1)} %get-tuple-element.81) | copy-start | bytes 3076
  27.2 10.7 %copy-start.34 = (f32[1,256]{1,0:T(1,128)}, f32[1,256]{1,0:T(1,128)S(1)}, u32[]{:S(2)}) copy-start(f32[1,256]{1,0:T(1,128)S(1)} %get-tuple-element.204) | copy-start | bytes 3076
  27.2 10.7 %copy-start.36 = (f32[1,256]{1,0:T(1,128)}, f32[1,256]{1,0:T(1,128)S(1)}, u32[]{:S(2)}) copy-start(f32[1,256]{1,0:T(1,128)S(1)} %get-tuple-element.242) | copy-start | bytes 3076
  29.0 14.4 %copy-start.38 = (f32[1,256]{1,0:T(1,128)}, f32[1,256]{1,0:T(1,128)S(1)}, u32[]{:S(2)}) copy-start(f32[1,256]{1,0:T(1,128)S(1)} %get-tuple-element.194) | copy-start | bytes 3076
  29.0 14.4 %copy-start.40 = (f32[1,256]{1,0:T(1,128)}, f32[1,256]{1,0:T(1,128)S(1)}, u32[]{:S(2)}) copy-start(f32[1,256]{1,0:T(1,128)S(1)} %get-tuple-element.245) | copy-start | bytes 3076
  30.8 12.6 %copy-start.42 = (f32[1,256]{1,0:T(1,128)}, f32[1,256]{1,0:T(1,128)S(1)}, u32[]{:S(2)}) copy-start(f32[1,256]{1,0:T(1,128)S(1)} %get-tuple-element.184) | copy-start | bytes 3076
  30.8 12.6 %copy-start.44 = (f32[1,256]{1,0:T(1,128)}, f32[1,256]{1,0:T(1,128)S(1)}, u32[]{:S(2)}) copy-start(f32[1,256]{1,0:T(1,128)S(1)} %get-tuple-element.248) | copy-start | bytes 3076
  32.5 10.9 %copy-start.46 = (f32[1,256]{1,0:T(1,128)}, f32[1,256]{1,0:T(1,128)S(1)}, u32[]{:S(2)}) copy-start(f32[1,256]{1,0:T(1,128)S(1)} %get-tuple-element.174) | copy-start | bytes 3076
  32.5 10.9 %copy-start.48 = (f32[1,256]{1,0:T(1,128)}, f32[1,256]{1,0:T(1,128)S(1)}, u32[]{:S(2)}) copy-start(f32[1,256]{1,0:T(1,128)S(1)} %get-tuple-element.251) | copy-start | bytes 3076
  34.3 9.1 %copy-start.50 = (f32[1,256]{1,0:T(1,128)}, f32[1,256]{1,0:T(1,128)S(1)}, u32[]{:S(2)}) copy-start(f32[1,256]{1,0:T(1,128)S(1)} %get-tuple-element.164) | copy-start | bytes 3076
  34.3 9.1 %copy-start.52 = (f32[1,256]{1,0:T(1,128)}, f32[1,256]{1,0:T(1,128)S(1)}, u32[]{:S(2)}) copy-start(f32[1,256]{1,0:T(1,128)S(1)} %get-tuple-element.254) | copy-start | bytes 3076
  36.1 7.3 %copy-start.54 = (f32[1,256]{1,0:T(1,128)}, f32[1,256]{1,0:T(1,128)S(1)}, u32[]{:S(2)}) copy-start(f32[1,256]{1,0:T(1,128)S(1)} %get-tuple-element.154) | copy-start | bytes 3076
  36.1 7.3 %copy-start.56 = (f32[1,256]{1,0:T(1,128)}, f32[1,256]{1,0:T(1,128)S(1)}, u32[]{:S(2)}) copy-start(f32[1,256]{1,0:T(1,128)S(1)} %get-tuple-element.257) | copy-start | bytes 3076
  37.8 5.6 %copy-start.58 = (f32[1,256]{1,0:T(1,128)}, f32[1,256]{1,0:T(1,128)S(1)}, u32[]{:S(2)}) copy-start(f32[1,256]{1,0:T(1,128)S(1)} %get-tuple-element.144) | copy-start | bytes 3076
  84.2 29.9 %all-to-all-start.2 = ((bf16[16,256,1,128]{3,1,2,0:T(8,128)(2,1)}), bf16[16,256,1,128]{3,1,2,0:T(8,128)(2,1)}, u32[]{:S(2)}, u32[]{:S(2)}) async-start(bf16[16,256,1,128]{3,1,2,0:T(8,128)(2,1)} %bitcast.245), calls=%async_computation.2 | async-start | bytes 2097152 | tf_op jit(solution)/shard_map/all_to_all | solution.py:133
  104.5 9.6 %copy-start.5 = (f32[1,2,16,16]{3,2,1,0:T(8,128)S(1)}, f32[1,2,16,16]{3,2,1,0:T(8,128)}, u32[]{:S(2)}) copy-start(f32[1,2,16,16]{3,2,1,0:T(8,128)} %get-tuple-element.221) | copy-start | bytes 6148
  111.4 6.4 %copy-start.8 = (f32[2,16,128]{2,1,0:T(8,128)S(1)}, f32[2,16,128]{2,1,0:T(8,128)}, u32[]{:S(2)}) copy-start(f32[2,16,128]{2,1,0:T(8,128)} %get-tuple-element.218) | copy-start | bytes 49156
  111.4 6.4 %copy-start.9 = (f32[2,16,128]{2,1,0:T(8,128)S(1)}, f32[2,16,128]{2,1,0:T(8,128)}, u32[]{:S(2)}) copy-start(f32[2,16,128]{2,1,0:T(8,128)} %get-tuple-element.219) | copy-start | bytes 49156
  124.8 6.9 %copy-start.4 = (f32[1,2,128,128]{3,2,1,0:T(8,128)S(1)}, f32[1,2,128,128]{3,2,1,0:T(8,128)}, u32[]{:S(2)}) copy-start(f32[1,2,128,128]{3,2,1,0:T(8,128)} %get-tuple-element.133) | copy-start | bytes 393220
  141.3 7.9 %copy-start = (f32[2,2,256,16,128]{4,2,0,3,1:T(8,128)S(1)}, f32[2,2,256,16,128]{4,2,0,3,1:T(8,128)}, u32[]{:S(2)}) copy-start(f32[2,2,256,16,128]{4,2,0,3,1:T(8,128)} %fusion.25) | copy-start | bytes 25165828
  149.2 4.6 %copy-start.10 = (f32[2,16,128]{2,1,0:T(8,128)S(1)}, f32[2,16,128]{2,1,0:T(8,128)}, u32[]{:S(2)}) copy-start(f32[2,16,128]{2,1,0:T(8,128)} %get-tuple-element.139) | copy-start | bytes 49156
  149.2 4.6 %copy-start.11 = (f32[2,16,128]{2,1,0:T(8,128)S(1)}, f32[2,16,128]{2,1,0:T(8,128)}, u32[]{:S(2)}) copy-start(f32[2,16,128]{2,1,0:T(8,128)} %get-tuple-element.140) | copy-start | bytes 49156
  149.2 4.6 %copy-start.12 = (f32[2,256]{1,0:T(2,128)S(1)}, f32[2,256]{1,0:T(2,128)}, u32[]{:S(2)}) copy-start(f32[2,256]{1,0:T(2,128)} %get-tuple-element.231) | copy-start | bytes 6148
  149.2 4.6 %copy-start.13 = (f32[2,256]{1,0:T(2,128)S(1)}, f32[2,256]{1,0:T(2,128)}, u32[]{:S(2)}) copy-start(f32[2,256]{1,0:T(2,128)} %get-tuple-element.232) | copy-start | bytes 6148
  149.2 4.6 %copy-start.14 = (f32[2,256]{1,0:T(2,128)S(1)}, f32[2,256]{1,0:T(2,128)}, u32[]{:S(2)}) copy-start(f32[2,256]{1,0:T(2,128)} %get-tuple-element.233) | copy-start | bytes 6148
  149.2 4.6 %copy-start.15 = (f32[2,256]{1,0:T(2,128)S(1)}, f32[2,256]{1,0:T(2,128)}, u32[]{:S(2)}) copy-start(f32[2,256]{1,0:T(2,128)} %get-tuple-element.234) | copy-start | bytes 6148
  149.2 4.6 %copy-start.16 = (f32[2,256]{1,0:T(2,128)S(1)}, f32[2,256]{1,0:T(2,128)}, u32[]{:S(2)}) copy-start(f32[2,256]{1,0:T(2,128)} %get-tuple-element.235) | copy-start | bytes 6148
  149.2 4.6 %copy-start.17 = (f32[2,256]{1,0:T(2,128)S(1)}, f32[2,256]{1,0:T(2,128)}, u32[]{:S(2)}) copy-start(f32[2,256]{1,0:T(2,128)} %get-tuple-element.236) | copy-start | bytes 6148
  149.3 4.6 %copy-start.18 = (f32[2,256]{1,0:T(2,128)S(1)}, f32[2,256]{1,0:T(2,128)}, u32[]{:S(2)}) copy-start(f32[2,256]{1,0:T(2,128)} %get-tuple-element.237) | copy-start | bytes 6148
  149.3 4.6 %copy-start.19 = (f32[2,256]{1,0:T(2,128)S(1)}, f32[2,256]{1,0:T(2,128)}, u32[]{:S(2)}) copy-start(f32[2,256]{1,0:T(2,128)} %get-tuple-element.222) | copy-start | bytes 6148
  149.3 4.6 %copy-start.20 = (f32[2,256]{1,0:T(2,128)S(1)}, f32[2,256]{1,0:T(2,128)}, u32[]{:S(2)}) copy-start(f32[2,256]{1,0:T(2,128)} %get-tuple-element.223) | copy-start | bytes 6148
  149.3 4.6 %copy-start.21 = (f32[2,256]{1,0:T(2,128)S(1)}, f32[2,256]{1,0:T(2,128)}, u32[]{:S(2)}) copy-start(f32[2,256]{1,0:T(2,128)} %get-tuple-element.224) | copy-start | bytes 6148
  149.3 4.6 %copy-start.22 = (f32[2,256]{1,0:T(2,128)S(1)}, f32[2,256]{1,0:T(2,128)}, u32[]{:S(2)}) copy-start(f32[2,256]{1,0:T(2,128)} %get-tuple-element.225) | copy-start | bytes 6148
  149.3 4.6 %copy-start.23 = (f32[2,256]{1,0:T(2,128)S(1)}, f32[2,256]{1,0:T(2,128)}, u32[]{:S(2)}) copy-start(f32[2,256]{1,0:T(2,128)} %get-tuple-element.226) | copy-start | bytes 6148
  149.3 4.6 %copy-start.24 = (f32[2,256]{1,0:T(2,128)S(1)}, f32[2,256]{1,0:T(2,128)}, u32[]{:S(2)}) copy-start(f32[2,256]{1,0:T(2,128)} %get-tuple-element.227) | copy-start | bytes 6148
  149.3 4.6 %copy-start.25 = (f32[2,256]{1,0:T(2,128)S(1)}, f32[2,256]{1,0:T(2,128)}, u32[]{:S(2)}) copy-start(f32[2,256]{1,0:T(2,128)} %get-tuple-element.228) | copy-start | bytes 6148
  149.3 4.6 %copy-start.26 = (f32[2,256]{1,0:T(2,128)S(1)}, f32[2,256]{1,0:T(2,128)}, u32[]{:S(2)}) copy-start(f32[2,256]{1,0:T(2,128)} %get-tuple-element.229) | copy-start | bytes 6148
  149.3 4.6 %copy-start.27 = (f32[2,256]{1,0:T(2,128)S(1)}, f32[2,256]{1,0:T(2,128)}, u32[]{:S(2)}) copy-start(f32[2,256]{1,0:T(2,128)} %get-tuple-element.230) | copy-start | bytes 6148
  149.4 4.6 %copy-start.29 = (f32[1,256]{1,0:T(1,128)S(1)}, f32[1,256]{1,0:T(1,128)}, u32[]{:S(2)}) copy-start(f32[1,256]{1,0:T(1,128)} %copy-done.28) | copy-start | bytes 3076
  149.4 4.6 %copy-start.31 = (f32[1,256]{1,0:T(1,128)S(1)}, f32[1,256]{1,0:T(1,128)}, u32[]{:S(2)}) copy-start(f32[1,256]{1,0:T(1,128)} %copy-done.30) | copy-start | bytes 3076
  149.4 4.6 %copy-start.33 = (f32[1,256]{1,0:T(1,128)S(1)}, f32[1,256]{1,0:T(1,128)}, u32[]{:S(2)}) copy-start(f32[1,256]{1,0:T(1,128)} %copy-done.32) | copy-start | bytes 3076
  149.4 4.6 %copy-start.35 = (f32[1,256]{1,0:T(1,128)S(1)}, f32[1,256]{1,0:T(1,128)}, u32[]{:S(2)}) copy-start(f32[1,256]{1,0:T(1,128)} %copy-done.34) | copy-start | bytes 3076
  149.4 4.6 %copy-start.37 = (f32[1,256]{1,0:T(1,128)S(1)}, f32[1,256]{1,0:T(1,128)}, u32[]{:S(2)}) copy-start(f32[1,256]{1,0:T(1,128)} %copy-done.36) | copy-start | bytes 3076
  149.4 4.6 %copy-start.39 = (f32[1,256]{1,0:T(1,128)S(1)}, f32[1,256]{1,0:T(1,128)}, u32[]{:S(2)}) copy-start(f32[1,256]{1,0:T(1,128)} %copy-done.38) | copy-start | bytes 3076
  149.4 4.6 %copy-start.41 = (f32[1,256]{1,0:T(1,128)S(1)}, f32[1,256]{1,0:T(1,128)}, u32[]{:S(2)}) copy-start(f32[1,256]{1,0:T(1,128)} %copy-done.40) | copy-start | bytes 3076
  149.4 4.6 %copy-start.43 = (f32[1,256]{1,0:T(1,128)S(1)}, f32[1,256]{1,0:T(1,128)}, u32[]{:S(2)}) copy-start(f32[1,256]{1,0:T(1,128)} %copy-done.42) | copy-start | bytes 3076
  149.4 4.6 %copy-start.45 = (f32[1,256]{1,0:T(1,128)S(1)}, f32[1,256]{1,0:T(1,128)}, u32[]{:S(2)}) copy-start(f32[1,256]{1,0:T(1,128)} %copy-done.44) | copy-start | bytes 3076
  149.4 4.6 %copy-start.47 = (f32[1,256]{1,0:T(1,128)S(1)}, f32[1,256]{1,0:T(1,128)}, u32[]{:S(2)}) copy-start(f32[1,256]{1,0:T(1,128)} %copy-done.46) | copy-start | bytes 3076
  149.5 4.6 %copy-start.49 = (f32[1,256]{1,0:T(1,128)S(1)}, f32[1,256]{1,0:T(1,128)}, u32[]{:S(2)}) copy-start(f32[1,256]{1,0:T(1,128)} %copy-done.48) | copy-start | bytes 3076
  149.5 4.6 %copy-start.51 = (f32[1,256]{1,0:T(1,128)S(1)}, f32[1,256]{1,0:T(1,128)}, u32[]{:S(2)}) copy-start(f32[1,256]{1,0:T(1,128)} %copy-done.50) | copy-start | bytes 3076
  149.5 4.6 %copy-start.53 = (f32[1,256]{1,0:T(1,128)S(1)}, f32[1,256]{1,0:T(1,128)}, u32[]{:S(2)}) copy-start(f32[1,256]{1,0:T(1,128)} %copy-done.52) | copy-start | bytes 3076
  149.5 4.6 %copy-start.55 = (f32[1,256]{1,0:T(1,128)S(1)}, f32[1,256]{1,0:T(1,128)}, u32[]{:S(2)}) copy-start(f32[1,256]{1,0:T(1,128)} %copy-done.54) | copy-start | bytes 3076
  149.5 4.6 %copy-start.57 = (f32[1,256]{1,0:T(1,128)S(1)}, f32[1,256]{1,0:T(1,128)}, u32[]{:S(2)}) copy-start(f32[1,256]{1,0:T(1,128)} %copy-done.56) | copy-start | bytes 3076
  149.5 4.6 %copy-start.59 = (f32[1,256]{1,0:T(1,128)S(1)}, f32[1,256]{1,0:T(1,128)}, u32[]{:S(2)}) copy-start(f32[1,256]{1,0:T(1,128)} %copy-done.58) | copy-start | bytes 3076
  149.5 4.6 %copy-start.60 = (f32[1,256]{1,0:T(1,128)S(1)}, f32[1,256]{1,0:T(1,128)}, u32[]{:S(2)}) copy-start(f32[1,256]{1,0:T(1,128)} %get-tuple-element.80) | copy-start | bytes 3076
  149.5 4.6 %copy-start.61 = (f32[256]{0:T(256)S(1)}, f32[256]{0:T(256)}, u32[]{:S(2)}) copy-start(f32[256]{0:T(256)} %get-tuple-element.217) | copy-start | bytes 3076
  154.2 36.7 %copy-start.65 = (f32[256]{0:T(256)S(1)}, f32[256]{0:T(256)}, u32[]{:S(2)}) copy-start(f32[256]{0:T(256)} %get-tuple-element.197) | copy-start | bytes 3076
  218.8 9.0 %copy-start.2 = (f32[2,2,256,16,128,1]{4,2,0,3,1,5:T(8,128)S(1)}, f32[2,2,256,16,128,1]{4,2,0,3,1,5:T(8,128)}, u32[]{:S(2)}) copy-start(f32[2,2,256,16,128,1]{4,2,0,3,1,5:T(8,128)} %maximum_bitcast_fusion.1) | copy-start | bytes 25165828
  249.7 6.4 %copy-start.6 = (f32[1,2,16,16]{3,2,1,0:T(8,128)S(1)}, f32[1,2,16,16]{3,2,1,0:T(8,128)}, u32[]{:S(2)}) copy-start(f32[1,2,16,16]{3,2,1,0:T(8,128)} %get-tuple-element.221) | copy-start | bytes 6148
  250.9 29.9 %all-to-all-start.1 = ((bf16[1,256,16,128]{3,1,0,2:T(8,128)(2,1)}), bf16[1,256,16,128]{3,1,0,2:T(8,128)(2,1)S(1)}, u32[]{:S(2)}, u32[]{:S(2)}) async-start(bf16[1,256,16,128]{3,1,0,2:T(8,128)(2,1)} %copy.94), calls=%async_computation.1 | async-start | bytes 2097152 | tf_op jit(solution)/shard_map/all_to_all | solution.py:141
  280.9 52.2 %all-to-all-start.3 = ((f32[1,256,16,128]{3,1,0,2:T(8,128)}), f32[1,256,16,128]{3,1,0,2:T(8,128)S(1)}, u32[]{:S(2)}, u32[]{:S(2)}) async-start(f32[1,256,16,128]{3,1,0,2:T(8,128)} %copy.102), calls=%async_computation.3 | async-start | bytes 4194304 | tf_op jit(solution)/shard_map/all_to_all | solution.py:154
  (7 other events, 24.3 us)
where the time goes:
time: 339 us; the launch traced here: 335 us
  other arithmetic  123 us (36%)
  waiting for transfers between devices  105 us (31%)
  matrix products  56.5 us (17%)
  local copies, waits for them, and re-layouts  26.8 us (8%)
  starting transfers between devices  21.7 us (6%)
    all_to_all x1, waiting for transfers between devices, on_device(): lax.all_to_all(lagged.reshape(1, local_width, devices, rows), 'seq', spli...  46.1 us
    all_to_all x1, waiting for transfers between devices, on_device(): lax.all_to_all(arranged, 'seq', split_axis=1, concat_axis=3, tiled=True)  38.4 us
    sub x1, other arithmetic, times_kernel(): spectrum[0] * kernel_re - spectrum[1] * kernel_im  36.7 us
    add x1, other arithmetic, times_kernel(): spectrum[0] * kernel_im + spectrum[1] * kernel_re  20 us
    dot_general x2, matrix products, inverse_transform(): jnp.einsum('rsjm,sbckm->rbckj', inverse_inner, spectrum, precision=HIGH_P...  18.3 us
    all_to_all x1, waiting for transfers between devices, on_device(): lax.all_to_all(gated.reshape(1, local_width, devices, rows), 'seq', split...  18.1 us
    dot_general x2, matrix products, forward_transform(): jnp.einsum('rsmj,sbckj->rbckm', forward_inner, turned, precision=HIGH_PRE...  17.4 us
    unnamed x138, local copies, waits for them, and re-layouts  10.8 us
  transfers between devices with their start and end apart: 4, of which 4 were waited for; matrix products, arithmetic and copies ran while one was open for 18% of the time, Pallas kernels for 0%

commit v1 on v0

--- a/solution.py
+++ b/solution.py
@@ -1,11 +1,17 @@
+import functools
 import math
 
 import jax
 import jax.numpy as jnp
 from jax import lax
+from jax.experimental import pallas as pl
+from jax.experimental.pallas import tpu as pltpu
 from jax.sharding import PartitionSpec as P
 
 HIGH_PRECISION = lax.Precision.HIGH
+LANES = 128
+HALO = 8
+FINE_PRODUCT = 256
 
 
 def make_tables(devices, rows):
@@ -162,9 +168,483 @@
     return (gated_output, filter_grad)
 
 
+def split_pair(value):
+    high = value.astype(jnp.bfloat16)
+    low = (value - high.astype(jnp.float32)).astype(jnp.bfloat16)
+    return (high, low)
+
+
+def split_outside(value):
+    high = lax.reduce_precision(value, 8, 7)
+    return (high.astype(jnp.bfloat16), (value - high).astype(jnp.bfloat16))
+
+
+def dot32(left, right):
+    return jnp.dot(left, right, preferred_element_type=jnp.float32)
+
+
+def turn(numerator, denominator):
+    angle = (2.0 * math.pi / denominator) * (numerator % denominator).astype(jnp.float32)
+    return (jnp.cos(angle), jnp.sin(angle))
+
+
+def spectral_tables(devices, rows, zero):
+    fine = FINE_PRODUCT // devices
+    coarse = jnp.arange(devices, dtype=jnp.int32) + zero
+    place = jnp.arange(rows, dtype=jnp.int32) + zero
+    base_cos, base_sin = turn(place[:, None] * place[None, :], rows)
+    twist_cos, twist_sin = turn((2 * coarse[:, None] + 1) * place[None, :], 4 * devices * rows)
+    cos = base_cos[None] * twist_cos[:, None, :] - base_sin[None] * twist_sin[:, None, :]
+    sin = base_sin[None] * twist_cos[:, None, :] + base_cos[None] * twist_sin[:, None, :]
+    forward = jnp.concatenate(
+        [jnp.concatenate([cos, sin], axis=2), jnp.concatenate([-sin, cos], axis=2)], axis=1
+    )
+    cos_t = cos.transpose(0, 2, 1)
+    sin_t = sin.transpose(0, 2, 1)
+    backward = jnp.concatenate(
+        [jnp.concatenate([cos_t, -sin_t], axis=2), jnp.concatenate([sin_t, cos_t], axis=2)], axis=1
+    )
+    outer_cos, outer_sin = turn((2 * coarse[:, None] + 1) * coarse[None, :], 4 * devices)
+    eye = jnp.eye(fine, dtype=jnp.float32)
+    pair = jnp.stack([outer_cos, -outer_sin], axis=1)
+    outer_forward = (pair[:, :, None, :, None] * eye[None, None, :, None, :]).reshape(
+        2 * FINE_PRODUCT, FINE_PRODUCT
+    )
+    back_pair = pair.transpose(2, 0, 1) * (1.0 / (devices * rows))
+    outer_backward = (back_pair[:, None, :, :, None] * eye[None, :, None, None, :]).reshape(
+        FINE_PRODUCT, 2 * FINE_PRODUCT
+    )
+    return tuple(
+        jnp.concatenate(split_outside(table), axis=-2)
+        for table in (forward, backward, outer_forward, outer_backward)
+    )
+
+
+def mix_body(where, query_in, key_in, value_in, before_q, before_k, before_v, weight_q, weight_k, weight_v, cot, sent, query_out, mixed_out, padded):
+    taps = weight_q.shape[0]
+    rows = query_in.shape[0]
+    tail = before_q.shape[0]
+    chip, core = where[0], where[1]
+    streams = ((query_in, before_q, weight_q), (key_in, before_k, weight_k), (value_in, before_v, weight_v))
+    for index, (block, before, _) in enumerate(streams):
+        padded[index, :tail, :] = before[...].astype(jnp.float32)
+        padded[index, tail:, :] = block[...].astype(jnp.float32)
+    for piece in range(query_in.shape[1] // LANES):
+        lanes = slice(piece * LANES, (piece + 1) * LANES)
+        filtered = []
+        for index, (_, _, weight) in enumerate(streams):
+            total = None
+            for tap in range(taps):
+                term = weight[tap : tap + 1, lanes] * padded[index, tail - tap : tail - tap + rows, lanes]
+                total = term if total is None else total + term
+            filtered.append(total)
+        mixed = (filtered[1] * filtered[2]).astype(jnp.bfloat16)
+        scaled = (filtered[0] * cot[:, lanes].astype(jnp.float32)).astype(jnp.bfloat16)
+        query_out[:, lanes] = filtered[0]
+        mixed_out[:, lanes] = mixed
+        side = (piece % 2) ^ core
+        slot = (piece // 2) ^ (chip % 2)
+        sent[side, slot, :, :LANES] = mixed
+        sent[side, slot, :, LANES:] = scaled
+
+
+def mix_streams(where, proj, before, short_weight, grad_out, chunk, chunks, devices):
+    rows, channels = grad_out.shape
+    taps = short_weight.shape[0]
+    tail = before.shape[0]
+    chips = devices // 2
+    step = 4 * LANES
+    steps = channels // chunks // step
+    base = chunk * steps
+    stride = channels // step
+
+    def stream_spec(height, stream):
+        return pl.BlockSpec((height, step), lambda g, w, s=stream: (0, s * stride + base + g))
+
+    return pl.pallas_call(
+        mix_body,
+        grid_spec=pltpu.PrefetchScalarGridSpec(
+            num_scalar_prefetch=1,
+            grid=(steps,),
+            in_specs=[stream_spec(rows, s) for s in range(3)]
+            + [stream_spec(tail, s) for s in range(3)]
+            + [stream_spec(taps, s) for s in range(3)]
+            + [pl.BlockSpec((rows, step), lambda g, w: (0, base + g))],
+            out_specs=[
+                pl.BlockSpec((2, 2, rows, 2 * LANES), lambda g, w: (0, g ^ (w[0] // 2), 0, 0)),
+                pl.BlockSpec((rows, step), lambda g, w: (0, g)),
+                pl.BlockSpec((rows, step), lambda g, w: (0, g)),
+            ],
+            scratch_shapes=[pltpu.VMEM((3, tail + rows, step), jnp.float32)],
+        ),
+        out_shape=[
+            jax.ShapeDtypeStruct((2, chips, rows, 2 * LANES), jnp.bfloat16),
+            jax.ShapeDtypeStruct((rows, channels // chunks), jnp.float32),
+            jax.ShapeDtypeStruct((rows, channels // chunks), jnp.bfloat16),
+        ],
+        cost_estimate=pl.CostEstimate(
+            flops=3_000_000, transcendentals=0, bytes_accessed=5_000_000
+        ),
+        name="mix",
+    )(where, *[proj] * 3, *[before] * 3, *[short_weight] * 3, grad_out)
+
+
+def near_body(mixed, decay, gain, skip, near_out, spread, answer):
+    rows, width = mixed.shape
+    tiles = width // LANES
+    modes = decay.shape[0]
+    lines = rows * tiles
+    for piece in range(tiles):
+        lanes = slice(piece * LANES, (piece + 1) * LANES)
+        block = mixed[:, lanes].astype(jnp.float32)
+        spread[pl.ds(piece, rows, stride=tiles), :] = block
+    for group in range(tiles // 8):
+        part = slice(group * 8, group * 8 + 8)
+        decays = [decay[r, part, :] for r in range(modes)]
+        gains = [gain[r, part, :] for r in range(modes)]
+        direct = skip[part, :]
+
+        def step(t, states, group=group, decays=decays, gains=gains, direct=direct):
+            at = pl.ds(pl.multiple_of(t * tiles + group * 8, 8), 8)
+            here = spread[at, :]
+            states = [d * h + here for d, h in zip(decays, states)]
+            terms = [g * h for g, h in zip(gains, states)] + [direct * here]
+            while len(terms) > 1:
+                terms = [a + b for a, b in zip(terms[::2], terms[1::2])] + (
+                    terms[-1:] if len(terms) % 2 else []
+                )
+            answer[at, :] = terms[0]
+            return states
+
+        start = [jnp.zeros((8, LANES), jnp.float32)] * modes
+        lax.fori_loop(0, rows, step, start, unroll=4)
+    for piece in range(tiles):
+        lanes = slice(piece * LANES, (piece + 1) * LANES)
+        near_out[:, lanes] = answer[pl.ds(piece, rows, stride=tiles), :]
+
+
+def near_part(mixed, decay, gain, skip):
+    rows, width = mixed.shape
+    tiles = width // LANES
+    return pl.pallas_call(
+        near_body,
+        out_shape=jax.ShapeDtypeStruct((rows, width), jnp.float32),
+        scratch_shapes=[
+            pltpu.VMEM((rows * tiles, LANES), jnp.float32),
+            pltpu.VMEM((rows * tiles, LANES), jnp.float32),
+        ],
+        cost_estimate=pl.CostEstimate(
+            flops=4_000_000, transcendentals=0, bytes_accessed=8_000_000
+        ),
+        name="near",
+    )(mixed, decay, gain, skip)
+
+
+def lag_body(where, own, other, *rest):
+    count = (len(rest) - 14)
+    sources = rest[:count]
+    (rate, amplitude, forward, backward, outer_forward, outer_backward, out,
+     stacked, lined, high, low, back_high, back_low, spare) = rest[count:]
+    step = pl.program_id(0)
+    chip, core = where[0], where[1]
+    chips = count + 1
+    devices = 2 * chips
+    rows = own.shape[-2]
+    fine = FINE_PRODUCT // devices
+    groups = rows // fine
+    modes = rate.shape[0]
+
+    @pl.when(step == 0)
+    def _():
+        for turned in range(chips):
+            for side in range(2):
+                position = 2 * (turned ^ chip) + (side ^ core)
+                at = pl.ds(pl.multiple_of(position * fine, fine), fine)
+                if turned == 0:
+                    block = (own, other)[side]
+                    whole = block[0, 0]
+                else:
+                    whole = sources[turned - 1][side]
+                for group in range(groups):
+                    stacked[group, at, :] = whole[group * fine : (group + 1) * fine, :]
+                lined[position] = whole[:, :LANES].astype(jnp.float32)
+        for group in range(groups):
+            signal = stacked[group]
+            first = dot32(outer_forward[: 2 * FINE_PRODUCT, :], signal) + dot32(
+                outer_forward[2 * FINE_PRODUCT :, :], signal
+            )
+            first_high, first_low = split_pair(first)
+            for k in range(devices):
+                for part in range(2):
+                    source = slice((2 * k + part) * fine, (2 * k + part + 1) * fine)
+                    target = slice(part * rows + group * fine, part * rows + (group + 1) * fine)
+                    high[k, target, :] = first_high[source, :]
+                    low[k, target, :] = first_low[source, :]
+
+    def inner():
+        table = forward[0]
+        spectrum = (
+            dot32(table[: 2 * rows], high[step])
+            + dot32(table[: 2 * rows], low[step])
+            + dot32(table[2 * rows :], high[step])
+        )
+        real_m, imag_m = spectrum[:rows, :LANES], spectrum[rows:, :LANES]
+        real_s, imag_s = spectrum[:rows, LANES:], spectrum[rows:, LANES:]
+        product = jnp.concatenate(
+            [real_m * real_s + imag_m * imag_s, real_m * imag_s - imag_m * real_s], axis=0
+        )
+        prod_high, prod_low = split_pair(product)
+        table_back = backward[0]
+        lagged = (
+            dot32(table_back[: 2 * rows], prod_high)
+            + dot32(table_back[: 2 * rows], prod_low)
+            + dot32(table_back[2 * rows :], prod_high)
+        )
+        lag_high, lag_low = split_pair(lagged)
+        for group in range(groups):
+            for part in range(2):
+                source = slice(part * rows + group * fine, part * rows + (group + 1) * fine)
+                at = pl.ds(pl.multiple_of((2 * step + part) * fine, fine), fine)
+                back_high[group, at, :] = lag_high[source, :]
+                back_low[group, at, :] = lag_low[source, :]
+
+    inner()
+
+    @pl.when(step == 1)
+    def _():
+        decay = jnp.exp(-rate[...])
+
+        def advance(t, states):
+            result = []
+            for p in range(devices):
+                here = jnp.broadcast_to(lined[p, pl.ds(t, 1), :], (modes, LANES))
+                result.append(decay * states[p] + here)
+            return tuple(result)
+
+        start = tuple(jnp.zeros((modes, LANES), jnp.float32) for _ in range(devices))
+        ends = lax.fori_loop(0, rows, advance, start, unroll=2)
+        far = jnp.exp(-float(rows) * rate[...])
+        lead = amplitude[...] * decay
+        carried = jnp.zeros((modes, LANES), jnp.float32)
+        for p in range(devices):
+            turned = (p // 2) ^ chip
+            side = (p % 2) ^ core
+            send_high, send_low = split_pair(lead * carried)
+            out[side, turned, rows : rows + modes, :] = send_high
+            out[side, turned, rows + modes : rows + 2 * modes, :] = send_low
+            carried = far * carried + ends[p]
+
+    @pl.when(step == devices - 1)
+    def _():
+        for group in range(groups):
+            result = (
+                dot32(outer_backward[:FINE_PRODUCT, :], back_high[group])
+                + dot32(outer_backward[:FINE_PRODUCT, :], back_low[group])
+                + dot32(outer_backward[FINE_PRODUCT:, :], back_high[group])
+            ).astype(jnp.bfloat16)
+            for p in range(devices):
+                turned = (p // 2) ^ chip
+                side = (p % 2) ^ core
+                out[side, turned, group * fine : (group + 1) * fine, :] = result[
+                    p * fine : (p + 1) * fine, :
+                ]
+
+
+def lag_part(where, sent, received, moved, rate, amplitude, tables, devices):
+    rows = sent.shape[-2]
+    chips = devices // 2
+    modes = rate.shape[0]
+    fine = FINE_PRODUCT // devices
+    groups = rows // fine
+    forward, backward, outer_forward, outer_backward = tables
+    whole = lambda shape: pl.BlockSpec(shape, lambda k, w: (0,) * len(shape))
+    return pl.pallas_call(
+        lag_body,
+        grid_spec=pltpu.PrefetchScalarGridSpec(
+            num_scalar_prefetch=1,
+            grid=(devices,),
+            in_specs=[
+                whole((1, 1, rows, 2 * LANES)),
+                whole((1, 1, rows, 2 * LANES)),
+            ]
+            + [whole((2, rows, 2 * LANES))] * (chips - 1)
+            + [
+                whole((modes, LANES)),
+                whole((modes, LANES)),
+                pl.BlockSpec((1, 4 * rows, 2 * rows), lambda k, w: (k, 0, 0)),
+                pl.BlockSpec((1, 4 * rows, 2 * rows), lambda k, w: (k, 0, 0)),
+                whole(outer_forward.shape),
+                whole(outer_backward.shape),
+            ],
+            out_specs=[whole((2, chips, rows + 2 * modes, LANES))],
+            scratch_shapes=[
+                pltpu.VMEM((groups, FINE_PRODUCT, 2 * LANES), jnp.bfloat16),
+                pltpu.VMEM((devices, rows, LANES), jnp.float32),
+                pltpu.VMEM((devices, 2 * rows, 2 * LANES), jnp.bfloat16),
+                pltpu.VMEM((devices, 2 * rows, 2 * LANES), jnp.bfloat16),
+                pltpu.VMEM((groups, 2 * FINE_PRODUCT, LANES), jnp.bfloat16),
+                pltpu.VMEM((groups, 2 * FINE_PRODUCT, LANES), jnp.bfloat16),
+                pltpu.VMEM((8, LANES), jnp.float32),
+            ],
+        ),
+        out_shape=[jax.ShapeDtypeStruct((2, chips, rows + 2 * modes, LANES), jnp.bfloat16)],
+        cost_estimate=pl.CostEstimate(
+            flops=5_000_000_000, transcendentals=0, bytes_accessed=12_000_000
+        ),
+        name="lags",
+    )(where, sent, received, *moved, rate, amplitude, forward, backward, outer_forward, outer_backward)[0]
+
+
+def finish_body(chips, where, own, other, *rest):
+    sources = rest[: chips - 1]
+    near, query, decay = rest[chips - 1 : chips + 2]
+    gated_out, grad_out = rest[-2:]
+    chip, core = where[0], where[1]
+    rows = near.shape[0]
+    modes = decay.shape[0]
+    line = lax.broadcasted_iota(jnp.int32, (8, LANES), 0)
+    for turned in range(chips):
+        for side in range(2):
+            owner = 2 * (turned ^ chip) + (side ^ core)
+            at = pl.ds(pl.multiple_of(owner * LANES, LANES), LANES)
+            block = (own, other)[side].at[0, 0] if turned == 0 else sources[turned - 1].at[side]
+            grad_out[:, at] = block[:rows, :].astype(jnp.float32)
+            lead = block[rows : rows + modes, :].astype(jnp.float32) + block[
+                rows + modes : rows + 2 * modes, :
+            ].astype(jnp.float32)
+            total = [near[8 * tile : 8 * tile + 8, at] for tile in range(rows // 8)]
+            rate_here = decay[:, at]
+            for mode in range(modes):
+                d1 = jnp.broadcast_to(rate_here[mode : mode + 1, :], (8, LANES))
+                d2 = d1 * d1
+                d4 = d2 * d2
+                d8 = d4 * d4
+                ones = jnp.ones_like(d1)
+                power = (
+                    jnp.where(line & 1 != 0, d1, ones)
+                    * jnp.where(line & 2 != 0, d2, ones)
+                    * jnp.where(line & 4 != 0, d4, ones)
+                )
+                term = power * lead[mode : mode + 1, :]
+                for tile in range(rows // 8):
+                    total[tile] = total[tile] + term
+                    if tile + 1 < rows // 8:
+                        term = term * d8
+            conv = jnp.concatenate(total, axis=0).astype(jnp.bfloat16)
+            gated_out[:, at] = (query[:, at] * conv.astype(jnp.float32)).astype(jnp.bfloat16)
+
+
+def finish_part(where, back, back_other, moved, near, query, decay, previous, chunk, chunks, devices):
+    rows, width = near.shape
+    chips = devices // 2
+    modes = decay.shape[0]
+    height = back.shape[2]
+    whole = lambda shape: pl.BlockSpec(shape, lambda g, w: (0,) * len(shape))
+    in_specs = (
+        [whole((1, 1, height, LANES))] * 2
+        + [whole((2, height, LANES))] * (chips - 1)
+        + [whole((rows, width)), whole((rows, width)), pl.BlockSpec((modes, width), lambda g, w: (0, chunk))]
+    )
+    args = [back, back_other, *moved, near, query, decay]
+    aliases = {}
+    if previous is not None:
+        in_specs += [pl.BlockSpec(memory_space=pl.ANY)] * 2
+        aliases = {len(args) + 1: 0, len(args) + 2: 1}
+        args += list(previous)
+    return pl.pallas_call(
+        functools.partial(finish_body, chips),
+        grid_spec=pltpu.PrefetchScalarGridSpec(
+            num_scalar_prefetch=1,
+            grid=(1,),
+            in_specs=in_specs,
+            out_specs=[pl.BlockSpec((rows, width), lambda g, w: (0, chunk))] * 2,
+        ),
+        out_shape=[
+            jax.ShapeDtypeStruct((rows, width * chunks), jnp.bfloat16),
+            jax.ShapeDtypeStruct((rows, width * chunks), jnp.float32),
+        ],
+        input_output_aliases=aliases,
+        cost_estimate=pl.CostEstimate(
+            flops=4_000_000, transcendentals=0, bytes_accessed=5_000_000
+        ),
+        name="finish",
+    )(where, *args)
+
+
+def swap(value, mask, devices):
+    return lax.ppermute(value, "seq", [(i, i ^ mask) for i in range(devices)])
+
+
+def exchange(outgoing, devices):
+    chips = devices // 2
+    received = swap(outgoing[1:2], 1, devices)
+    moved = [
+        swap(jnp.concatenate([outgoing[0, k : k + 1], received[0, k : k + 1]], axis=0), 2 * k, devices)
+        for k in range(1, chips)
+    ]
+    return (received, moved)
+
+
+def fast_on_device(proj, short_weight, residues, rates, skip, grad_out):
+    devices = lax.axis_size("seq")
+    rows, channels = grad_out.shape
+    modes = rates.shape[0]
+    chunks = channels // (devices * LANES)
+    me = lax.axis_index("seq")
+    where = jnp.stack([me // 2, me % 2]).astype(jnp.int32)
+    before = lax.ppermute(
+        proj[rows - HALO :], "seq", [(i, i + 1) for i in range(devices - 1)]
+    )
+    mixes = [
+        mix_streams(where, proj, before, short_weight, grad_out, chunk, chunks, devices)
+        for chunk in range(chunks)
+    ]
+    zero = lax.optimization_barrier((jnp.zeros((), jnp.int32), mixes[0][0]))[0]
+    tables = spectral_tables(devices, rows, zero)
+    decay = jnp.exp(-rates)
+    amplitude = residues * jnp.sqrt(rates)
+    width = channels // chunks
+    backs = []
+    for chunk in range(chunks):
+        sent, query, mixed = mixes[chunk]
+        received, moved = exchange(sent, devices)
+        start = chunk * width + me * LANES
+        rate_local = lax.dynamic_slice_in_dim(rates, start, LANES, 1)
+        amplitude_local = lax.dynamic_slice_in_dim(amplitude, start, LANES, 1)
+        backs.append(
+            lag_part(where, sent, received, moved, rate_local, amplitude_local, tables, devices)
+        )
+    shape = (modes, chunks, width // LANES, LANES)
+    decay_tiles = decay.reshape(shape)
+    gain_tiles = amplitude.reshape(shape)
+    skip_tiles = skip.reshape(shape[1:])
+    result = None
+    for chunk in range(chunks):
+        sent, query, mixed = mixes[chunk]
+        near = near_part(mixed, decay_tiles[:, chunk], gain_tiles[:, chunk], skip_tiles[chunk])
+        received, moved = exchange(backs[chunk], devices)
+        result = finish_part(
+            where, backs[chunk], received, moved, near, query, decay, result, chunk, chunks, devices
+        )
+    return tuple(result)
+
+
 def solution(mesh):
+    def body(proj, short_weight, residues, rates, skip, grad_out):
+        devices = lax.axis_size("seq")
+        rows, channels = grad_out.shape
+        fits = (
+            devices in (4, 8, 16)
+            and rows % LANES == 0
+            and channels % (devices * LANES) == 0
+            and residues.shape[0] == 16
+            and short_weight.shape[0] <= HALO + 1
+        )
+        chosen = fast_on_device if fits else on_device
+        return chosen(proj, short_weight, residues, rates, skip, grad_out)
+
     return jax.shard_map(
-        on_device,
+        body,
         mesh=mesh,
         in_specs=(P(("groups", "seq"), None), P(), P(), P(), P(), P(("groups", "seq"), None)),
         out_specs=(P(("groups", "seq"), None), P(("groups", "seq"), None)),

time: 339 us -> 207 us (0.61)
  the two profiles are of different devices: /device:TPU:13 before, /device:TPU:0 now
where the time goes in v1:
time: 207 us; the launch traced here: 206 us
  Pallas kernels  78.5 us (38%)
  starting transfers between devices  77.2 us (37%)
  local copies, waits for them, and re-layouts  24.9 us (12%)
  other arithmetic  19.4 us (9%)
  waiting for transfers between devices  4.39 us (2%)
    ppermute x32, starting transfers between devices, swap(): return lax.ppermute(value, 'seq', [(i, i ^ mask) for i in range(devices)])  74.8 us
    pallas_call x2, Pallas kernels, lag_part(): pl.pallas_call(lag_body, grid_spec=pltpu.PrefetchScalarGridSpec(num_scala...  43.7 us
    pallas_call x2, Pallas kernels, mix_streams(): pl.pallas_call(mix_body, grid_spec=pltpu.PrefetchScalarGridSpec(num_scala...  13.3 us
    pallas_call x2, Pallas kernels, near_part(): pl.pallas_call(near_body, out_shape=jax.ShapeDtypeStruct((rows, width), j...  11 us
    pallas_call x2, Pallas kernels, finish_part(): pl.pallas_call(functools.partial(finish_body, chips), grid_spec=pltpu.Pre...  10.6 us
    mul x1, local copies, waits for them, and re-layouts, spectral_tables(): back_pair[:, None, :, :, None] * eye[None, :, None, None, :]  7.07 us
    concatenate x4, other arithmetic, spectral_tables(): jnp.concatenate(split_outside(table), axis=-2)  6.52 us
    ppermute x32, waiting for transfers between devices, swap(): return lax.ppermute(value, 'seq', [(i, i ^ mask) for i in range(devices)])  4.39 us
  transfers between devices with their start and end apart: 33, of which 2 were waited for; matrix products, arithmetic and copies ran while one was open for 11% of the time, Pallas kernels for 32%

profile of v1, /device:TPU:0, one launch (start us, length us, event | category | flops | bytes accessed | tf_op | source)
XLA Modules:
  0.0 205.9 jit_solution(15657544720498577613)
XLA Ops:
  0.6 0.9 slice.223
  1.6 2.4 %collective-permute-start = (bf16[8,12288]{1,0:T(8,128)(2,1)S(1)}, bf16[8,12288]{1,0:T(8,128)(2,1)S(1)}, u32[]{:S(2)}, u32[]{:S(2)}) collective-permute-start(bf16[8,12288]{1,0:T(8,128)(2,1)S(1)} %slice.223), channel_id=1, source_target_pairs={{0,1},{1,2},{2,3},{3,4},{4,5},{5,6},{6,7},{7,8},{8,9},{9,10},{10,1... | collective-permute-start | bytes 589832 | tf_op jit(solution)/shard_map/ppermute | solution.py:595
  4.0 1.8 negate_exponential_fusion
  6.0 0.7 pad_add_fusion.where
  6.6 1.3 constant_dynamic-slice_fusion
  8.0 0.8 slice_bitcast_fusion
  8.8 0.7 copy-done
  9.5 6.6 %mix.3 = (bf16[2,8,128,256]{3,2,1,0:T(8,128)(2,1)}, f32[128,2048]{1,0:T(8,128)}, bf16[128,2048]{1,0:T(8,128)(2,1)}) custom-call(s32[2]{0:T(128)} %pad_add_fusion.where, bf16[128,12288]{1,0:T(8,128)(2,1)} %value_in.3, bf16[128,12288]{1,0:T(8,128)(2,1)} %value_in.3, bf16[128,12288]{1,0:T(8,128)(2,1)} %value_in.3, bf16[8,12288]{1,0:T(8,128)(2,1)} %copy-done, ...), custom_call_target="tpu_custom_call" | custom-call | flops 3000000 | bytes 5000000 | tf_op jit(solution)/shard_map/mix/pallas_call | solution.py:264
  16.1 1.1 slice.258
  18.0 4.2 %broadcast_multiply_fusion = f32[16,16,16,2,16]{4,3,2,1,0:T(2,128)} fusion(f32[16,16]{1,0:T(8,128)S(1)} %fusion.17, f32[16,16,2]{2,1,0:T(8,128)S(1)} %copy.19), kind=kLoop, calls=%fused_computation.10 | loop fusion | flops 131072 | bytes 527360 | tf_op jit(solution)/shard_map/mul | solution.py:214
  22.2 7.1 %mul.272 = f32[256,512]{1,0:T(8,128)S(1)} reshape(f32[16,16,16,2,16]{4,3,2,1,0:T(2,128)} %broadcast_multiply_fusion) | data formatting | bytes 1048576 | tf_op jit(solution)/shard_map/mul | solution.py:214
  29.4 2.4 %broadcast_multiply_fusion.1 = f32[16,2,16,16,16]{4,3,2,1,0:T(8,128)} fusion(f32[16,16]{1,0:T(8,128)S(1)} %fusion.17, f32[16,2,16]{2,1,0:T(2,128)S(1)} %copy.18), kind=kLoop, calls=%fused_computation.11 | loop fusion | flops 131072 | bytes 527360 | tf_op jit(solution)/shard_map/mul | solution.py:210
  31.8 3.5 %mul.265 = f32[512,256]{1,0:T(8,128)S(1)} reshape(f32[16,2,16,16,16]{4,3,2,1,0:T(8,128)} %broadcast_multiply_fusion.1) | data formatting | bytes 1048576 | tf_op jit(solution)/shard_map/mul | solution.py:210
  35.4 2.7 %collective-permute-start.17 = (bf16[1,8,128,256]{3,2,1,0:T(8,128)(2,1)S(1)}, bf16[1,8,128,256]{3,2,1,0:T(8,128)(2,1)S(1)}, u32[]{:S(2)}, u32[]{:S(2)}) collective-permute-start(bf16[1,8,128,256]{3,2,1,0:T(8,128)(2,1)S(1)} %slice.258), channel_id=1, source_target_pairs={{0,1},{1,0},{2,3},{3,2},{4,5},{5,4},{6,7},{7,6},{8,9},{9,8},{10,11... | collective-permute-start | bytes 1572872 | tf_op jit(solution)/shard_map/ppermute | solution.py:575
  38.0 6.6 %mix.2 = (bf16[2,8,128,256]{3,2,1,0:T(8,128)(2,1)}, f32[128,2048]{1,0:T(8,128)}, bf16[128,2048]{1,0:T(8,128)(2,1)}) custom-call(s32[2]{0:T(128)} %pad_add_fusion.where, bf16[128,12288]{1,0:T(8,128)(2,1)} %value_in.3, bf16[128,12288]{1,0:T(8,128)(2,1)} %value_in.3, bf16[128,12288]{1,0:T(8,128)(2,1)} %value_in.3, bf16[8,12288]{1,0:T(8,128)(2,1)} %copy-done, ...), custom_call_target="tpu_custom_call" | custom-call | flops 3000000 | bytes 5000000 | tf_op jit(solution)/shard_map/mix/pallas_call | solution.py:264
  44.7 1.1 slice.224
  45.9 0.8 pad_maximum_fusion.3.rest_12_
  46.7 1.0 fusion.5
  47.7 0.9 reduce-precision_convert_fusion
  48.6 2.4 %pad_maximum_fusion.1.rest_10_ = bf16[16,512,256]{2,1,0:T(8,128)(2,1)} fusion(bf16[16,256,256]{2,1,0:T(8,128)(2,1)S(1)} %get-tuple-element.21, bf16[16,256,256]{2,1,0:T(8,128)(2,1)S(1)} %get-tuple-element.20), kind=kLoop, calls=%fused_computation.9 | loop fusion | flops 8388608 | bytes 8388608 | tf_op jit(solution)/shard_map/concatenate | solution.py:218
  51.0 0.8 reduce-precision_convert_fusion.1
  51.8 2.4 %pad_maximum_fusion.rest_9_ = bf16[16,512,256]{2,1,0:T(8,128)(2,1)} fusion(bf16[16,256,256]{2,1,0:T(8,128)(2,1)S(1)} %get-tuple-element.23, bf16[16,256,256]{2,1,0:T(8,128)(2,1)S(1)} %get-tuple-element.22), kind=kLoop, calls=%fused_computation.7 | loop fusion | flops 8388608 | bytes 8388608 | tf_op jit(solution)/shard_map/concatenate | solution.py:218
  54.3 0.8 pad_maximum_fusion.2.rest_11_
  55.1 1.1 slice_bitcast_fusion.18
  56.2 1.1 slice_bitcast_fusion.25
  57.3 1.6 collective-permute-start.18
  58.9 1.6 collective-permute-start.19
  61.1 2.7 %collective-permute-start.21 = (bf16[2,128,256]{2,1,0:T(8,128)(2,1)S(1)}, bf16[2,128,256]{2,1,0:T(8,128)(2,1)S(1)}, u32[]{:S(2)}, u32[]{:S(2)}) collective-permute-start(bf16[2,128,256]{2,1,0:T(8,128)(2,1)S(1)} %pad_maximum_fusion.14), channel_id=1, source_target_pairs={{0,8},{1,9},{2,10},{3,11},{4,12},{5,13},{6,14},{7,15},{8,0},{9,1},... | collective-permute-start | bytes 393224 | tf_op jit(solution)/shard_map/ppermute | solution.py:575
  63.8 1.4 collective-permute-start.22
  65.3 2.8 %collective-permute-start.23 = (bf16[2,128,256]{2,1,0:T(8,128)(2,1)S(1)}, bf16[2,128,256]{2,1,0:T(8,128)(2,1)S(1)}, u32[]{:S(2)}, u32[]{:S(2)}) collective-permute-start(bf16[2,128,256]{2,1,0:T(8,128)(2,1)S(1)} %pad_maximum_fusion.16), channel_id=1, source_target_pairs={{0,12},{1,13},{2,14},{3,15},{4,8},{5,9},{6,10},{7,11},{8,4},{9,5},... | collective-permute-start | bytes 393224 | tf_op jit(solution)/shard_map/ppermute | solution.py:575
  68.1 1.5 collective-permute-done.19.rest_1_
  69.6 2.5 %collective-permute-start.24 = (bf16[2,128,256]{2,1,0:T(8,128)(2,1)S(1)}, bf16[2,128,256]{2,1,0:T(8,128)(2,1)S(1)}, u32[]{:S(2)}, u32[]{:S(2)}) collective-permute-start(bf16[2,128,256]{2,1,0:T(8,128)(2,1)S(1)} %pad_maximum_fusion.17), channel_id=1, source_target_pairs={{0,14},{1,15},{2,12},{3,13},{4,10},{5,11},{6,8},{7,9},{8,6},{9,7},... | collective-permute-start | bytes 393224 | tf_op jit(solution)/shard_map/ppermute | solution.py:575
  72.1 2.2 %collective-permute-start.8 = (bf16[2,128,256]{2,1,0:T(8,128)(2,1)S(1)}, bf16[2,128,256]{2,1,0:T(8,128)(2,1)S(1)}, u32[]{:S(2)}, u32[]{:S(2)}) collective-permute-start(bf16[2,128,256]{2,1,0:T(8,128)(2,1)S(1)} %pad_maximum_fusion.10), channel_id=1, source_target_pairs={{0,14},{1,15},{2,12},{3,13},{4,10},{5,11},{6,8},{7,9},{8,6},{9,7},... | collective-permute-start | bytes 393224 | tf_op jit(solution)/shard_map/ppermute | solution.py:575
  74.3 13.1 %collective-permute-start.7 = (bf16[2,128,256]{2,1,0:T(8,128)(2,1)S(1)}, bf16[2,128,256]{2,1,0:T(8,128)(2,1)S(1)}, u32[]{:S(2)}, u32[]{:S(2)}) collective-permute-start(bf16[2,128,256]{2,1,0:T(8,128)(2,1)S(1)} %pad_maximum_fusion.9), channel_id=1, source_target_pairs={{0,12},{1,13},{2,14},{3,15},{4,8},{5,9},{6,10},{7,11},{8,4},{9,5},... | collective-permute-start | bytes 393224 | tf_op jit(solution)/shard_map/ppermute | solution.py:575
  87.7 10.1 %collective-permute-start.5 = (bf16[2,128,256]{2,1,0:T(8,128)(2,1)S(1)}, bf16[2,128,256]{2,1,0:T(8,128)(2,1)S(1)}, u32[]{:S(2)}, u32[]{:S(2)}) collective-permute-start(bf16[2,128,256]{2,1,0:T(8,128)(2,1)S(1)} %pad_maximum_fusion.7), channel_id=1, source_target_pairs={{0,8},{1,9},{2,10},{3,11},{4,12},{5,13},{6,14},{7,15},{8,0},{9,1},... | collective-permute-start | bytes 393224 | tf_op jit(solution)/shard_map/ppermute | solution.py:575
  97.8 2.1 %collective-permute-start.4 = (bf16[2,128,256]{2,1,0:T(8,128)(2,1)S(1)}, bf16[2,128,256]{2,1,0:T(8,128)(2,1)S(1)}, u32[]{:S(2)}, u32[]{:S(2)}) collective-permute-start(bf16[2,128,256]{2,1,0:T(8,128)(2,1)S(1)} %pad_maximum_fusion.6), channel_id=1, source_target_pairs={{0,6},{1,7},{2,4},{3,5},{4,2},{5,3},{6,0},{7,1},{8,14},{9,15},{10,... | collective-permute-start | bytes 393224 | tf_op jit(solution)/shard_map/ppermute | solution.py:575
  99.9 3.2 %collective-permute-start.3 = (bf16[2,128,256]{2,1,0:T(8,128)(2,1)S(1)}, bf16[2,128,256]{2,1,0:T(8,128)(2,1)}, u32[]{:S(2)}, u32[]{:S(2)}) collective-permute-start(bf16[2,128,256]{2,1,0:T(8,128)(2,1)S(1)} %pad_maximum_fusion.5), channel_id=1, source_target_pairs={{0,4},{1,5},{2,6},{3,7},{4,0},{5,1},{6,2},{7,3},{8,12},{9,13},{10,... | collective-permute-start | bytes 393224 | tf_op jit(solution)/shard_map/ppermute | solution.py:575
  103.2 1.5 collective-permute-start.2
  104.8 21.9 %lags.3.own = bf16[2,8,160,128]{3,2,1,0:T(8,128)(2,1)} custom-call(s32[2]{0:T(128)} %pad_add_fusion.where, bf16[2,8,128,256]{3,2,1,0:T(8,128)(2,1)} %get-tuple-element.12.own, bf16[1,8,128,256]{3,2,1,0:T(8,128)(2,1)} %copy-done.4, bf16[2,128,256]{2,1,0:T(8,128)(2,1)} %copy-done.20, bf16[2,128,256]{2,1,0:T(8,128)(2,1)} %copy-done.21, ...), custom_call_target="tpu_custom_call" | custom-call | flops 5000000000 | bytes 12000000 | tf_op jit(solution)/shard_map/lags/pallas_call | solution.py:461
  126.7 1.0 slice.323
  128.5 21.8 %lags.2.own = bf16[2,8,160,128]{3,2,1,0:T(8,128)(2,1)} custom-call(s32[2]{0:T(128)} %pad_add_fusion.where, bf16[2,8,128,256]{3,2,1,0:T(8,128)(2,1)} %get-tuple-element.11.own, bf16[1,8,128,256]{3,2,1,0:T(8,128)(2,1)} %copy-done.3, bf16[2,128,256]{2,1,0:T(8,128)(2,1)} %copy-done.32, bf16[2,128,256]{2,1,0:T(8,128)(2,1)} %collective-permute-done.3.rest_1_, ...), custom_call_target="tpu_custom_call" | custom-call | flops 5000000000 | bytes 12000000 | tf_op jit(solution)/shard_map/lags/pallas_call | solution.py:461
  150.3 0.9 slice_bitcast_fusion.33
  151.3 1.0 slice.299
  152.3 0.6 collective-permute-start.9
  152.8 0.9 slice_bitcast_fusion.47
  153.8 3.2 %collective-permute-start.32 = (bf16[2,160,128]{2,1,0:T(8,128)(2,1)S(1)}, bf16[2,160,128]{2,1,0:T(8,128)(2,1)S(1)}, u32[]{:S(2)}, u32[]{:S(2)}) collective-permute-start(bf16[2,160,128]{2,1,0:T(8,128)(2,1)S(1)} %pad_maximum_fusion.31), channel_id=1, source_target_pairs={{0,14},{1,15},{2,12},{3,13},{4,10},{5,11},{6,8},{7,9},{8,6},{9,7},... | collective-permute-start | bytes 245768 | tf_op jit(solution)/shard_map/ppermute | solution.py:575
  157.1 0.7 collective-permute-start.31
  157.8 2.8 %collective-permute-start.30 = (bf16[2,160,128]{2,1,0:T(8,128)(2,1)S(1)}, bf16[2,160,128]{2,1,0:T(8,128)(2,1)S(1)}, u32[]{:S(2)}, u32[]{:S(2)}) collective-permute-start(bf16[2,160,128]{2,1,0:T(8,128)(2,1)S(1)} %pad_maximum_fusion.29), channel_id=1, source_target_pairs={{0,10},{1,11},{2,8},{3,9},{4,14},{5,15},{6,12},{7,13},{8,2},{9,3},... | collective-permute-start | bytes 245768 | tf_op jit(solution)/shard_map/ppermute | solution.py:575
  160.7 1.1 collective-permute-start.29
  161.8 1.2 collective-permute-start.28
  163.2 5.3 %collective-permute-start.27 = (bf16[2,160,128]{2,1,0:T(8,128)(2,1)S(1)}, bf16[2,160,128]{2,1,0:T(8,128)(2,1)S(1)}, u32[]{:S(2)}, u32[]{:S(2)}) collective-permute-start(bf16[2,160,128]{2,1,0:T(8,128)(2,1)S(1)} %pad_maximum_fusion.26), channel_id=1, source_target_pairs={{0,4},{1,5},{2,6},{3,7},{4,0},{5,1},{6,2},{7,3},{8,12},{9,13},{10,... | collective-permute-start | bytes 245768 | tf_op jit(solution)/shard_map/ppermute | solution.py:575
  168.9 2.8 %collective-permute-done.30.rest_4_ = bf16[2,160,128]{2,1,0:T(8,128)(2,1)S(1)} collective-permute-done((bf16[2,160,128]{2,1,0:T(8,128)(2,1)S(1)}, bf16[2,160,128]{2,1,0:T(8,128)(2,1)S(1)}, u32[]{:S(2)}, u32[]{:S(2)}) %collective-permute-start.30) | collective-permute-done | bytes 81952 | tf_op jit(solution)/shard_map/ppermute | solution.py:575
  171.7 3.2 %collective-permute-start.16 = (bf16[2,160,128]{2,1,0:T(8,128)(2,1)S(1)}, bf16[2,160,128]{2,1,0:T(8,128)(2,1)S(1)}, u32[]{:S(2)}, u32[]{:S(2)}) collective-permute-start(bf16[2,160,128]{2,1,0:T(8,128)(2,1)S(1)} %pad_maximum_fusion.24), channel_id=1, source_target_pairs={{0,14},{1,15},{2,12},{3,13},{4,10},{5,11},{6,8},{7,9},{8,6},{9,7},... | collective-permute-start | bytes 245768 | tf_op jit(solution)/shard_map/ppermute | solution.py:575
  174.8 0.8 collective-permute-start.15
  175.7 3.7 %collective-permute-start.13 = (bf16[2,160,128]{2,1,0:T(8,128)(2,1)S(1)}, bf16[2,160,128]{2,1,0:T(8,128)(2,1)S(1)}, u32[]{:S(2)}, u32[]{:S(2)}) collective-permute-start(bf16[2,160,128]{2,1,0:T(8,128)(2,1)S(1)} %pad_maximum_fusion.21), channel_id=1, source_target_pairs={{0,8},{1,9},{2,10},{3,11},{4,12},{5,13},{6,14},{7,15},{8,0},{9,1},... | collective-permute-start | bytes 245768 | tf_op jit(solution)/shard_map/ppermute | solution.py:575
  179.4 0.9 collective-permute-start.12
  180.3 1.2 collective-permute-start.11
  181.6 1.4 collective-permute-start.10
  182.9 0.6 slice_bitcast_fusion.60
  183.6 5.5 %near.3.rest_7_ = f32[128,2048]{1,0:T(8,128)} custom-call(bf16[128,2048]{1,0:T(8,128)(2,1)} %get-tuple-element.16.mixed, f32[16,16,128]{2,1,0:T(8,128)} %get-tuple-element.116.decay, f32[16,16,128]{2,1,0:T(8,128)} %get-tuple-element.84.gain, f32[16,128]{1,0:T(8,128)} %get-tuple-element.101.skip), custom_call_target="tpu_custom_call" | custom-call | flops 4000000 | bytes 8000000 | tf_op jit(solution)/shard_map/near/pallas_call | solution.py:329
  189.0 5.5 %near.2.rest_7_ = f32[128,2048]{1,0:T(8,128)} custom-call(bf16[128,2048]{1,0:T(8,128)(2,1)} %get-tuple-element.14.mixed, f32[16,16,128]{2,1,0:T(8,128)} %get-tuple-element.115.decay, f32[16,16,128]{2,1,0:T(8,128)} %get-tuple-element.85.gain, f32[16,128]{1,0:T(8,128)} %get-tuple-element.102.skip), custom_call_target="tpu_custom_call" | custom-call | flops 4000000 | bytes 8000000 | tf_op jit(solution)/shard_map/near/pallas_call | solution.py:329
  194.6 5.3 %finish.2 = (bf16[128,4096]{1,0:T(8,128)(2,1)}, f32[128,4096]{1,0:T(8,128)}) custom-call(s32[2]{0:T(128)} %pad_add_fusion.where, bf16[2,8,160,128]{3,2,1,0:T(8,128)(2,1)} %lags.3.own, bf16[1,8,160,128]{3,2,1,0:T(8,128)(2,1)} %copy-done.2, bf16[2,160,128]{2,1,0:T(8,128)(2,1)} %copy-done.18, bf16[2,160,128]{2,1,0:T(8,128)(2,1)} %copy-done.17, ...), custom_call_target="tpu_custom_call" | custom-call | flops 4000000 | bytes 5000000 | tf_op jit(solution)/shard_map/finish/pallas_call | solution.py:554
  200.0 0.5 copy-done.7
  200.6 5.3 %finish.3 = (bf16[128,4096]{1,0:T(8,128)(2,1)}, f32[128,4096]{1,0:T(8,128)}) custom-call(s32[2]{0:T(128)} %pad_add_fusion.where, bf16[2,8,160,128]{3,2,1,0:T(8,128)(2,1)} %lags.2.own, bf16[1,8,160,128]{3,2,1,0:T(8,128)(2,1)} %copy-done.1, bf16[2,160,128]{2,1,0:T(8,128)(2,1)} %copy-done.11, ...), custom_call_target="tpu_custom_call", output_to_operand_aliasing={{0}: (13, {}), {1}: (14, {})} | custom-call | flops 4000000 | bytes 5000000 | tf_op jit(solution)/shard_map/finish/pallas_call | solution.py:554
  (146 shorter events, 3.7 us)
Async XLA Ops:
  1.6 7.2 %collective-permute-start = (bf16[8,12288]{1,0:T(8,128)(2,1)S(1)}, bf16[8,12288]{1,0:T(8,128)(2,1)S(1)}, u32[]{:S(2)}, u32[]{:S(2)}) collective-permute-start(bf16[8,12288]{1,0:T(8,128)(2,1)S(1)} %slice.223), channel_id=1, source_target_pairs={{0,1},{1,2},{2,3},{3,4},{4,5},{5,6},{6,7},{7,8},{8,9},{9,10},{10,1... | collective-permute-start | bytes 589832 | tf_op jit(solution)/shard_map/ppermute | solution.py:595
  8.8 0.7 copy-start
  35.4 21.9 %collective-permute-start.17 = (bf16[1,8,128,256]{3,2,1,0:T(8,128)(2,1)S(1)}, bf16[1,8,128,256]{3,2,1,0:T(8,128)(2,1)S(1)}, u32[]{:S(2)}, u32[]{:S(2)}) collective-permute-start(bf16[1,8,128,256]{3,2,1,0:T(8,128)(2,1)S(1)} %slice.258), channel_id=1, source_target_pairs={{0,1},{1,0},{2,3},{3,2},{4,5},{5,4},{6,7},{7,6},{8,9},{9,8},{10,11... | collective-permute-start | bytes 1572872 | tf_op jit(solution)/shard_map/ppermute | solution.py:575
  45.8 18.0 %collective-permute-start.1 = (bf16[1,8,128,256]{3,2,1,0:T(8,128)(2,1)S(1)}, bf16[1,8,128,256]{3,2,1,0:T(8,128)(2,1)S(1)}, u32[]{:S(2)}, u32[]{:S(2)}) collective-permute-start(bf16[1,8,128,256]{3,2,1,0:T(8,128)(2,1)S(1)} %slice.224), channel_id=1, source_target_pairs={{0,1},{1,0},{2,3},{3,2},{4,5},{5,4},{6,7},{7,6},{8,9},{9,8},{10,11... | collective-permute-start | bytes 1572872 | tf_op jit(solution)/shard_map/ppermute | solution.py:575
  57.2 47.5 %copy-start.4 = (bf16[1,8,128,256]{3,2,1,0:T(8,128)(2,1)}, bf16[1,8,128,256]{3,2,1,0:T(8,128)(2,1)S(1)}, u32[]{:S(2)}) copy-start(bf16[1,8,128,256]{3,2,1,0:T(8,128)(2,1)S(1)} %collective-permute-done.17.other) | copy-start | bytes 1572868
  57.3 8.0 %collective-permute-start.18 = (bf16[2,128,256]{2,1,0:T(8,128)(2,1)S(1)}, bf16[2,128,256]{2,1,0:T(8,128)(2,1)S(1)}, u32[]{:S(2)}, u32[]{:S(2)}) collective-permute-start(bf16[2,128,256]{2,1,0:T(8,128)(2,1)S(1)} %pad_maximum_fusion.11), channel_id=1, source_target_pairs={{0,2},{1,3},{2,0},{3,1},{4,6},{5,7},{6,4},{7,5},{8,10},{9,11},{10,... | collective-permute-start | bytes 393224 | tf_op jit(solution)/shard_map/ppermute | solution.py:575
  58.9 10.7 %collective-permute-start.19 = (bf16[2,128,256]{2,1,0:T(8,128)(2,1)S(1)}, bf16[2,128,256]{2,1,0:T(8,128)(2,1)S(1)}, u32[]{:S(2)}, u32[]{:S(2)}) collective-permute-start(bf16[2,128,256]{2,1,0:T(8,128)(2,1)S(1)} %pad_maximum_fusion.12), channel_id=1, source_target_pairs={{0,4},{1,5},{2,6},{3,7},{4,0},{5,1},{6,2},{7,3},{8,12},{9,13},{10,... | collective-permute-start | bytes 393224 | tf_op jit(solution)/shard_map/ppermute | solution.py:575
  60.6 11.5 %collective-permute-start.20 = (bf16[2,128,256]{2,1,0:T(8,128)(2,1)S(1)}, bf16[2,128,256]{2,1,0:T(8,128)(2,1)S(1)}, u32[]{:S(2)}, u32[]{:S(2)}) collective-permute-start(bf16[2,128,256]{2,1,0:T(8,128)(2,1)S(1)} %pad_maximum_fusion.13), channel_id=1, source_target_pairs={{0,6},{1,7},{2,4},{3,5},{4,2},{5,3},{6,0},{7,1},{8,14},{9,15},{10,... | collective-permute-start | bytes 393224 | tf_op jit(solution)/shard_map/ppermute | solution.py:575
  61.1 13.3 %collective-permute-start.21 = (bf16[2,128,256]{2,1,0:T(8,128)(2,1)S(1)}, bf16[2,128,256]{2,1,0:T(8,128)(2,1)S(1)}, u32[]{:S(2)}, u32[]{:S(2)}) collective-permute-start(bf16[2,128,256]{2,1,0:T(8,128)(2,1)S(1)} %pad_maximum_fusion.14), channel_id=1, source_target_pairs={{0,8},{1,9},{2,10},{3,11},{4,12},{5,13},{6,14},{7,15},{8,0},{9,1},... | collective-permute-start | bytes 393224 | tf_op jit(solution)/shard_map/ppermute | solution.py:575
  63.8 62.9 %copy-start.3 = (bf16[1,8,128,256]{3,2,1,0:T(8,128)(2,1)}, bf16[1,8,128,256]{3,2,1,0:T(8,128)(2,1)S(1)}, u32[]{:S(2)}) copy-start(bf16[1,8,128,256]{3,2,1,0:T(8,128)(2,1)S(1)} %collective-permute-done.1.other) | copy-start | bytes 1572868
  63.8 23.7 %collective-permute-start.22 = (bf16[2,128,256]{2,1,0:T(8,128)(2,1)S(1)}, bf16[2,128,256]{2,1,0:T(8,128)(2,1)S(1)}, u32[]{:S(2)}, u32[]{:S(2)}) collective-permute-start(bf16[2,128,256]{2,1,0:T(8,128)(2,1)S(1)} %pad_maximum_fusion.15), channel_id=1, source_target_pairs={{0,10},{1,11},{2,8},{3,9},{4,14},{5,15},{6,12},{7,13},{8,2},{9,3},... | collective-permute-start | bytes 393224 | tf_op jit(solution)/shard_map/ppermute | solution.py:575
  65.3 39.4 %copy-start.20 = (bf16[2,128,256]{2,1,0:T(8,128)(2,1)}, bf16[2,128,256]{2,1,0:T(8,128)(2,1)S(1)}, u32[]{:S(2)}) copy-start(bf16[2,128,256]{2,1,0:T(8,128)(2,1)S(1)} %collective-permute-done.18.rest_0_) | copy-start | bytes 393220
  65.3 22.3 %collective-permute-start.23 = (bf16[2,128,256]{2,1,0:T(8,128)(2,1)S(1)}, bf16[2,128,256]{2,1,0:T(8,128)(2,1)S(1)}, u32[]{:S(2)}, u32[]{:S(2)}) collective-permute-start(bf16[2,128,256]{2,1,0:T(8,128)(2,1)S(1)} %pad_maximum_fusion.16), channel_id=1, source_target_pairs={{0,12},{1,13},{2,14},{3,15},{4,8},{5,9},{6,10},{7,11},{8,4},{9,5},... | collective-permute-start | bytes 393224 | tf_op jit(solution)/shard_map/ppermute | solution.py:575
  69.6 35.1 %copy-start.21 = (bf16[2,128,256]{2,1,0:T(8,128)(2,1)}, bf16[2,128,256]{2,1,0:T(8,128)(2,1)S(1)}, u32[]{:S(2)}) copy-start(bf16[2,128,256]{2,1,0:T(8,128)(2,1)S(1)} %collective-permute-done.19.rest_1_) | copy-start | bytes 393220
  69.6 28.2 %collective-permute-start.24 = (bf16[2,128,256]{2,1,0:T(8,128)(2,1)S(1)}, bf16[2,128,256]{2,1,0:T(8,128)(2,1)S(1)}, u32[]{:S(2)}, u32[]{:S(2)}) collective-permute-start(bf16[2,128,256]{2,1,0:T(8,128)(2,1)S(1)} %pad_maximum_fusion.17), channel_id=1, source_target_pairs={{0,14},{1,15},{2,12},{3,13},{4,10},{5,11},{6,8},{7,9},{8,6},{9,7},... | collective-permute-start | bytes 393224 | tf_op jit(solution)/shard_map/ppermute | solution.py:575
  72.1 32.6 %copy-start.22 = (bf16[2,128,256]{2,1,0:T(8,128)(2,1)}, bf16[2,128,256]{2,1,0:T(8,128)(2,1)S(1)}, u32[]{:S(2)}) copy-start(bf16[2,128,256]{2,1,0:T(8,128)(2,1)S(1)} %collective-permute-done.20.rest_2_) | copy-start | bytes 393220
  72.1 27.8 %collective-permute-start.8 = (bf16[2,128,256]{2,1,0:T(8,128)(2,1)S(1)}, bf16[2,128,256]{2,1,0:T(8,128)(2,1)S(1)}, u32[]{:S(2)}, u32[]{:S(2)}) collective-permute-start(bf16[2,128,256]{2,1,0:T(8,128)(2,1)S(1)} %pad_maximum_fusion.10), channel_id=1, source_target_pairs={{0,14},{1,15},{2,12},{3,13},{4,10},{5,11},{6,8},{7,9},{8,6},{9,7},... | collective-permute-start | bytes 393224 | tf_op jit(solution)/shard_map/ppermute | solution.py:575
  74.3 30.4 %copy-start.23 = (bf16[2,128,256]{2,1,0:T(8,128)(2,1)}, bf16[2,128,256]{2,1,0:T(8,128)(2,1)S(1)}, u32[]{:S(2)}) copy-start(bf16[2,128,256]{2,1,0:T(8,128)(2,1)S(1)} %collective-permute-done.21.rest_3_) | copy-start | bytes 393220
  74.3 28.9 %collective-permute-start.7 = (bf16[2,128,256]{2,1,0:T(8,128)(2,1)S(1)}, bf16[2,128,256]{2,1,0:T(8,128)(2,1)S(1)}, u32[]{:S(2)}, u32[]{:S(2)}) collective-permute-start(bf16[2,128,256]{2,1,0:T(8,128)(2,1)S(1)} %pad_maximum_fusion.9), channel_id=1, source_target_pairs={{0,12},{1,13},{2,14},{3,15},{4,8},{5,9},{6,10},{7,11},{8,4},{9,5},... | collective-permute-start | bytes 393224 | tf_op jit(solution)/shard_map/ppermute | solution.py:575
  87.5 17.2 %copy-start.24 = (bf16[2,128,256]{2,1,0:T(8,128)(2,1)}, bf16[2,128,256]{2,1,0:T(8,128)(2,1)S(1)}, u32[]{:S(2)}) copy-start(bf16[2,128,256]{2,1,0:T(8,128)(2,1)S(1)} %collective-permute-done.22.rest_4_) | copy-start | bytes 393220
  87.5 40.1 %collective-permute-start.6 = (bf16[2,128,256]{2,1,0:T(8,128)(2,1)S(1)}, bf16[2,128,256]{2,1,0:T(8,128)(2,1)S(1)}, u32[]{:S(2)}, u32[]{:S(2)}) collective-permute-start(bf16[2,128,256]{2,1,0:T(8,128)(2,1)S(1)} %pad_maximum_fusion.8), channel_id=1, source_target_pairs={{0,10},{1,11},{2,8},{3,9},{4,14},{5,15},{6,12},{7,13},{8,2},{9,3},... | collective-permute-start | bytes 393224 | tf_op jit(solution)/shard_map/ppermute | solution.py:575
  87.7 17.1 %copy-start.27 = (bf16[2,128,256]{2,1,0:T(8,128)(2,1)}, bf16[2,128,256]{2,1,0:T(8,128)(2,1)S(1)}, u32[]{:S(2)}) copy-start(bf16[2,128,256]{2,1,0:T(8,128)(2,1)S(1)} %collective-permute-done.23.rest_5_) | copy-start | bytes 393220
  87.7 40.1 %collective-permute-start.5 = (bf16[2,128,256]{2,1,0:T(8,128)(2,1)S(1)}, bf16[2,128,256]{2,1,0:T(8,128)(2,1)S(1)}, u32[]{:S(2)}, u32[]{:S(2)}) collective-permute-start(bf16[2,128,256]{2,1,0:T(8,128)(2,1)S(1)} %pad_maximum_fusion.7), channel_id=1, source_target_pairs={{0,8},{1,9},{2,10},{3,11},{4,12},{5,13},{6,14},{7,15},{8,0},{9,1},... | collective-permute-start | bytes 393224 | tf_op jit(solution)/shard_map/ppermute | solution.py:575
  97.8 6.9 %copy-start.29 = (bf16[2,128,256]{2,1,0:T(8,128)(2,1)}, bf16[2,128,256]{2,1,0:T(8,128)(2,1)S(1)}, u32[]{:S(2)}) copy-start(bf16[2,128,256]{2,1,0:T(8,128)(2,1)S(1)} %collective-permute-done.24.rest_6_) | copy-start | bytes 393220
  97.8 30.0 %collective-permute-start.4 = (bf16[2,128,256]{2,1,0:T(8,128)(2,1)S(1)}, bf16[2,128,256]{2,1,0:T(8,128)(2,1)S(1)}, u32[]{:S(2)}, u32[]{:S(2)}) collective-permute-start(bf16[2,128,256]{2,1,0:T(8,128)(2,1)S(1)} %pad_maximum_fusion.6), channel_id=1, source_target_pairs={{0,6},{1,7},{2,4},{3,5},{4,2},{5,3},{6,0},{7,1},{8,14},{9,15},{10,... | collective-permute-start | bytes 393224 | tf_op jit(solution)/shard_map/ppermute | solution.py:575
  99.9 26.7 %copy-start.25 = (bf16[2,128,256]{2,1,0:T(8,128)(2,1)}, bf16[2,128,256]{2,1,0:T(8,128)(2,1)S(1)}, u32[]{:S(2)}) copy-start(bf16[2,128,256]{2,1,0:T(8,128)(2,1)S(1)} %collective-permute-done.8.rest_6_) | copy-start | bytes 393220
  99.9 27.9 %collective-permute-start.3 = (bf16[2,128,256]{2,1,0:T(8,128)(2,1)S(1)}, bf16[2,128,256]{2,1,0:T(8,128)(2,1)}, u32[]{:S(2)}, u32[]{:S(2)}) collective-permute-start(bf16[2,128,256]{2,1,0:T(8,128)(2,1)S(1)} %pad_maximum_fusion.5), channel_id=1, source_target_pairs={{0,4},{1,5},{2,6},{3,7},{4,0},{5,1},{6,2},{7,3},{8,12},{9,13},{10,... | collective-permute-start | bytes 393224 | tf_op jit(solution)/shard_map/ppermute | solution.py:575
  103.2 1.6 copy-start.26
  103.2 24.6 %collective-permute-start.2 = (bf16[2,128,256]{2,1,0:T(8,128)(2,1)S(1)}, bf16[2,128,256]{2,1,0:T(8,128)(2,1)S(1)}, u32[]{:S(2)}, u32[]{:S(2)}) collective-permute-start(bf16[2,128,256]{2,1,0:T(8,128)(2,1)S(1)} %pad_maximum_fusion.4), channel_id=1, source_target_pairs={{0,2},{1,3},{2,0},{3,1},{4,6},{5,7},{6,4},{7,5},{8,10},{9,11},{10,... | collective-permute-start | bytes 393224 | tf_op jit(solution)/shard_map/ppermute | solution.py:575
  127.7 26.1 %collective-permute-start.25 = (bf16[1,8,160,128]{3,2,1,0:T(8,128)(2,1)S(1)}, bf16[1,8,160,128]{3,2,1,0:T(8,128)(2,1)S(1)}, u32[]{:S(2)}, u32[]{:S(2)}) collective-permute-start(bf16[1,8,160,128]{3,2,1,0:T(8,128)(2,1)S(1)} %slice.323), channel_id=1, source_target_pairs={{0,1},{1,0},{2,3},{3,2},{4,5},{5,4},{6,7},{7,6},{8,9},{9,8},{10,11... | collective-permute-start | bytes 983048 | tf_op jit(solution)/shard_map/ppermute | solution.py:575
  127.8 0.6 copy-start.30
  127.8 0.7 copy-start.31
  127.8 0.7 copy-start.32
  150.3 32.6 %copy-start.19 = (f32[4096]{0:T(1024)S(1)}, f32[4096]{0:T(1024)}, u32[]{:S(2)}) copy-start(f32[4096]{0:T(1024)} %param.10) | copy-start | bytes 49156
  152.3 9.5 %collective-permute-start.9 = (bf16[1,8,160,128]{3,2,1,0:T(8,128)(2,1)S(1)}, bf16[1,8,160,128]{3,2,1,0:T(8,128)(2,1)S(1)}, u32[]{:S(2)}, u32[]{:S(2)}) collective-permute-start(bf16[1,8,160,128]{3,2,1,0:T(8,128)(2,1)S(1)} %slice.299), channel_id=1, source_target_pairs={{0,1},{1,0},{2,3},{3,2},{4,5},{5,4},{6,7},{7,6},{8,9},{9,8},{10,11... | collective-permute-start | bytes 983048 | tf_op jit(solution)/shard_map/ppermute | solution.py:575
  153.8 40.8 %copy-start.2 = (bf16[1,8,160,128]{3,2,1,0:T(8,128)(2,1)}, bf16[1,8,160,128]{3,2,1,0:T(8,128)(2,1)S(1)}, u32[]{:S(2)}) copy-start(bf16[1,8,160,128]{3,2,1,0:T(8,128)(2,1)S(1)} %collective-permute-done.25.other) | copy-start | bytes 983044
  153.8 9.3 %collective-permute-start.32 = (bf16[2,160,128]{2,1,0:T(8,128)(2,1)S(1)}, bf16[2,160,128]{2,1,0:T(8,128)(2,1)S(1)}, u32[]{:S(2)}, u32[]{:S(2)}) collective-permute-start(bf16[2,160,128]{2,1,0:T(8,128)(2,1)S(1)} %pad_maximum_fusion.31), channel_id=1, source_target_pairs={{0,14},{1,15},{2,12},{3,13},{4,10},{5,11},{6,8},{7,9},{8,6},{9,7},... | collective-permute-start | bytes 245768 | tf_op jit(solution)/shard_map/ppermute | solution.py:575
  157.1 11.4 %collective-permute-start.31 = (bf16[2,160,128]{2,1,0:T(8,128)(2,1)S(1)}, bf16[2,160,128]{2,1,0:T(8,128)(2,1)S(1)}, u32[]{:S(2)}, u32[]{:S(2)}) collective-permute-start(bf16[2,160,128]{2,1,0:T(8,128)(2,1)S(1)} %pad_maximum_fusion.30), channel_id=1, source_target_pairs={{0,12},{1,13},{2,14},{3,15},{4,8},{5,9},{6,10},{7,11},{8,4},{9,5},... | collective-permute-start | bytes 245768 | tf_op jit(solution)/shard_map/ppermute | solution.py:575
  157.8 13.9 %collective-permute-start.30 = (bf16[2,160,128]{2,1,0:T(8,128)(2,1)S(1)}, bf16[2,160,128]{2,1,0:T(8,128)(2,1)S(1)}, u32[]{:S(2)}, u32[]{:S(2)}) collective-permute-start(bf16[2,160,128]{2,1,0:T(8,128)(2,1)S(1)} %pad_maximum_fusion.29), channel_id=1, source_target_pairs={{0,10},{1,11},{2,8},{3,9},{4,14},{5,15},{6,12},{7,13},{8,2},{9,3},... | collective-permute-start | bytes 245768 | tf_op jit(solution)/shard_map/ppermute | solution.py:575
  160.7 14.2 %collective-permute-start.29 = (bf16[2,160,128]{2,1,0:T(8,128)(2,1)S(1)}, bf16[2,160,128]{2,1,0:T(8,128)(2,1)S(1)}, u32[]{:S(2)}, u32[]{:S(2)}) collective-permute-start(bf16[2,160,128]{2,1,0:T(8,128)(2,1)S(1)} %pad_maximum_fusion.28), channel_id=1, source_target_pairs={{0,8},{1,9},{2,10},{3,11},{4,12},{5,13},{6,14},{7,15},{8,0},{9,1},... | collective-permute-start | bytes 245768 | tf_op jit(solution)/shard_map/ppermute | solution.py:575
  161.8 38.0 %copy-start.1 = (bf16[1,8,160,128]{3,2,1,0:T(8,128)(2,1)}, bf16[1,8,160,128]{3,2,1,0:T(8,128)(2,1)S(1)}, u32[]{:S(2)}) copy-start(bf16[1,8,160,128]{3,2,1,0:T(8,128)(2,1)S(1)} %collective-permute-done.9.other) | copy-start | bytes 983044
  161.8 13.8 %collective-permute-start.28 = (bf16[2,160,128]{2,1,0:T(8,128)(2,1)S(1)}, bf16[2,160,128]{2,1,0:T(8,128)(2,1)S(1)}, u32[]{:S(2)}, u32[]{:S(2)}) collective-permute-start(bf16[2,160,128]{2,1,0:T(8,128)(2,1)S(1)} %pad_maximum_fusion.27), channel_id=1, source_target_pairs={{0,6},{1,7},{2,4},{3,5},{4,2},{5,3},{6,0},{7,1},{8,14},{9,15},{10,... | collective-permute-start | bytes 245768 | tf_op jit(solution)/shard_map/ppermute | solution.py:575
  163.2 31.4 %copy-start.12 = (bf16[2,160,128]{2,1,0:T(8,128)(2,1)}, bf16[2,160,128]{2,1,0:T(8,128)(2,1)S(1)}, u32[]{:S(2)}) copy-start(bf16[2,160,128]{2,1,0:T(8,128)(2,1)S(1)} %collective-permute-done.32.rest_6_) | copy-start | bytes 245764
  163.2 12.5 %collective-permute-start.27 = (bf16[2,160,128]{2,1,0:T(8,128)(2,1)S(1)}, bf16[2,160,128]{2,1,0:T(8,128)(2,1)S(1)}, u32[]{:S(2)}, u32[]{:S(2)}) collective-permute-start(bf16[2,160,128]{2,1,0:T(8,128)(2,1)S(1)} %pad_maximum_fusion.26), channel_id=1, source_target_pairs={{0,4},{1,5},{2,6},{3,7},{4,0},{5,1},{6,2},{7,3},{8,12},{9,13},{10,... | collective-permute-start | bytes 245768 | tf_op jit(solution)/shard_map/ppermute | solution.py:575
  168.5 26.1 %copy-start.13 = (bf16[2,160,128]{2,1,0:T(8,128)(2,1)}, bf16[2,160,128]{2,1,0:T(8,128)(2,1)S(1)}, u32[]{:S(2)}) copy-start(bf16[2,160,128]{2,1,0:T(8,128)(2,1)S(1)} %collective-permute-done.31.rest_5_) | copy-start | bytes 245764
  168.5 11.0 %collective-permute-start.26 = (bf16[2,160,128]{2,1,0:T(8,128)(2,1)S(1)}, bf16[2,160,128]{2,1,0:T(8,128)(2,1)S(1)}, u32[]{:S(2)}, u32[]{:S(2)}) collective-permute-start(bf16[2,160,128]{2,1,0:T(8,128)(2,1)S(1)} %pad_maximum_fusion.25), channel_id=1, source_target_pairs={{0,2},{1,3},{2,0},{3,1},{4,6},{5,7},{6,4},{7,5},{8,10},{9,11},{10,... | collective-permute-start | bytes 245768 | tf_op jit(solution)/shard_map/ppermute | solution.py:575
  171.7 22.9 %copy-start.14 = (bf16[2,160,128]{2,1,0:T(8,128)(2,1)}, bf16[2,160,128]{2,1,0:T(8,128)(2,1)S(1)}, u32[]{:S(2)}) copy-start(bf16[2,160,128]{2,1,0:T(8,128)(2,1)S(1)} %collective-permute-done.30.rest_4_) | copy-start | bytes 245764
  171.7 8.6 %collective-permute-start.16 = (bf16[2,160,128]{2,1,0:T(8,128)(2,1)S(1)}, bf16[2,160,128]{2,1,0:T(8,128)(2,1)S(1)}, u32[]{:S(2)}, u32[]{:S(2)}) collective-permute-start(bf16[2,160,128]{2,1,0:T(8,128)(2,1)S(1)} %pad_maximum_fusion.24), channel_id=1, source_target_pairs={{0,14},{1,15},{2,12},{3,13},{4,10},{5,11},{6,8},{7,9},{8,6},{9,7},... | collective-permute-start | bytes 245768 | tf_op jit(solution)/shard_map/ppermute | solution.py:575
  174.8 19.7 %copy-start.15 = (bf16[2,160,128]{2,1,0:T(8,128)(2,1)}, bf16[2,160,128]{2,1,0:T(8,128)(2,1)S(1)}, u32[]{:S(2)}) copy-start(bf16[2,160,128]{2,1,0:T(8,128)(2,1)S(1)} %collective-permute-done.29.rest_3_) | copy-start | bytes 245764
  174.8 6.7 %collective-permute-start.15 = (bf16[2,160,128]{2,1,0:T(8,128)(2,1)S(1)}, bf16[2,160,128]{2,1,0:T(8,128)(2,1)S(1)}, u32[]{:S(2)}, u32[]{:S(2)}) collective-permute-start(bf16[2,160,128]{2,1,0:T(8,128)(2,1)S(1)} %pad_maximum_fusion.23), channel_id=1, source_target_pairs={{0,12},{1,13},{2,14},{3,15},{4,8},{5,9},{6,10},{7,11},{8,4},{9,5},... | collective-permute-start | bytes 245768 | tf_op jit(solution)/shard_map/ppermute | solution.py:575
  175.6 18.9 %copy-start.16 = (bf16[2,160,128]{2,1,0:T(8,128)(2,1)}, bf16[2,160,128]{2,1,0:T(8,128)(2,1)S(1)}, u32[]{:S(2)}) copy-start(bf16[2,160,128]{2,1,0:T(8,128)(2,1)S(1)} %collective-permute-done.28.rest_2_) | copy-start | bytes 245764
  175.6 24.2 %collective-permute-start.14 = (bf16[2,160,128]{2,1,0:T(8,128)(2,1)S(1)}, bf16[2,160,128]{2,1,0:T(8,128)(2,1)S(1)}, u32[]{:S(2)}, u32[]{:S(2)}) collective-permute-start(bf16[2,160,128]{2,1,0:T(8,128)(2,1)S(1)} %pad_maximum_fusion.22), channel_id=1, source_target_pairs={{0,10},{1,11},{2,8},{3,9},{4,14},{5,15},{6,12},{7,13},{8,2},{9,3},... | collective-permute-start | bytes 245768 | tf_op jit(solution)/shard_map/ppermute | solution.py:575
  175.7 18.8 %copy-start.17 = (bf16[2,160,128]{2,1,0:T(8,128)(2,1)}, bf16[2,160,128]{2,1,0:T(8,128)(2,1)S(1)}, u32[]{:S(2)}) copy-start(bf16[2,160,128]{2,1,0:T(8,128)(2,1)S(1)} %collective-permute-done.27.rest_1_) | copy-start | bytes 245764
  175.7 24.2 %collective-permute-start.13 = (bf16[2,160,128]{2,1,0:T(8,128)(2,1)S(1)}, bf16[2,160,128]{2,1,0:T(8,128)(2,1)S(1)}, u32[]{:S(2)}, u32[]{:S(2)}) collective-permute-start(bf16[2,160,128]{2,1,0:T(8,128)(2,1)S(1)} %pad_maximum_fusion.21), channel_id=1, source_target_pairs={{0,8},{1,9},{2,10},{3,11},{4,12},{5,13},{6,14},{7,15},{8,0},{9,1},... | collective-permute-start | bytes 245768 | tf_op jit(solution)/shard_map/ppermute | solution.py:575
  179.4 15.1 %copy-start.18 = (bf16[2,160,128]{2,1,0:T(8,128)(2,1)}, bf16[2,160,128]{2,1,0:T(8,128)(2,1)S(1)}, u32[]{:S(2)}) copy-start(bf16[2,160,128]{2,1,0:T(8,128)(2,1)S(1)} %collective-permute-done.26.rest_0_) | copy-start | bytes 245764
  179.4 20.5 %collective-permute-start.12 = (bf16[2,160,128]{2,1,0:T(8,128)(2,1)S(1)}, bf16[2,160,128]{2,1,0:T(8,128)(2,1)S(1)}, u32[]{:S(2)}, u32[]{:S(2)}) collective-permute-start(bf16[2,160,128]{2,1,0:T(8,128)(2,1)S(1)} %pad_maximum_fusion.20), channel_id=1, source_target_pairs={{0,6},{1,7},{2,4},{3,5},{4,2},{5,3},{6,0},{7,1},{8,14},{9,15},{10,... | collective-permute-start | bytes 245768 | tf_op jit(solution)/shard_map/ppermute | solution.py:575
  180.3 19.6 %copy-start.5 = (bf16[2,160,128]{2,1,0:T(8,128)(2,1)}, bf16[2,160,128]{2,1,0:T(8,128)(2,1)S(1)}, u32[]{:S(2)}) copy-start(bf16[2,160,128]{2,1,0:T(8,128)(2,1)S(1)} %collective-permute-done.16.rest_6_) | copy-start | bytes 245764
  180.3 19.6 %collective-permute-start.11 = (bf16[2,160,128]{2,1,0:T(8,128)(2,1)S(1)}, bf16[2,160,128]{2,1,0:T(8,128)(2,1)S(1)}, u32[]{:S(2)}, u32[]{:S(2)}) collective-permute-start(bf16[2,160,128]{2,1,0:T(8,128)(2,1)S(1)} %pad_maximum_fusion.19), channel_id=1, source_target_pairs={{0,4},{1,5},{2,6},{3,7},{4,0},{5,1},{6,2},{7,3},{8,12},{9,13},{10,... | collective-permute-start | bytes 245768 | tf_op jit(solution)/shard_map/ppermute | solution.py:575
  181.6 18.4 %copy-start.6 = (bf16[2,160,128]{2,1,0:T(8,128)(2,1)}, bf16[2,160,128]{2,1,0:T(8,128)(2,1)S(1)}, u32[]{:S(2)}) copy-start(bf16[2,160,128]{2,1,0:T(8,128)(2,1)S(1)} %collective-permute-done.15.rest_5_) | copy-start | bytes 245764
  181.6 18.4 %collective-permute-start.10 = (bf16[2,160,128]{2,1,0:T(8,128)(2,1)S(1)}, bf16[2,160,128]{2,1,0:T(8,128)(2,1)S(1)}, u32[]{:S(2)}, u32[]{:S(2)}) collective-permute-start(bf16[2,160,128]{2,1,0:T(8,128)(2,1)S(1)} %pad_maximum_fusion.18), channel_id=1, source_target_pairs={{0,2},{1,3},{2,0},{3,1},{4,6},{5,7},{6,4},{7,5},{8,10},{9,11},{10,... | collective-permute-start | bytes 245768 | tf_op jit(solution)/shard_map/ppermute | solution.py:575
  199.9 0.6 copy-start.8
  199.9 0.7 copy-start.9
  199.9 0.7 copy-start.10
  200.0 0.7 copy-start.11
  (2 other events, 1.3 us)

commit v2 on v1

v2 whole, which is shorter than its diff:
```python
import functools
import math

import jax
import jax.numpy as jnp
from jax import lax
from jax.experimental import pallas as pl
from jax.experimental.pallas import tpu as pltpu
from jax.sharding import PartitionSpec as P

HIGH_PRECISION = lax.Precision.HIGH
LANES = 128
HALO = 8
FINE_PRODUCT = 256
UNROLL = 8
CHIP_GROUP = 4
FINISH_GROUP = 4
CHIP_ORDER = (4, 1, 5, 2, 6, 3, 7)
SINE = (1.0, -1.0 / 6, 1.0 / 120, -1.0 / 5040, 1.0 / 362880, -1.0 / 39916800, 1.0 / 6227020800)


def make_tables(devices, rows):
    length = devices * rows
    halves = jnp.arange(2, dtype=jnp.int32)
    coarse = jnp.arange(devices, dtype=jnp.int32)
    fine_pos = jnp.arange(rows, dtype=jnp.int32)
    outer_turn = (
        coarse[None, None, :] * (2 * coarse[None, :, None] + halves[:, None, None]) % (2 * devices)
    )
    outer_angle = -math.pi / devices * outer_turn.astype(jnp.float32)
    twist_turn = (
        fine_pos[None, None, :] * (2 * coarse[None, :, None] + halves[:, None, None]) % (2 * length)
    )
    twist_angle = -math.pi / length * twist_turn.astype(jnp.float32)
    inner_turn = fine_pos[:, None] * fine_pos[None, :] % rows
    inner_angle = -2.0 * math.pi / rows * inner_turn.astype(jnp.float32)
    outer_stack = jnp.stack([jnp.cos(outer_angle), jnp.sin(outer_angle)])
    inverse_outer = outer_stack * (0.5 / length)
    inner_cos = jnp.cos(inner_angle)
    inner_sin = jnp.sin(inner_angle)
    forward_inner = jnp.stack(
        [jnp.stack([inner_cos, -inner_sin]), jnp.stack([inner_sin, inner_cos])]
    )
    inverse_inner = jnp.stack(
        [jnp.stack([inner_cos, inner_sin]), jnp.stack([-inner_sin, inner_cos])]
    )
    return (
        outer_stack,
        inverse_outer,
        jnp.cos(twist_angle)[:, None],
        jnp.sin(twist_angle)[:, None],
        forward_inner,
        inverse_inner,
    )


def forward_transform(signal, tables):
    outer_stack, inverse_outer, twist_re, twist_im, forward_inner, inverse_inner = tables
    first = jnp.einsum(
        "rbkp,cpj->rbckj", outer_stack, signal.astype(jnp.float32), precision=HIGH_PRECISION
    )
    turned = jnp.stack(
        [first[0] * twist_re - first[1] * twist_im, first[0] * twist_im + first[1] * twist_re]
    )
    return jnp.einsum("rsmj,sbckj->rbckm", forward_inner, turned, precision=HIGH_PRECISION)


def inverse_transform(spectrum, tables):
    outer_stack, inverse_outer, twist_re, twist_im, forward_inner, inverse_inner = tables
    back = jnp.einsum("rsjm,sbckm->rbckj", inverse_inner, spectrum, precision=HIGH_PRECISION)
    turned = jnp.stack(
        [back[0] * twist_re + back[1] * twist_im, back[1] * twist_re - back[0] * twist_im]
    )
    return jnp.einsum("rbkp,rbckj->cpj", inverse_outer, turned, precision=HIGH_PRECISION)


def filter_spectrum(residue_local, rate_local, skip_local, devices, rows):
    length = devices * rows
    halves = jnp.arange(2, dtype=jnp.int32)[:, None, None, None]
    coarse = jnp.arange(devices, dtype=jnp.int32)[None, None, :, None]
    fine_pos = jnp.arange(rows, dtype=jnp.int32)[None, None, None, :]
    frequency = 2 * (coarse + devices * fine_pos) + halves
    half_angle = math.pi / (2 * length) * frequency.astype(jnp.float32)
    sine_half = jnp.sin(half_angle)
    sine_sq = sine_half * sine_half
    sine_full = 2.0 * sine_half * jnp.cos(half_angle)
    parity_sign = (1 - 2 * halves).astype(jnp.float32)
    local_width = residue_local.shape[1]
    kernel_re = jnp.zeros((2, local_width, devices, rows), jnp.float32)
    kernel_im = jnp.zeros((2, local_width, devices, rows), jnp.float32)
    for mode_index in range(residue_local.shape[0]):
        rate_row = rate_local[mode_index][None, :, None, None]
        amplitude = residue_local[mode_index][None, :, None, None] * jnp.sqrt(rate_row)
        decay_factor = jnp.exp(-rate_row)
        decay_gap = -jnp.expm1(-rate_row)
        tail_factor = jnp.exp(-rate_row * length)
        denominator = decay_gap * decay_gap + 4.0 * decay_factor * sine_sq
        weighting = amplitude * (1.0 - tail_factor * parity_sign) / denominator
        kernel_re = kernel_re + weighting * (decay_gap + 2.0 * decay_factor * sine_sq)
        kernel_im = kernel_im - weighting * decay_factor * sine_full
    kernel_re = kernel_re + skip_local[None, :, None, None]
    return (kernel_re, kernel_im)


def times_kernel(spectrum, kernel_re, kernel_im):
    return jnp.stack(
        [
            spectrum[0] * kernel_re - spectrum[1] * kernel_im,
            spectrum[0] * kernel_im + spectrum[1] * kernel_re,
        ]
    )


def on_device(proj, short_weight, residues, rates, skip, grad_out):
    devices = lax.axis_size("seq")
    rows = proj.shape[0]
    channels = grad_out.shape[1]
    local_width = channels // devices
    length = devices * rows
    tap_count = short_weight.shape[0]
    first_channel = lax.axis_index("seq") * local_width
    residue_local = lax.dynamic_slice_in_dim(residues, first_channel, local_width, 1)
    rate_local = lax.dynamic_slice_in_dim(rates, first_channel, local_width, 1)
    skip_local = lax.dynamic_slice_in_dim(skip, first_channel, local_width, 0)
    tables = make_tables(devices, rows)
    kernel_re, kernel_im = filter_spectrum(residue_local, rate_local, skip_local, devices, rows)
    arranged = proj.T.reshape(3, devices, local_width, 1, rows)
    streams = lax.all_to_all(arranged, "seq", split_axis=1, concat_axis=3, tiled=True).reshape(
        3, local_width, length
    )
    weight_local = lax.dynamic_slice_in_dim(
        short_weight.reshape(tap_count, 3, channels), first_channel, local_width, 2
    )
    padded = jnp.pad(streams, ((0, 0), (0, 0), (tap_count - 1, 0)))
    filtered = jnp.zeros((3, local_width, length), jnp.float32)
    for tap_index in range(tap_count):
        offset = tap_count - 1 - tap_index
        filtered = filtered + weight_local[tap_index][:, :, None] * padded[
            :, :, offset : offset + length
        ].astype(jnp.float32)
    query_part = filtered[0].reshape(local_width, devices, rows)
    mixed = (filtered[1] * filtered[2]).astype(jnp.bfloat16).reshape(local_width, devices, rows)
    cot_arranged = grad_out.T.reshape(devices, local_width, 1, rows)
    cotangent = lax.all_to_all(
        cot_arranged, "seq", split_axis=0, concat_axis=2, tiled=True
    ).reshape(local_width, devices, rows)
    mixed_spec = forward_transform(mixed, tables)
    conv = inverse_transform(times_kernel(mixed_spec, kernel_re, kernel_im), tables).astype(
        jnp.bfloat16
    )
    gated = (query_part * conv.astype(jnp.float32)).astype(jnp.bfloat16)
    gated_rows = lax.all_to_all(
        gated.reshape(1, local_width, devices, rows), "seq", split_axis=2, concat_axis=0, tiled=True
    )
    gated_output = gated_rows.reshape(channels, rows).T
    scaled = (query_part * cotangent.astype(jnp.float32)).astype(jnp.bfloat16)
    scaled_spec = forward_transform(scaled, tables)
    lag_spec = jnp.stack(
        [
            mixed_spec[0] * scaled_spec[0] + mixed_spec[1] * scaled_spec[1],
            mixed_spec[0] * scaled_spec[1] - mixed_spec[1] * scaled_spec[0],
        ]
    )
    lagged = inverse_transform(lag_spec, tables)
    lagged_rows = lax.all_to_all(
        lagged.reshape(1, local_width, devices, rows),
        "seq",
        split_axis=2,
        concat_axis=0,
        tiled=True,
    )
    filter_grad = lagged_rows.reshape(channels, rows).T
    return (gated_output, filter_grad)


def split_pair(value):
    high = value.astype(jnp.bfloat16)
    low = (value - high.astype(jnp.float32)).astype(jnp.bfloat16)
    return (high, low)


def split_outside(value):
    high = lax.reduce_precision(value, 8, 7)
    return (high.astype(jnp.bfloat16), (value - high).astype(jnp.bfloat16))


def dot32(left, right):
    return jnp.dot(left, right, preferred_element_type=jnp.float32)


def cosines(turns, whole):
    folded = jnp.bitwise_and(turns + whole // 2, whole - 1) - whole // 2
    angle = (2.0 * math.pi / whole) * (whole // 4 - jnp.abs(folded)).astype(jnp.float32)
    square = angle * angle
    series = jnp.full_like(angle, SINE[-1])
    for factor in SINE[-2::-1]:
        series = series * square + factor
    return angle * series


def grid_of(height, width, zero):
    shape = (height, width)
    return (
        lax.broadcasted_iota(jnp.int32, shape, 0) + zero,
        lax.broadcasted_iota(jnp.int32, shape, 1) + zero,
    )


def spectral_tables(devices, rows, zero):
    fine = FINE_PRODUCT // devices
    line, lane = grid_of(2 * rows, 2 * rows, zero)
    quarter = (line // rows - lane // rows) * (rows // 4)
    base = cosines((line % rows) * (lane % rows) + quarter, rows)
    base_back = cosines((line % rows) * (lane % rows) - quarter, rows)
    line, lane = grid_of(2 * FINE_PRODUCT, FINE_PRODUCT, zero)
    coarse = line % FINE_PRODUCT // fine
    outer = jnp.where(
        line % fine == lane % fine,
        cosines((2 * coarse + 1) * (lane // fine) + line // FINE_PRODUCT * devices, 4 * devices),
        0.0,
    )
    line, lane = grid_of(FINE_PRODUCT, 2 * FINE_PRODUCT, zero)
    coarse = lane % FINE_PRODUCT // fine
    outer_back = jnp.where(
        line % fine == lane % fine,
        cosines((2 * coarse + 1) * (line // fine) + lane // FINE_PRODUCT * devices, 4 * devices)
        * (1.0 / (devices * rows)),
        0.0,
    )
    line, lane = grid_of(FINE_PRODUCT, LANES, zero)
    odd = 2 * (line // fine) + 1
    length = devices * rows
    first = odd * (line % fine)
    twist = jnp.stack(
        [
            cosines(first, 4 * length),
            cosines(first - length, 4 * length),
            cosines(odd * fine, 4 * length),
            cosines(odd * fine - length, 4 * length),
        ]
    )
    packed = [
        jnp.concatenate(split_outside(table), axis=0)
        for table in (base, base_back, outer, outer_back)
    ]
    return (*packed, twist)


def mix_body(where, query_in, key_in, value_in, before_q, before_k, before_v, weight_q, weight_k, weight_v, cot, kept, given, query_out, mixed_out, padded):
    taps = weight_q.shape[0]
    rows = query_in.shape[0]
    tail = before_q.shape[0]
    chip, core = where[0], where[1]
    streams = ((query_in, before_q, weight_q), (key_in, before_k, weight_k), (value_in, before_v, weight_v))
    for index, (block, before, _) in enumerate(streams):
        padded[index, :tail, :] = before[...].astype(jnp.float32)
        padded[index, tail:, :] = block[...].astype(jnp.float32)
    group = kept.shape[0]
    for index in range(group):
        slot = index ^ (chip % group)
        for side, sent in enumerate((kept, given)):
            piece = 2 * index + (core ^ side)
            lanes = pl.ds(pl.multiple_of(piece * LANES, LANES), LANES)
            filtered = []
            for stream, (_, _, weight) in enumerate(streams):
                total = None
                for tap in range(taps):
                    term = weight[tap : tap + 1, lanes] * padded[stream, tail - tap : tail - tap + rows, lanes]
                    total = term if total is None else total + term
                filtered.append(total)
            mixed = (filtered[1] * filtered[2]).astype(jnp.bfloat16)
            scaled = (filtered[0] * cot[:, lanes].astype(jnp.float32)).astype(jnp.bfloat16)
            query_out[:, lanes] = filtered[0]
            mixed_out[:, lanes] = mixed
            sent[slot, :, :LANES] = mixed
            sent[slot, :, LANES:] = scaled


def mix_streams(where, proj, before, short_weight, grad_out, chunk, chunks, devices):
    rows, channels = grad_out.shape
    taps = short_weight.shape[0]
    tail = before.shape[0]
    chips = devices // 2
    group = CHIP_GROUP
    step = 2 * group * LANES
    steps = channels // chunks // step
    base = chunk * steps
    stride = channels // step

    def stream_spec(height, stream):
        return pl.BlockSpec((height, step), lambda g, w, s=stream: (0, s * stride + base + g))

    return pl.pallas_call(
        mix_body,
        grid_spec=pltpu.PrefetchScalarGridSpec(
            num_scalar_prefetch=1,
            grid=(steps,),
            in_specs=[stream_spec(rows, s) for s in range(3)]
            + [stream_spec(tail, s) for s in range(3)]
            + [stream_spec(taps, s) for s in range(3)]
            + [pl.BlockSpec((rows, step), lambda g, w: (0, base + g))],
            out_specs=[
                pl.BlockSpec((group, rows, 2 * LANES), lambda g, w: (g ^ (w[0] // group), 0, 0)),
                pl.BlockSpec((group, rows, 2 * LANES), lambda g, w: (g ^ (w[0] // group), 0, 0)),
                pl.BlockSpec((rows, step), lambda g, w: (0, g)),
                pl.BlockSpec((rows, step), lambda g, w: (0, g)),
            ],
            scratch_shapes=[pltpu.VMEM((3, tail + rows, step), jnp.float32)],
        ),
        out_shape=[
            jax.ShapeDtypeStruct((chips, rows, 2 * LANES), jnp.bfloat16),
            jax.ShapeDtypeStruct((chips, rows, 2 * LANES), jnp.bfloat16),
            jax.ShapeDtypeStruct((rows, channels // chunks), jnp.float32),
            jax.ShapeDtypeStruct((rows, channels // chunks), jnp.bfloat16),
        ],
        cost_estimate=pl.CostEstimate(
            flops=3_000_000, transcendentals=0, bytes_accessed=5_000_000
        ),
        name="mix",
    )(where, *[proj] * 3, *[before] * 3, *[short_weight] * 3, grad_out)


def near_body(mixed, decay, gain, skip, near_out, spread, answer):
    rows, width = mixed.shape
    tiles = width // LANES
    modes = decay.shape[0]
    lines = rows * tiles
    for piece in range(tiles):
        lanes = slice(piece * LANES, (piece + 1) * LANES)
        block = mixed[:, lanes].astype(jnp.float32)
        spread[pl.ds(piece, rows, stride=tiles), :] = block
    for group in range(tiles // 8):
        part = slice(group * 8, group * 8 + 8)
        decays = [decay[r, part, :] for r in range(modes)]
        gains = [gain[r, part, :] for r in range(modes)]
        direct = skip[part, :]

        def step(t, states, group=group, decays=decays, gains=gains, direct=direct):
            at = pl.ds(pl.multiple_of(t * tiles + group * 8, 8), 8)
            here = spread[at, :]
            states = [d * h + here for d, h in zip(decays, states)]
            terms = [g * h for g, h in zip(gains, states)] + [direct * here]
            while len(terms) > 1:
                terms = [a + b for a, b in zip(terms[::2], terms[1::2])] + (
                    terms[-1:] if len(terms) % 2 else []
                )
            answer[at, :] = terms[0]
            return states

        start = [jnp.zeros((8, LANES), jnp.float32)] * modes
        lax.fori_loop(0, rows, step, start, unroll=4)
    for piece in range(tiles):
        lanes = slice(piece * LANES, (piece + 1) * LANES)
        near_out[:, lanes] = answer[pl.ds(piece, rows, stride=tiles), :]


def near_part(mixed, decay, gain, skip):
    rows, width = mixed.shape
    tiles = width // LANES
    return pl.pallas_call(
        near_body,
        out_shape=jax.ShapeDtypeStruct((rows, width), jnp.float32),
        scratch_shapes=[
            pltpu.VMEM((rows * tiles, LANES), jnp.float32),
            pltpu.VMEM((rows * tiles, LANES), jnp.float32),
        ],
        cost_estimate=pl.CostEstimate(
            flops=4_000_000, transcendentals=0, bytes_accessed=8_000_000
        ),
        name="near",
    )(mixed, decay, gain, skip)


def lag_body(chips, where, own, other, *rest):
    sources = rest[: chips - 1]
    (rate, amplitude, forward, backward, outer_forward, outer_backward, twist, out,
     stacked, lined, high, low, back, turns) = rest[chips - 1 :]
    chip, core = where[0], where[1]
    devices = 2 * chips
    rows = own.shape[-2]
    fine = FINE_PRODUCT // devices
    groups = rows // fine
    modes = rate.shape[0]

    for turned in range(chips):
        for side in range(2):
            position = 2 * (turned ^ chip) + (side ^ core)
            at = pl.ds(pl.multiple_of(position * fine, fine), fine)
            whole = (own, other)[side][0] if turned == 0 else sources[turned - 1][side]
            for group in range(groups):
                stacked[group, at, :] = whole[group * fine : (group + 1) * fine, :]
            lined[position] = whole[:, :LANES].astype(jnp.float32)

    turns[0, 0] = twist[0]
    turns[0, 1] = twist[1]
    for group in range(1, groups):
        cos, sin = turns[group - 1, 0], turns[group - 1, 1]
        turns[group, 0] = cos * twist[2] - sin * twist[3]
        turns[group, 1] = sin * twist[2] + cos * twist[3]

    def outer_step(group, carry):
        signal = stacked[group]
        first = dot32(outer_forward[: 2 * FINE_PRODUCT, :], signal) + dot32(
            outer_forward[2 * FINE_PRODUCT :, :], signal
        )
        cos, sin = turns[group, 0], turns[group, 1]
        cos = jnp.concatenate([cos, cos], axis=1)
        sin = jnp.concatenate([sin, sin], axis=1)
        real, imag = first[:FINE_PRODUCT], first[FINE_PRODUCT:]
        pairs = (split_pair(real * cos + imag * sin), split_pair(imag * cos - real * sin))
        for k in range(devices):
            source = slice(k * fine, (k + 1) * fine)
            for part in range(2):
                at = pl.ds(pl.multiple_of(part * rows + group * fine, fine), fine)
                high[k, at, :] = pairs[part][0][source, :]
                low[k, at, :] = pairs[part][1][source, :]
        return carry

    lax.fori_loop(0, groups, outer_step, 0, unroll=4)

    def inner_step(k, carry):
        spectrum = (
            dot32(forward[: 2 * rows], high[k])
            + dot32(forward[: 2 * rows], low[k])
            + dot32(forward[2 * rows :], high[k])
        )
        real_m, imag_m = spectrum[:rows, :LANES], spectrum[rows:, :LANES]
        real_s, imag_s = spectrum[:rows, LANES:], spectrum[rows:, LANES:]
        product = jnp.concatenate(
            [real_m * real_s + imag_m * imag_s, real_m * imag_s - imag_m * real_s], axis=0
        )
        prod_high, prod_low = split_pair(product)
        lagged = (
            dot32(backward[: 2 * rows], prod_high)
            + dot32(backward[: 2 * rows], prod_low)
            + dot32(backward[2 * rows :], prod_high)
        )
        for group in range(groups):
            for part in range(2):
                source = slice(part * rows + group * fine, part * rows + (group + 1) * fine)
                at = pl.ds(pl.multiple_of(part * FINE_PRODUCT + k * fine, fine), fine)
                back[group, at, :] = lagged[source, :]
        return carry

    lax.fori_loop(0, devices, inner_step, 0, unroll=UNROLL)

    decay = jnp.exp(-rate[...])

    def advance(t, states):
        result = []
        for p in range(devices):
            here = jnp.broadcast_to(lined[p, pl.ds(t, 1), :], (modes, LANES))
            result.append(decay * states[p] + here)
        return tuple(result)

    start = tuple(jnp.zeros((modes, LANES), jnp.float32) for _ in range(devices))
    ends = lax.fori_loop(0, rows, advance, start, unroll=8)
    far = jnp.exp(-float(rows) * rate[...])
    lead = amplitude[...] * decay
    carried = jnp.zeros((modes, LANES), jnp.float32)
    for p in range(devices):
        turned = (p // 2) ^ chip
        side = (p % 2) ^ core
        send_high, send_low = split_pair(lead * carried)
        out[side, turned, rows : rows + modes, :] = send_high
        out[side, turned, rows + modes : rows + 2 * modes, :] = send_low
        carried = far * carried + ends[p]

    def last_step(group, carry):
        cos, sin = turns[group, 0], turns[group, 1]
        real, imag = back[group, :FINE_PRODUCT, :], back[group, FINE_PRODUCT:, :]
        turned_back = jnp.concatenate([real * cos - imag * sin, real * sin + imag * cos], axis=0)
        back_high, back_low = split_pair(turned_back)
        result = (
            dot32(outer_backward[:FINE_PRODUCT, :], back_high)
            + dot32(outer_backward[:FINE_PRODUCT, :], back_low)
            + dot32(outer_backward[FINE_PRODUCT:, :], back_high)
        ).astype(jnp.bfloat16)
        at = pl.ds(pl.multiple_of(group * fine, fine), fine)
        for p in range(devices):
            turned = (p // 2) ^ chip
            side = (p % 2) ^ core
            out[side, turned, at, :] = result[p * fine : (p + 1) * fine, :]
        return carry

    lax.fori_loop(0, groups, last_step, 0, unroll=4)


def lag_part(where, sent, received, moved, rate, amplitude, tables, devices):
    rows = sent.shape[-2]
    chips = devices // 2
    modes = rate.shape[0]
    groups = rows * devices // FINE_PRODUCT
    whole = lambda shape: pl.BlockSpec(shape, lambda k, w: (0,) * len(shape))
    return pl.pallas_call(
        functools.partial(lag_body, chips),
        grid_spec=pltpu.PrefetchScalarGridSpec(
            num_scalar_prefetch=1,
            grid=(1,),
            in_specs=[whole((1, rows, 2 * LANES))] * 2
            + [whole((2, rows, 2 * LANES))] * (chips - 1)
            + [whole((modes, LANES))] * 2
            + [whole(table.shape) for table in tables],
            out_specs=[whole((2, chips, rows + 2 * modes, LANES))],
            scratch_shapes=[
                pltpu.VMEM((groups, FINE_PRODUCT, 2 * LANES), jnp.bfloat16),
                pltpu.VMEM((devices, rows, LANES), jnp.float32),
                pltpu.VMEM((devices, 2 * rows, 2 * LANES), jnp.bfloat16),
                pltpu.VMEM((devices, 2 * rows, 2 * LANES), jnp.bfloat16),
                pltpu.VMEM((groups, 2 * FINE_PRODUCT, LANES), jnp.float32),
                pltpu.VMEM((groups, 2, FINE_PRODUCT, LANES), jnp.float32),
            ],
        ),
        out_shape=[jax.ShapeDtypeStruct((2, chips, rows + 2 * modes, LANES), jnp.bfloat16)],
        cost_estimate=pl.CostEstimate(
            flops=5_000_000_000, transcendentals=0, bytes_accessed=12_000_000
        ),
        name="lags",
    )(where, sent, received, *moved, rate, amplitude, *tables)[0]


def finish_body(chips, group, where, own, other, *rest):
    sources = rest[: chips - 1]
    near, query, decay = rest[chips - 1 : chips + 2]
    gated_out, grad_out = rest[-2:]
    chip, core = where[0], where[1]
    rows = near.shape[0]
    modes = decay.shape[0]
    line = lax.broadcasted_iota(jnp.int32, (8, LANES), 0)

    def work(turned, side):
        column = 2 * ((turned ^ chip) % group) + (side ^ core)
        at = pl.ds(pl.multiple_of(column * LANES, LANES), LANES)
        block = (own, other)[side].at[0] if turned == 0 else sources[turned - 1].at[side]
        grad_out[:, at] = block[:rows, :].astype(jnp.float32)
        lead = block[rows : rows + modes, :].astype(jnp.float32) + block[
            rows + modes : rows + 2 * modes, :
        ].astype(jnp.float32)
        total = [near[8 * tile : 8 * tile + 8, at] for tile in range(rows // 8)]
        rate_here = decay[:, at]
        for mode in range(modes):
            d1 = jnp.broadcast_to(rate_here[mode : mode + 1, :], (8, LANES))
            d2 = d1 * d1
            d4 = d2 * d2
            d8 = d4 * d4
            ones = jnp.ones_like(d1)
            power = (
                jnp.where(line & 1 != 0, d1, ones)
                * jnp.where(line & 2 != 0, d2, ones)
                * jnp.where(line & 4 != 0, d4, ones)
            )
            term = power * lead[mode : mode + 1, :]
            for tile in range(rows // 8):
                total[tile] = total[tile] + term
                if tile + 1 < rows // 8:
                    term = term * d8
        conv = jnp.concatenate(total, axis=0).astype(jnp.bfloat16)
        gated_out[:, at] = (query[:, at] * conv.astype(jnp.float32)).astype(jnp.bfloat16)

    for first in range(0, chips, group):

        @pl.when(pl.program_id(0) == first // group)
        def _(first=first):
            for turned in range(first, first + group):
                for side in range(2):
                    work(turned, side)


def finish_part(where, back, back_other, moved, near, query, decay, previous, chunk, chunks, devices):
    rows, width = near.shape
    chips = devices // 2
    modes = decay.shape[0]
    height = back.shape[1]
    group = FINISH_GROUP
    step = 2 * group * LANES
    steps = width // step
    whole = lambda shape: pl.BlockSpec(shape, lambda g, w: (0,) * len(shape))
    column = lambda g, w: g ^ (w[0] // group)
    in_specs = (
        [whole((1, height, LANES))] * 2
        + [whole((2, height, LANES))] * (chips - 1)
        + [pl.BlockSpec((rows, step), lambda g, w: (0, column(g, w)))] * 2
        + [pl.BlockSpec((modes, step), lambda g, w: (0, chunk * steps + column(g, w)))]
    )
    args = [back, back_other, *moved, near, query, decay]
    aliases = {}
    if previous is not None:
        in_specs += [pl.BlockSpec(memory_space=pl.ANY)] * 2
        aliases = {len(args) + 1: 0, len(args) + 2: 1}
        args += list(previous)
    return pl.pallas_call(
        functools.partial(finish_body, chips, group),
        grid_spec=pltpu.PrefetchScalarGridSpec(
            num_scalar_prefetch=1,
            grid=(steps,),
            in_specs=in_specs,
            out_specs=[
                pl.BlockSpec((rows, step), lambda g, w: (0, chunk * steps + column(g, w)))
            ]
            * 2,
        ),
        out_shape=[
            jax.ShapeDtypeStruct((rows, width * chunks), jnp.bfloat16),
            jax.ShapeDtypeStruct((rows, width * chunks), jnp.float32),
        ],
        input_output_aliases=aliases,
        cost_estimate=pl.CostEstimate(
            flops=4_000_000, transcendentals=0, bytes_accessed=5_000_000
        ),
        name="finish",
    )(where, *args)


def swap(value, mask, devices):
    return lax.ppermute(value, "seq", [(i, i ^ mask) for i in range(devices)])


def after(value, *earlier):
    return lax.optimization_barrier((value, earlier))[0]


def hand_over(given, devices):
    return swap(given, 1, devices)


def spread_out(kept, received, devices):
    chips = devices // 2
    moved = {}
    for k in CHIP_ORDER:
        if k < chips:
            block = jnp.concatenate([kept[k : k + 1], received[k : k + 1]], axis=0)
            moved[k] = swap(block, 2 * k, devices)
    return [moved[k] for k in range(1, chips)]


def fast_on_device(proj, short_weight, residues, rates, skip, grad_out):
    devices = lax.axis_size("seq")
    rows, channels = grad_out.shape
    modes = rates.shape[0]
    chunks = channels // (devices * LANES)
    width = channels // chunks
    me = lax.axis_index("seq")
    where = jnp.stack([me // 2, me % 2]).astype(jnp.int32)
    before = lax.ppermute(
        proj[rows - HALO :], "seq", [(i, i + 1) for i in range(devices - 1)]
    )
    shape = (modes, chunks, width // LANES, LANES)
    mixes, ready = [], []
    token = before
    for chunk in range(chunks):
        kept, given, query, mixed = mix_streams(
            after(where, token), proj, before, short_weight, grad_out, chunk, chunks, devices
        )
        received = hand_over(given, devices)
        moved = spread_out(kept, received, devices)
        mixes.append((query, mixed))
        ready.append((kept, received, moved))
        token = moved[0]
    last = ready[-1][1]
    zero = after(jnp.zeros((), jnp.int32), last)
    tables = spectral_tables(devices, rows, zero)
    rates_late, residues_late, skip_late = after((rates, residues, skip), last)
    decay = jnp.exp(-rates_late)
    amplitude = residues_late * jnp.sqrt(rates_late)
    decay_tiles = decay.reshape(shape)
    gain_tiles = amplitude.reshape(shape)
    skip_tiles = skip_late.reshape(shape[1:])
    result = None
    nears, returns = [], []
    token = None
    for chunk in range(chunks):
        kept, received, moved = ready[chunk]
        near = near_part(
            after(mixes[chunk][1], tables if token is None else token),
            decay_tiles[:, chunk],
            gain_tiles[:, chunk],
            skip_tiles[chunk],
        )
        start = chunk * width + me * LANES
        rate_local = lax.dynamic_slice_in_dim(rates_late, start, LANES, 1)
        amplitude_local = lax.dynamic_slice_in_dim(amplitude, start, LANES, 1)
        guard = (token,) if chunk else (near, *[one[2][0] for one in ready[1:2]])
        back = lag_part(
            after(where, *guard), kept, received, moved, rate_local, amplitude_local, tables, devices
        )
        back_received = hand_over(back[1], devices)
        back_moved = spread_out(back[0], back_received, devices)
        nears.append(near)
        returns.append((back[0], back_received, back_moved))
        token = back_moved[0]
    for chunk in range(chunks):
        back_kept, back_received, back_moved = returns[chunk]
        result = finish_part(
            where, back_kept, back_received, back_moved, nears[chunk], mixes[chunk][0], decay,
            result, chunk, chunks, devices,
        )
    return tuple(result)


def solution(mesh):
    def body(proj, short_weight, residues, rates, skip, grad_out):
        devices = lax.axis_size("seq")
        rows, channels = grad_out.shape
        fits = (
            devices in (4, 8, 16)
            and rows % LANES == 0
            and channels % (devices * LANES) == 0
            and residues.shape[0] == 16
            and short_weight.shape[0] <= HALO + 1
        )
        chosen = fast_on_device if fits else on_device
        return chosen(proj, short_weight, residues, rates, skip, grad_out)

    return jax.shard_map(
        body,
        mesh=mesh,
        in_specs=(P(("groups", "seq"), None), P(), P(), P(), P(), P(("groups", "seq"), None)),
        out_specs=(P(("groups", "seq"), None), P(("groups", "seq"), None)),
        check_vma=False,
    )
```

time: 207 us -> 152 us (0.73)
  starting transfers between devices: 77.2 us -> 60.7 us
  Pallas kernels: 78.5 us -> 62.6 us
  local copies, waits for them, and re-layouts: 24.9 us -> 13.5 us
  other arithmetic: 19.4 us -> 9.16 us
    ppermute x32, starting transfers between devices: 74.8 us -> 58.3 us  [swap(): return lax.ppermute(value, 'seq', [(i, i ^ mask) for i in range(devices)])]
    pallas_call x4, Pallas kernels: 54.3 us -> 38.9 us  [the longest x2 28.7 us: lag_part(): pl.pallas_call(functools.partial(lag_body, chips), grid_spec=pltpu.Prefet...]
    mul x3 -> x0, local copies, waits for them, and re-layouts: 10.7 us -> none  [the longest x1 7.07 us: spectral_tables(): back_pair[:, None, :, :, None] * eye[None, :, None, None, :]]
    mul x3 -> x1, other arithmetic: 6.61 us -> 0.52 us  [cosines(): return angle * series]
    concatenate x32, other arithmetic: 6.88 us -> 3.48 us  [the longest x4 3.13 us: spectral_tables(): jnp.concatenate(split_outside(table), axis=0)]
    slice x4 -> x8, local copies, waits for them, and re-layouts: 4.15 us -> 4.07 us  [spread_out(): block = jnp.concatenate([kept[k:k + 1], received[k:k + 1]], axis=0)]
  transfers between devices with their start and end apart: 33 -> 33, of which waited for: 2 -> 6; matrix products, arithmetic and copies ran while one was open for 11% -> 13% of each run, Pallas kernels for 32% -> 34%
where the time goes in v2:
time: 152 us; the launch traced here: 151 us
  Pallas kernels  62.6 us (41%)
  starting transfers between devices  60.7 us (40%)
  local copies, waits for them, and re-layouts  13.5 us (9%)
  other arithmetic  9.16 us (6%)
  waiting for transfers between devices  3.5 us (2%)
    ppermute x32, starting transfers between devices, swap(): return lax.ppermute(value, 'seq', [(i, i ^ mask) for i in range(devices)])  58.3 us
    pallas_call x2, Pallas kernels, lag_part(): pl.pallas_call(functools.partial(lag_body, chips), grid_spec=pltpu.Prefet...  28.7 us
    pallas_call x2, Pallas kernels, mix_streams(): pl.pallas_call(mix_body, grid_spec=pltpu.PrefetchScalarGridSpec(num_scala...  12.6 us
    pallas_call x2, Pallas kernels, near_part(): pl.pallas_call(near_body, out_shape=jax.ShapeDtypeStruct((rows, width), j...  11 us
    pallas_call x2, Pallas kernels, finish_part(): pl.pallas_call(functools.partial(finish_body, chips, group), grid_spec=pl...  10.2 us
    slice x8, local copies, waits for them, and re-layouts, spread_out(): block = jnp.concatenate([kept[k:k + 1], received[k:k + 1]], axis=0)  4.07 us
    concatenate x4, other arithmetic, spectral_tables(): jnp.concatenate(split_outside(table), axis=0)  3.13 us
  transfers between devices with their start and end apart: 33, of which 6 were waited for; matrix products, arithmetic and copies ran while one was open for 13% of the time, Pallas kernels for 34%

profile of v2, /device:TPU:0, one launch (start us, length us, event | category | flops | bytes accessed | tf_op | source)
XLA Modules:
  0.0 150.8 jit_solution(17537492072902489970)
XLA Ops:
  0.6 0.9 slice.281
  1.6 2.4 %collective-permute-start = (bf16[8,12288]{1,0:T(8,128)(2,1)S(1)}, bf16[8,12288]{1,0:T(8,128)(2,1)S(1)}, u32[]{:S(2)}, u32[]{:S(2)}) collective-permute-start(bf16[8,12288]{1,0:T(8,128)(2,1)S(1)} %slice.281), channel_id=1, source_target_pairs={{0,1},{1,2},{2,3},{3,4},{4,5},{5,6},{6,7},{7,8},{8,9},{9,10},{10,1... | collective-permute-start | bytes 589832 | tf_op jit(solution)/shard_map/ppermute | solution.py:644
  4.0 0.6 pad_add_fusion.where
  5.0 0.7 copy-done
  5.7 6.3 %mix.2 = (bf16[8,128,256]{2,1,0:T(8,128)(2,1)}, bf16[8,128,256]{2,1,0:T(8,128)(2,1)}, f32[128,2048]{1,0:T(8,128)}, bf16[128,2048]{1,0:T(8,128)(2,1)}) custom-call(s32[2]{0:T(128)} %pad_add_fusion.where, bf16[128,12288]{1,0:T(8,128)(2,1)} %value_in.3, bf16[128,12288]{1,0:T(8,128)(2,1)} %value_in.3, bf16[128,12288]{1,0:T(8,128)(2,1)} %value_in.3, ...), custom_call_target="tpu_custom_call" | custom-call | flops 3000000 | bytes 5000000 | tf_op jit(solution)/shard_map/mix/pallas_call | solution.py:293
  12.0 4.2 %collective-permute-start.1 = (bf16[8,128,256]{2,1,0:T(8,128)(2,1)}, bf16[8,128,256]{2,1,0:T(8,128)(2,1)S(1)}, u32[]{:S(2)}, u32[]{:S(2)}) collective-permute-start(bf16[8,128,256]{2,1,0:T(8,128)(2,1)} %get-tuple-element.25), channel_id=1, source_target_pairs={{0,1},{1,0},{2,3},{3,2},{4,5},{5,4},{6,7},{7,6},{8,9},{9,8},{10,11... | collective-permute-start | bytes 1572872 | tf_op jit(solution)/shard_map/ppermute | solution.py:615
  16.2 1.1 fusion.77
  17.3 0.7 collective-permute-done.1.other
  18.1 2.8 %collective-permute-start.2 = (bf16[2,128,256]{2,1,0:T(8,128)(2,1)S(1)}, bf16[2,128,256]{2,1,0:T(8,128)(2,1)S(1)}, u32[]{:S(2)}, u32[]{:S(2)}) collective-permute-start(bf16[2,128,256]{2,1,0:T(8,128)(2,1)S(1)} %pad_maximum_fusion.5), channel_id=1, source_target_pairs={{0,2},{1,3},{2,0},{3,1},{4,6},{5,7},{6,4},{7,5},{8,10},{9,11},{10,... | collective-permute-start | bytes 393224 | tf_op jit(solution)/shard_map/ppermute | solution.py:615
  20.9 1.6 %collective-permute-start.5 = (bf16[2,128,256]{2,1,0:T(8,128)(2,1)S(1)}, bf16[2,128,256]{2,1,0:T(8,128)(2,1)S(1)}, u32[]{:S(2)}, u32[]{:S(2)}) collective-permute-start(bf16[2,128,256]{2,1,0:T(8,128)(2,1)S(1)} %pad_maximum_fusion.7), channel_id=1, source_target_pairs={{0,4},{1,5},{2,6},{3,7},{4,0},{5,1},{6,2},{7,3},{8,12},{9,13},{10,... | collective-permute-start | bytes 393224 | tf_op jit(solution)/shard_map/ppermute | solution.py:615
  22.5 0.9 collective-permute-start.6
  23.5 3.1 %collective-permute-start.7 = (bf16[2,128,256]{2,1,0:T(8,128)(2,1)S(1)}, bf16[2,128,256]{2,1,0:T(8,128)(2,1)S(1)}, u32[]{:S(2)}, u32[]{:S(2)}) collective-permute-start(bf16[2,128,256]{2,1,0:T(8,128)(2,1)S(1)} %pad_maximum_fusion.9), channel_id=1, source_target_pairs={{0,8},{1,9},{2,10},{3,11},{4,12},{5,13},{6,14},{7,15},{8,0},{9,1},... | collective-permute-start | bytes 393224 | tf_op jit(solution)/shard_map/ppermute | solution.py:615
  26.6 6.3 %mix.3 = (bf16[8,128,256]{2,1,0:T(8,128)(2,1)}, bf16[8,128,256]{2,1,0:T(8,128)(2,1)}, f32[128,2048]{1,0:T(8,128)}, bf16[128,2048]{1,0:T(8,128)(2,1)}) custom-call(s32[2]{0:T(128)} %pad_add_fusion.where, bf16[128,12288]{1,0:T(8,128)(2,1)} %value_in.3, bf16[128,12288]{1,0:T(8,128)(2,1)} %value_in.3, bf16[128,12288]{1,0:T(8,128)(2,1)} %value_in.3, ...), custom_call_target="tpu_custom_call" | custom-call | flops 3000000 | bytes 5000000 | tf_op jit(solution)/shard_map/mix/pallas_call | solution.py:293
  33.0 1.9 %collective-permute-start.8 = (bf16[2,128,256]{2,1,0:T(8,128)(2,1)S(1)}, bf16[2,128,256]{2,1,0:T(8,128)(2,1)S(1)}, u32[]{:S(2)}, u32[]{:S(2)}) collective-permute-start(bf16[2,128,256]{2,1,0:T(8,128)(2,1)S(1)} %pad_maximum_fusion.10), channel_id=1, source_target_pairs={{0,10},{1,11},{2,8},{3,9},{4,14},{5,15},{6,12},{7,13},{8,2},{9,3},... | collective-permute-start | bytes 393224 | tf_op jit(solution)/shard_map/ppermute | solution.py:615
  35.0 1.1 fusion.75
  36.2 1.2 reduce-precision_convert_fusion.1
  37.5 1.0 reduce-precision_convert_fusion
  38.5 0.5 add_multiply_fusion.5
  39.0 0.8 negate_exponential_fusion
  39.9 0.6 slice_bitcast_fusion.22
  40.6 1.5 collective-permute-start.4
  42.1 0.6 reduce-precision_convert_fusion.2
  42.7 0.7 pad_maximum_fusion.3.rest_9_
  43.4 0.7 pad_maximum_fusion.4.rest_10_
  44.1 0.9 pad_maximum_fusion.rest_11_
  45.0 0.8 pad_maximum_fusion.1.rest_12_
  45.8 0.8 slice_bitcast_fusion.4
  46.7 0.8 pad_maximum_fusion.2.rest_13_
  47.6 2.1 %collective-permute-start.9 = (bf16[2,128,256]{2,1,0:T(8,128)(2,1)S(1)}, bf16[2,128,256]{2,1,0:T(8,128)(2,1)S(1)}, u32[]{:S(2)}, u32[]{:S(2)}) collective-permute-start(bf16[2,128,256]{2,1,0:T(8,128)(2,1)S(1)} %pad_maximum_fusion.11), channel_id=1, source_target_pairs={{0,12},{1,13},{2,14},{3,15},{4,8},{5,9},{6,10},{7,11},{8,4},{9,5},... | collective-permute-start | bytes 393224 | tf_op jit(solution)/shard_map/ppermute | solution.py:615
  49.7 1.7 %collective-permute-start.10 = (bf16[2,128,256]{2,1,0:T(8,128)(2,1)S(1)}, bf16[2,128,256]{2,1,0:T(8,128)(2,1)S(1)}, u32[]{:S(2)}, u32[]{:S(2)}) collective-permute-start(bf16[2,128,256]{2,1,0:T(8,128)(2,1)S(1)} %pad_maximum_fusion.12), channel_id=1, source_target_pairs={{0,14},{1,15},{2,12},{3,13},{4,10},{5,11},{6,8},{7,9},{8,6},{9,7},... | collective-permute-start | bytes 393224 | tf_op jit(solution)/shard_map/ppermute | solution.py:615
  51.4 0.6 constant_dynamic-slice_fusion
  52.1 5.5 %near.2.rest_7_ = f32[128,2048]{1,0:T(8,128)} custom-call(bf16[128,2048]{1,0:T(8,128)(2,1)} %get-tuple-element.29.mixed, f32[16,16,128]{2,1,0:T(8,128)} %get-tuple-element.147.decay, f32[16,16,128]{2,1,0:T(8,128)} %get-tuple-element.106.gain, f32[16,128]{1,0:T(8,128)} %get-tuple-element.118.skip), custom_call_target="tpu_custom_call" | custom-call | flops 4000000 | bytes 8000000 | tf_op jit(solution)/shard_map/near/pallas_call | solution.py:360
  57.7 2.8 %collective-permute-start.14 = (bf16[2,128,256]{2,1,0:T(8,128)(2,1)S(1)}, bf16[2,128,256]{2,1,0:T(8,128)(2,1)S(1)}, u32[]{:S(2)}, u32[]{:S(2)}) collective-permute-start(bf16[2,128,256]{2,1,0:T(8,128)(2,1)S(1)} %pad_maximum_fusion.14), channel_id=1, source_target_pairs={{0,6},{1,7},{2,4},{3,5},{4,2},{5,3},{6,0},{7,1},{8,14},{9,15},{10,... | collective-permute-start | bytes 393224 | tf_op jit(solution)/shard_map/ppermute | solution.py:615
  60.5 0.8 collective-permute-start.15
  61.3 2.2 %collective-permute-start.16 = (bf16[2,128,256]{2,1,0:T(8,128)(2,1)S(1)}, bf16[2,128,256]{2,1,0:T(8,128)(2,1)S(1)}, u32[]{:S(2)}, u32[]{:S(2)}) collective-permute-start(bf16[2,128,256]{2,1,0:T(8,128)(2,1)S(1)} %pad_maximum_fusion.16), channel_id=1, source_target_pairs={{0,10},{1,11},{2,8},{3,9},{4,14},{5,15},{6,12},{7,13},{8,2},{9,3},... | collective-permute-start | bytes 393224 | tf_op jit(solution)/shard_map/ppermute | solution.py:615
  63.6 0.6 copy-done.34
  64.2 14.5 %lags.2 = bf16[2,8,160,128]{3,2,1,0:T(8,128)(2,1)} custom-call(s32[2]{0:T(128)} %pad_add_fusion.where, bf16[8,128,256]{2,1,0:T(8,128)(2,1)} %get-tuple-element.24.own, bf16[8,128,256]{2,1,0:T(8,128)(2,1)} %copy-done.4, bf16[2,128,256]{2,1,0:T(8,128)(2,1)} %copy-done.22, bf16[2,128,256]{2,1,0:T(8,128)(2,1)} %copy-done.23, bf16[2,128,256]{2,1,0:T(8,128)(2,1)} %copy-done.24, ...), custom_call_target="tpu_custom_call" | custom-call | flops 5000000000 | bytes 12000000 | tf_op jit(solution)/shard_map/lags/pallas_call | solution.py:495
  78.6 1.8 %slice_bitcast_fusion = (bf16[8,160,128]{2,1,0:T(8,128)(2,1)}, bf16[8,160,128]{2,1,0:T(8,128)(2,1)S(1)}) fusion(bf16[2,8,160,128]{3,2,1,0:T(8,128)(2,1)} %lags.2), kind=kLoop, calls=%fused_computation.79 | loop fusion | bytes 1310720 | tf_op jit(solution)/shard_map/squeeze | solution.py:687
  80.5 0.9 slice_bitcast_fusion.8
  81.4 0.7 collective-permute-done.11.other
  82.1 1.5 collective-permute-start.12
  83.7 2.2 %collective-permute-start.17 = (bf16[2,128,256]{2,1,0:T(8,128)(2,1)S(1)}, bf16[2,128,256]{2,1,0:T(8,128)(2,1)S(1)}, u32[]{:S(2)}, u32[]{:S(2)}) collective-permute-start(bf16[2,128,256]{2,1,0:T(8,128)(2,1)S(1)} %pad_maximum_fusion.17), channel_id=1, source_target_pairs={{0,12},{1,13},{2,14},{3,15},{4,8},{5,9},{6,10},{7,11},{8,4},{9,5},... | collective-permute-start | bytes 393224 | tf_op jit(solution)/shard_map/ppermute | solution.py:615
  85.9 0.8 collective-permute-done.12.rest_0_
  86.7 3.0 %collective-permute-start.18 = (bf16[2,128,256]{2,1,0:T(8,128)(2,1)S(1)}, bf16[2,128,256]{2,1,0:T(8,128)(2,1)S(1)}, u32[]{:S(2)}, u32[]{:S(2)}) collective-permute-start(bf16[2,128,256]{2,1,0:T(8,128)(2,1)S(1)} %pad_maximum_fusion.18), channel_id=1, source_target_pairs={{0,14},{1,15},{2,12},{3,13},{4,10},{5,11},{6,8},{7,9},{8,6},{9,7},... | collective-permute-start | bytes 393224 | tf_op jit(solution)/shard_map/ppermute | solution.py:615
  89.8 2.1 %collective-permute-start.28 = (bf16[2,160,128]{2,1,0:T(8,128)(2,1)S(1)}, bf16[2,160,128]{2,1,0:T(8,128)(2,1)S(1)}, u32[]{:S(2)}, u32[]{:S(2)}) collective-permute-start(bf16[2,160,128]{2,1,0:T(8,128)(2,1)S(1)} %pad_maximum_fusion.28), channel_id=1, source_target_pairs={{0,6},{1,7},{2,4},{3,5},{4,2},{5,3},{6,0},{7,1},{8,14},{9,15},{10,... | collective-permute-start | bytes 245768 | tf_op jit(solution)/shard_map/ppermute | solution.py:615
  92.2 3.5 %collective-permute-start.30 = (bf16[2,160,128]{2,1,0:T(8,128)(2,1)S(1)}, bf16[2,160,128]{2,1,0:T(8,128)(2,1)S(1)}, u32[]{:S(2)}, u32[]{:S(2)}) collective-permute-start(bf16[2,160,128]{2,1,0:T(8,128)(2,1)S(1)} %pad_maximum_fusion.30), channel_id=1, source_target_pairs={{0,10},{1,11},{2,8},{3,9},{4,14},{5,15},{6,12},{7,13},{8,2},{9,3},... | collective-permute-start | bytes 245768 | tf_op jit(solution)/shard_map/ppermute | solution.py:615
  95.8 0.6 copy-done.35
  96.4 14.3 %lags.3 = bf16[2,8,160,128]{3,2,1,0:T(8,128)(2,1)} custom-call(s32[2]{0:T(128)} %pad_add_fusion.where, bf16[8,128,256]{2,1,0:T(8,128)(2,1)} %get-tuple-element.33.own, bf16[8,128,256]{2,1,0:T(8,128)(2,1)} %copy-done.3, bf16[2,128,256]{2,1,0:T(8,128)(2,1)} %copy-done.26, bf16[2,128,256]{2,1,0:T(8,128)(2,1)} %copy-done.28, bf16[2,128,256]{2,1,0:T(8,128)(2,1)} %copy-done.29, ...), custom_call_target="tpu_custom_call" | custom-call | flops 5000000000 | bytes 12000000 | tf_op jit(solution)/shard_map/lags/pallas_call | solution.py:495
  110.7 1.9 %slice_bitcast_fusion.1 = (bf16[8,160,128]{2,1,0:T(8,128)(2,1)S(1)}, bf16[8,160,128]{2,1,0:T(8,128)(2,1)}) fusion(bf16[2,8,160,128]{3,2,1,0:T(8,128)(2,1)} %lags.3), kind=kLoop, calls=%fused_computation.80 | loop fusion | bytes 1310720 | tf_op jit(solution)/shard_map/squeeze | solution.py:686
  112.6 0.9 slice_bitcast_fusion.14
  113.5 0.7 collective-permute-done.19.other
  114.2 2.1 %collective-permute-start.31 = (bf16[2,160,128]{2,1,0:T(8,128)(2,1)S(1)}, bf16[2,160,128]{2,1,0:T(8,128)(2,1)S(1)}, u32[]{:S(2)}, u32[]{:S(2)}) collective-permute-start(bf16[2,160,128]{2,1,0:T(8,128)(2,1)S(1)} %pad_maximum_fusion.31), channel_id=1, source_target_pairs={{0,12},{1,13},{2,14},{3,15},{4,8},{5,9},{6,10},{7,11},{8,4},{9,5},... | collective-permute-start | bytes 245768 | tf_op jit(solution)/shard_map/ppermute | solution.py:615
  116.5 2.6 %collective-permute-start.32 = (bf16[2,160,128]{2,1,0:T(8,128)(2,1)S(1)}, bf16[2,160,128]{2,1,0:T(8,128)(2,1)S(1)}, u32[]{:S(2)}, u32[]{:S(2)}) collective-permute-start(bf16[2,160,128]{2,1,0:T(8,128)(2,1)S(1)} %pad_maximum_fusion.32), channel_id=1, source_target_pairs={{0,14},{1,15},{2,12},{3,13},{4,10},{5,11},{6,8},{7,9},{8,6},{9,7},... | collective-permute-start | bytes 245768 | tf_op jit(solution)/shard_map/ppermute | solution.py:615
  119.1 0.6 collective-permute-start.20
  119.7 2.4 %collective-permute-start.21 = (bf16[2,160,128]{2,1,0:T(8,128)(2,1)S(1)}, bf16[2,160,128]{2,1,0:T(8,128)(2,1)S(1)}, u32[]{:S(2)}, u32[]{:S(2)}) collective-permute-start(bf16[2,160,128]{2,1,0:T(8,128)(2,1)S(1)} %pad_maximum_fusion.21), channel_id=1, source_target_pairs={{0,4},{1,5},{2,6},{3,7},{4,0},{5,1},{6,2},{7,3},{8,12},{9,13},{10,... | collective-permute-start | bytes 245768 | tf_op jit(solution)/shard_map/ppermute | solution.py:615
  122.1 0.9 collective-permute-start.22
  123.0 2.9 %collective-permute-start.23 = (bf16[2,160,128]{2,1,0:T(8,128)(2,1)S(1)}, bf16[2,160,128]{2,1,0:T(8,128)(2,1)S(1)}, u32[]{:S(2)}, u32[]{:S(2)}) collective-permute-start(bf16[2,160,128]{2,1,0:T(8,128)(2,1)S(1)} %pad_maximum_fusion.23), channel_id=1, source_target_pairs={{0,8},{1,9},{2,10},{3,11},{4,12},{5,13},{6,14},{7,15},{8,0},{9,1},... | collective-permute-start | bytes 245768 | tf_op jit(solution)/shard_map/ppermute | solution.py:615
  125.9 2.9 %collective-permute-start.24 = (bf16[2,160,128]{2,1,0:T(8,128)(2,1)S(1)}, bf16[2,160,128]{2,1,0:T(8,128)(2,1)S(1)}, u32[]{:S(2)}, u32[]{:S(2)}) collective-permute-start(bf16[2,160,128]{2,1,0:T(8,128)(2,1)S(1)} %pad_maximum_fusion.24), channel_id=1, source_target_pairs={{0,10},{1,11},{2,8},{3,9},{4,14},{5,15},{6,12},{7,13},{8,2},{9,3},... | collective-permute-start | bytes 245768 | tf_op jit(solution)/shard_map/ppermute | solution.py:615
  128.8 1.8 %collective-permute-start.25 = (bf16[2,160,128]{2,1,0:T(8,128)(2,1)S(1)}, bf16[2,160,128]{2,1,0:T(8,128)(2,1)S(1)}, u32[]{:S(2)}, u32[]{:S(2)}) collective-permute-start(bf16[2,160,128]{2,1,0:T(8,128)(2,1)S(1)} %pad_maximum_fusion.25), channel_id=1, source_target_pairs={{0,12},{1,13},{2,14},{3,15},{4,8},{5,9},{6,10},{7,11},{8,4},{9,5},... | collective-permute-start | bytes 245768 | tf_op jit(solution)/shard_map/ppermute | solution.py:615
  130.6 3.6 %collective-permute-start.26 = (bf16[2,160,128]{2,1,0:T(8,128)(2,1)S(1)}, bf16[2,160,128]{2,1,0:T(8,128)(2,1)S(1)}, u32[]{:S(2)}, u32[]{:S(2)}) collective-permute-start(bf16[2,160,128]{2,1,0:T(8,128)(2,1)S(1)} %pad_maximum_fusion.26), channel_id=1, source_target_pairs={{0,14},{1,15},{2,12},{3,13},{4,10},{5,11},{6,8},{7,9},{8,6},{9,7},... | collective-permute-start | bytes 245768 | tf_op jit(solution)/shard_map/ppermute | solution.py:615
  134.2 5.5 %near.3.rest_7_ = f32[128,2048]{1,0:T(8,128)} custom-call(bf16[128,2048]{1,0:T(8,128)(2,1)} %get-tuple-element.37.mixed, f32[16,16,128]{2,1,0:T(8,128)} %get-tuple-element.148.decay, f32[16,16,128]{2,1,0:T(8,128)} %get-tuple-element.105.gain, f32[16,128]{1,0:T(8,128)} %get-tuple-element.117.skip), custom_call_target="tpu_custom_call" | custom-call | flops 4000000 | bytes 8000000 | tf_op jit(solution)/shard_map/near/pallas_call | solution.py:360
  139.8 5.2 %finish.2 = (bf16[128,4096]{1,0:T(8,128)(2,1)}, f32[128,4096]{1,0:T(8,128)}) custom-call(s32[2]{0:T(128)} %pad_add_fusion.where, bf16[8,160,128]{2,1,0:T(8,128)(2,1)} %get-tuple-element.49.own, bf16[8,160,128]{2,1,0:T(8,128)(2,1)} %copy-done.1, bf16[2,160,128]{2,1,0:T(8,128)(2,1)} %copy-done.7, bf16[2,160,128]{2,1,0:T(8,128)(2,1)} %copy-done.8, ...), custom_call_target="tpu_custom_call" | custom-call | flops 4000000 | bytes 5000000 | tf_op jit(solution)/shard_map/finish/pallas_call | solution.py:591
  145.1 0.5 copy-done.15
  145.8 5.0 %finish.3 = (bf16[128,4096]{1,0:T(8,128)(2,1)}, f32[128,4096]{1,0:T(8,128)}) custom-call(s32[2]{0:T(128)} %pad_add_fusion.where, bf16[8,160,128]{2,1,0:T(8,128)(2,1)} %get-tuple-element.59.own, bf16[8,160,128]{2,1,0:T(8,128)(2,1)} %copy-done.2, bf16[2,160,128]{2,1,0:T(8,128)(2,1)} %copy-done.13, ...), custom_call_target="tpu_custom_call", output_to_operand_aliasing={{0}: (13, {}), {1}: (14, {})} | custom-call | flops 4000000 | bytes 5000000 | tf_op jit(solution)/shard_map/finish/pallas_call | solution.py:591
  (148 shorter events, 2.1 us)
Async XLA Ops:
  1.6 3.5 %collective-permute-start = (bf16[8,12288]{1,0:T(8,128)(2,1)S(1)}, bf16[8,12288]{1,0:T(8,128)(2,1)S(1)}, u32[]{:S(2)}, u32[]{:S(2)}) collective-permute-start(bf16[8,12288]{1,0:T(8,128)(2,1)S(1)} %slice.281), channel_id=1, source_target_pairs={{0,1},{1,2},{2,3},{3,4},{4,5},{5,6},{6,7},{7,8},{8,9},{9,10},{10,1... | collective-permute-start | bytes 589832 | tf_op jit(solution)/shard_map/ppermute | solution.py:644
  5.0 0.7 copy-start
  12.0 6.0 %collective-permute-start.1 = (bf16[8,128,256]{2,1,0:T(8,128)(2,1)}, bf16[8,128,256]{2,1,0:T(8,128)(2,1)S(1)}, u32[]{:S(2)}, u32[]{:S(2)}) collective-permute-start(bf16[8,128,256]{2,1,0:T(8,128)(2,1)} %get-tuple-element.25), channel_id=1, source_target_pairs={{0,1},{1,0},{2,3},{3,2},{4,5},{5,4},{6,7},{7,6},{8,9},{9,8},{10,11... | collective-permute-start | bytes 1572872 | tf_op jit(solution)/shard_map/ppermute | solution.py:615
  18.0 14.9 %copy-start.4 = (bf16[8,128,256]{2,1,0:T(8,128)(2,1)}, bf16[8,128,256]{2,1,0:T(8,128)(2,1)S(1)}, u32[]{:S(2)}) copy-start(bf16[8,128,256]{2,1,0:T(8,128)(2,1)S(1)} %collective-permute-done.1.other) | copy-start | bytes 1572868
  18.1 8.5 %collective-permute-start.2 = (bf16[2,128,256]{2,1,0:T(8,128)(2,1)S(1)}, bf16[2,128,256]{2,1,0:T(8,128)(2,1)S(1)}, u32[]{:S(2)}, u32[]{:S(2)}) collective-permute-start(bf16[2,128,256]{2,1,0:T(8,128)(2,1)S(1)} %pad_maximum_fusion.5), channel_id=1, source_target_pairs={{0,2},{1,3},{2,0},{3,1},{4,6},{5,7},{6,4},{7,5},{8,10},{9,11},{10,... | collective-permute-start | bytes 393224 | tf_op jit(solution)/shard_map/ppermute | solution.py:615
  20.9 26.7 %collective-permute-start.5 = (bf16[2,128,256]{2,1,0:T(8,128)(2,1)S(1)}, bf16[2,128,256]{2,1,0:T(8,128)(2,1)S(1)}, u32[]{:S(2)}, u32[]{:S(2)}) collective-permute-start(bf16[2,128,256]{2,1,0:T(8,128)(2,1)S(1)} %pad_maximum_fusion.7), channel_id=1, source_target_pairs={{0,4},{1,5},{2,6},{3,7},{4,0},{5,1},{6,2},{7,3},{8,12},{9,13},{10,... | collective-permute-start | bytes 393224 | tf_op jit(solution)/shard_map/ppermute | solution.py:615
  22.5 35.0 %collective-permute-start.6 = (bf16[2,128,256]{2,1,0:T(8,128)(2,1)S(1)}, bf16[2,128,256]{2,1,0:T(8,128)(2,1)S(1)}, u32[]{:S(2)}, u32[]{:S(2)}) collective-permute-start(bf16[2,128,256]{2,1,0:T(8,128)(2,1)S(1)} %pad_maximum_fusion.8), channel_id=1, source_target_pairs={{0,6},{1,7},{2,4},{3,5},{4,2},{5,3},{6,0},{7,1},{8,14},{9,15},{10,... | collective-permute-start | bytes 393224 | tf_op jit(solution)/shard_map/ppermute | solution.py:615
  23.5 34.2 %collective-permute-start.7 = (bf16[2,128,256]{2,1,0:T(8,128)(2,1)S(1)}, bf16[2,128,256]{2,1,0:T(8,128)(2,1)S(1)}, u32[]{:S(2)}, u32[]{:S(2)}) collective-permute-start(bf16[2,128,256]{2,1,0:T(8,128)(2,1)S(1)} %pad_maximum_fusion.9), channel_id=1, source_target_pairs={{0,8},{1,9},{2,10},{3,11},{4,12},{5,13},{6,14},{7,15},{8,0},{9,1},... | collective-permute-start | bytes 393224 | tf_op jit(solution)/shard_map/ppermute | solution.py:615
  26.6 6.3 %copy-start.22 = (bf16[2,128,256]{2,1,0:T(8,128)(2,1)}, bf16[2,128,256]{2,1,0:T(8,128)(2,1)S(1)}, u32[]{:S(2)}) copy-start(bf16[2,128,256]{2,1,0:T(8,128)(2,1)S(1)} %collective-permute-done.2.rest_0_) | copy-start | bytes 393220
  32.9 6.1 %copy-start.5 = (f32[16,4096]{1,0:T(8,128)S(1)}, f32[16,4096]{1,0:T(8,128)}, u32[]{:S(2)}) copy-start(f32[16,4096]{1,0:T(8,128)} %param.9) | copy-start | bytes 786436
  32.9 6.1 %copy-start.6 = (f32[16,4096]{1,0:T(8,128)S(1)}, f32[16,4096]{1,0:T(8,128)}, u32[]{:S(2)}) copy-start(f32[16,4096]{1,0:T(8,128)} %param.8) | copy-start | bytes 786436
  32.9 3.1 %collective-permute-start.3 = (bf16[8,128,256]{2,1,0:T(8,128)(2,1)}, bf16[8,128,256]{2,1,0:T(8,128)(2,1)S(1)}, u32[]{:S(2)}, u32[]{:S(2)}) collective-permute-start(bf16[8,128,256]{2,1,0:T(8,128)(2,1)} %get-tuple-element.27), channel_id=1, source_target_pairs={{0,1},{1,0},{2,3},{3,2},{4,5},{5,4},{6,7},{7,6},{8,9},{9,8},{10,11... | collective-permute-start | bytes 1572872 | tf_op jit(solution)/shard_map/ppermute | solution.py:615
  33.0 27.5 %collective-permute-start.8 = (bf16[2,128,256]{2,1,0:T(8,128)(2,1)S(1)}, bf16[2,128,256]{2,1,0:T(8,128)(2,1)S(1)}, u32[]{:S(2)}, u32[]{:S(2)}) collective-permute-start(bf16[2,128,256]{2,1,0:T(8,128)(2,1)S(1)} %pad_maximum_fusion.10), channel_id=1, source_target_pairs={{0,10},{1,11},{2,8},{3,9},{4,14},{5,15},{6,12},{7,13},{8,2},{9,3},... | collective-permute-start | bytes 393224 | tf_op jit(solution)/shard_map/ppermute | solution.py:615
  36.0 3.9 %copy-start.21 = (f32[4096]{0:T(1024)S(1)}, f32[4096]{0:T(1024)}, u32[]{:S(2)}) copy-start(f32[4096]{0:T(1024)} %param.10) | copy-start | bytes 49156
  36.0 4.5 %copy-start.3 = (bf16[8,128,256]{2,1,0:T(8,128)(2,1)}, bf16[8,128,256]{2,1,0:T(8,128)(2,1)S(1)}, u32[]{:S(2)}) copy-start(bf16[8,128,256]{2,1,0:T(8,128)(2,1)S(1)} %collective-permute-done.3.other) | copy-start | bytes 1572868
  40.6 9.1 %collective-permute-start.4 = (bf16[2,128,256]{2,1,0:T(8,128)(2,1)S(1)}, bf16[2,128,256]{2,1,0:T(8,128)(2,1)S(1)}, u32[]{:S(2)}, u32[]{:S(2)}) collective-permute-start(bf16[2,128,256]{2,1,0:T(8,128)(2,1)S(1)} %pad_maximum_fusion.6), channel_id=1, source_target_pairs={{0,2},{1,3},{2,0},{3,1},{4,6},{5,7},{6,4},{7,5},{8,10},{9,11},{10,... | collective-permute-start | bytes 393224 | tf_op jit(solution)/shard_map/ppermute | solution.py:615
  47.6 16.0 %copy-start.23 = (bf16[2,128,256]{2,1,0:T(8,128)(2,1)}, bf16[2,128,256]{2,1,0:T(8,128)(2,1)S(1)}, u32[]{:S(2)}) copy-start(bf16[2,128,256]{2,1,0:T(8,128)(2,1)S(1)} %collective-permute-done.5.rest_1_) | copy-start | bytes 393220
  47.6 13.8 %collective-permute-start.9 = (bf16[2,128,256]{2,1,0:T(8,128)(2,1)S(1)}, bf16[2,128,256]{2,1,0:T(8,128)(2,1)S(1)}, u32[]{:S(2)}, u32[]{:S(2)}) collective-permute-start(bf16[2,128,256]{2,1,0:T(8,128)(2,1)S(1)} %pad_maximum_fusion.11), channel_id=1, source_target_pairs={{0,12},{1,13},{2,14},{3,15},{4,8},{5,9},{6,10},{7,11},{8,4},{9,5},... | collective-permute-start | bytes 393224 | tf_op jit(solution)/shard_map/ppermute | solution.py:615
  49.7 28.9 %copy-start.26 = (bf16[2,128,256]{2,1,0:T(8,128)(2,1)}, bf16[2,128,256]{2,1,0:T(8,128)(2,1)S(1)}, u32[]{:S(2)}) copy-start(bf16[2,128,256]{2,1,0:T(8,128)(2,1)S(1)} %collective-permute-done.4.rest_0_) | copy-start | bytes 393220
  49.7 13.8 %collective-permute-start.10 = (bf16[2,128,256]{2,1,0:T(8,128)(2,1)S(1)}, bf16[2,128,256]{2,1,0:T(8,128)(2,1)S(1)}, u32[]{:S(2)}, u32[]{:S(2)}) collective-permute-start(bf16[2,128,256]{2,1,0:T(8,128)(2,1)S(1)} %pad_maximum_fusion.12), channel_id=1, source_target_pairs={{0,14},{1,15},{2,12},{3,13},{4,10},{5,11},{6,8},{7,9},{8,6},{9,7},... | collective-permute-start | bytes 393224 | tf_op jit(solution)/shard_map/ppermute | solution.py:615
  57.6 6.0 %copy-start.24 = (bf16[2,128,256]{2,1,0:T(8,128)(2,1)}, bf16[2,128,256]{2,1,0:T(8,128)(2,1)S(1)}, u32[]{:S(2)}) copy-start(bf16[2,128,256]{2,1,0:T(8,128)(2,1)S(1)} %collective-permute-done.6.rest_2_) | copy-start | bytes 393220
  57.6 26.1 %collective-permute-start.13 = (bf16[2,128,256]{2,1,0:T(8,128)(2,1)S(1)}, bf16[2,128,256]{2,1,0:T(8,128)(2,1)S(1)}, u32[]{:S(2)}, u32[]{:S(2)}) collective-permute-start(bf16[2,128,256]{2,1,0:T(8,128)(2,1)S(1)} %pad_maximum_fusion.13), channel_id=1, source_target_pairs={{0,4},{1,5},{2,6},{3,7},{4,0},{5,1},{6,2},{7,3},{8,12},{9,13},{10,... | collective-permute-start | bytes 393224 | tf_op jit(solution)/shard_map/ppermute | solution.py:615
  57.7 5.9 %copy-start.25 = (bf16[2,128,256]{2,1,0:T(8,128)(2,1)}, bf16[2,128,256]{2,1,0:T(8,128)(2,1)S(1)}, u32[]{:S(2)}) copy-start(bf16[2,128,256]{2,1,0:T(8,128)(2,1)S(1)} %collective-permute-done.7.rest_3_) | copy-start | bytes 393220
  57.7 32.0 %collective-permute-start.14 = (bf16[2,128,256]{2,1,0:T(8,128)(2,1)S(1)}, bf16[2,128,256]{2,1,0:T(8,128)(2,1)S(1)}, u32[]{:S(2)}, u32[]{:S(2)}) collective-permute-start(bf16[2,128,256]{2,1,0:T(8,128)(2,1)S(1)} %pad_maximum_fusion.14), channel_id=1, source_target_pairs={{0,6},{1,7},{2,4},{3,5},{4,2},{5,3},{6,0},{7,1},{8,14},{9,15},{10,... | collective-permute-start | bytes 393224 | tf_op jit(solution)/shard_map/ppermute | solution.py:615
  60.5 3.0 %copy-start.27 = (bf16[2,128,256]{2,1,0:T(8,128)(2,1)}, bf16[2,128,256]{2,1,0:T(8,128)(2,1)S(1)}, u32[]{:S(2)}) copy-start(bf16[2,128,256]{2,1,0:T(8,128)(2,1)S(1)} %collective-permute-done.8.rest_4_) | copy-start | bytes 393220
  60.5 29.3 %collective-permute-start.15 = (bf16[2,128,256]{2,1,0:T(8,128)(2,1)S(1)}, bf16[2,128,256]{2,1,0:T(8,128)(2,1)S(1)}, u32[]{:S(2)}, u32[]{:S(2)}) collective-permute-start(bf16[2,128,256]{2,1,0:T(8,128)(2,1)S(1)} %pad_maximum_fusion.15), channel_id=1, source_target_pairs={{0,8},{1,9},{2,10},{3,11},{4,12},{5,13},{6,14},{7,15},{8,0},{9,1},... | collective-permute-start | bytes 393224 | tf_op jit(solution)/shard_map/ppermute | solution.py:615
  61.3 2.2 %copy-start.32 = (bf16[2,128,256]{2,1,0:T(8,128)(2,1)}, bf16[2,128,256]{2,1,0:T(8,128)(2,1)S(1)}, u32[]{:S(2)}) copy-start(bf16[2,128,256]{2,1,0:T(8,128)(2,1)S(1)} %collective-permute-done.9.rest_5_) | copy-start | bytes 393220
  61.3 30.6 %collective-permute-start.16 = (bf16[2,128,256]{2,1,0:T(8,128)(2,1)S(1)}, bf16[2,128,256]{2,1,0:T(8,128)(2,1)S(1)}, u32[]{:S(2)}, u32[]{:S(2)}) collective-permute-start(bf16[2,128,256]{2,1,0:T(8,128)(2,1)S(1)} %pad_maximum_fusion.16), channel_id=1, source_target_pairs={{0,10},{1,11},{2,8},{3,9},{4,14},{5,15},{6,12},{7,13},{8,2},{9,3},... | collective-permute-start | bytes 393224 | tf_op jit(solution)/shard_map/ppermute | solution.py:615
  80.5 1.6 %collective-permute-start.11 = (bf16[8,160,128]{2,1,0:T(8,128)(2,1)S(1)}, bf16[8,160,128]{2,1,0:T(8,128)(2,1)S(1)}, u32[]{:S(2)}, u32[]{:S(2)}) collective-permute-start(bf16[8,160,128]{2,1,0:T(8,128)(2,1)S(1)} %get-tuple-element.50), channel_id=1, source_target_pairs={{0,1},{1,0},{2,3},{3,2},{4,5},{5,4},{6,7},{7,6},{8,9},{9,8},{10,11... | collective-permute-start | bytes 983048 | tf_op jit(solution)/shard_map/ppermute | solution.py:615
  82.1 28.6 %copy-start.1 = (bf16[8,160,128]{2,1,0:T(8,128)(2,1)}, bf16[8,160,128]{2,1,0:T(8,128)(2,1)S(1)}, u32[]{:S(2)}) copy-start(bf16[8,160,128]{2,1,0:T(8,128)(2,1)S(1)} %collective-permute-done.11.other) | copy-start | bytes 983044
  82.1 4.6 %collective-permute-start.12 = (bf16[2,160,128]{2,1,0:T(8,128)(2,1)S(1)}, bf16[2,160,128]{2,1,0:T(8,128)(2,1)S(1)}, u32[]{:S(2)}, u32[]{:S(2)}) collective-permute-start(bf16[2,160,128]{2,1,0:T(8,128)(2,1)S(1)} %pad_maximum_fusion.19), channel_id=1, source_target_pairs={{0,2},{1,3},{2,0},{3,1},{4,6},{5,7},{6,4},{7,5},{8,10},{9,11},{10,... | collective-permute-start | bytes 245768 | tf_op jit(solution)/shard_map/ppermute | solution.py:615
  83.7 12.1 %copy-start.28 = (bf16[2,128,256]{2,1,0:T(8,128)(2,1)}, bf16[2,128,256]{2,1,0:T(8,128)(2,1)S(1)}, u32[]{:S(2)}) copy-start(bf16[2,128,256]{2,1,0:T(8,128)(2,1)S(1)} %collective-permute-done.13.rest_1_) | copy-start | bytes 393220
  83.7 8.5 %collective-permute-start.17 = (bf16[2,128,256]{2,1,0:T(8,128)(2,1)S(1)}, bf16[2,128,256]{2,1,0:T(8,128)(2,1)S(1)}, u32[]{:S(2)}, u32[]{:S(2)}) collective-permute-start(bf16[2,128,256]{2,1,0:T(8,128)(2,1)S(1)} %pad_maximum_fusion.17), channel_id=1, source_target_pairs={{0,12},{1,13},{2,14},{3,15},{4,8},{5,9},{6,10},{7,11},{8,4},{9,5},... | collective-permute-start | bytes 393224 | tf_op jit(solution)/shard_map/ppermute | solution.py:615
  86.7 24.0 %copy-start.7 = (bf16[2,160,128]{2,1,0:T(8,128)(2,1)}, bf16[2,160,128]{2,1,0:T(8,128)(2,1)S(1)}, u32[]{:S(2)}) copy-start(bf16[2,160,128]{2,1,0:T(8,128)(2,1)S(1)} %collective-permute-done.12.rest_0_) | copy-start | bytes 245764
  86.7 9.1 %collective-permute-start.18 = (bf16[2,128,256]{2,1,0:T(8,128)(2,1)S(1)}, bf16[2,128,256]{2,1,0:T(8,128)(2,1)S(1)}, u32[]{:S(2)}, u32[]{:S(2)}) collective-permute-start(bf16[2,128,256]{2,1,0:T(8,128)(2,1)S(1)} %pad_maximum_fusion.18), channel_id=1, source_target_pairs={{0,14},{1,15},{2,12},{3,13},{4,10},{5,11},{6,8},{7,9},{8,6},{9,7},... | collective-permute-start | bytes 393224 | tf_op jit(solution)/shard_map/ppermute | solution.py:615
  89.7 6.1 %copy-start.29 = (bf16[2,128,256]{2,1,0:T(8,128)(2,1)}, bf16[2,128,256]{2,1,0:T(8,128)(2,1)S(1)}, u32[]{:S(2)}) copy-start(bf16[2,128,256]{2,1,0:T(8,128)(2,1)S(1)} %collective-permute-done.14.rest_2_) | copy-start | bytes 393220
  89.7 26.7 %collective-permute-start.27 = (bf16[2,160,128]{2,1,0:T(8,128)(2,1)S(1)}, bf16[2,160,128]{2,1,0:T(8,128)(2,1)S(1)}, u32[]{:S(2)}, u32[]{:S(2)}) collective-permute-start(bf16[2,160,128]{2,1,0:T(8,128)(2,1)S(1)} %pad_maximum_fusion.27), channel_id=1, source_target_pairs={{0,4},{1,5},{2,6},{3,7},{4,0},{5,1},{6,2},{7,3},{8,12},{9,13},{10,... | collective-permute-start | bytes 245768 | tf_op jit(solution)/shard_map/ppermute | solution.py:615
  89.8 6.0 %copy-start.30 = (bf16[2,128,256]{2,1,0:T(8,128)(2,1)}, bf16[2,128,256]{2,1,0:T(8,128)(2,1)S(1)}, u32[]{:S(2)}) copy-start(bf16[2,128,256]{2,1,0:T(8,128)(2,1)S(1)} %collective-permute-done.15.rest_3_) | copy-start | bytes 393220
  89.8 29.3 %collective-permute-start.28 = (bf16[2,160,128]{2,1,0:T(8,128)(2,1)S(1)}, bf16[2,160,128]{2,1,0:T(8,128)(2,1)S(1)}, u32[]{:S(2)}, u32[]{:S(2)}) collective-permute-start(bf16[2,160,128]{2,1,0:T(8,128)(2,1)S(1)} %pad_maximum_fusion.28), channel_id=1, source_target_pairs={{0,6},{1,7},{2,4},{3,5},{4,2},{5,3},{6,0},{7,1},{8,14},{9,15},{10,... | collective-permute-start | bytes 245768 | tf_op jit(solution)/shard_map/ppermute | solution.py:615
  91.9 3.9 %copy-start.31 = (bf16[2,128,256]{2,1,0:T(8,128)(2,1)}, bf16[2,128,256]{2,1,0:T(8,128)(2,1)S(1)}, u32[]{:S(2)}) copy-start(bf16[2,128,256]{2,1,0:T(8,128)(2,1)S(1)} %collective-permute-done.16.rest_4_) | copy-start | bytes 393220
  91.9 27.8 %collective-permute-start.29 = (bf16[2,160,128]{2,1,0:T(8,128)(2,1)S(1)}, bf16[2,160,128]{2,1,0:T(8,128)(2,1)S(1)}, u32[]{:S(2)}, u32[]{:S(2)}) collective-permute-start(bf16[2,160,128]{2,1,0:T(8,128)(2,1)S(1)} %pad_maximum_fusion.29), channel_id=1, source_target_pairs={{0,8},{1,9},{2,10},{3,11},{4,12},{5,13},{6,14},{7,15},{8,0},{9,1},... | collective-permute-start | bytes 245768 | tf_op jit(solution)/shard_map/ppermute | solution.py:615
  92.2 3.6 %copy-start.33 = (bf16[2,128,256]{2,1,0:T(8,128)(2,1)}, bf16[2,128,256]{2,1,0:T(8,128)(2,1)S(1)}, u32[]{:S(2)}) copy-start(bf16[2,128,256]{2,1,0:T(8,128)(2,1)S(1)} %collective-permute-done.17.rest_5_) | copy-start | bytes 393220
  92.2 29.9 %collective-permute-start.30 = (bf16[2,160,128]{2,1,0:T(8,128)(2,1)S(1)}, bf16[2,160,128]{2,1,0:T(8,128)(2,1)S(1)}, u32[]{:S(2)}, u32[]{:S(2)}) collective-permute-start(bf16[2,160,128]{2,1,0:T(8,128)(2,1)S(1)} %pad_maximum_fusion.30), channel_id=1, source_target_pairs={{0,10},{1,11},{2,8},{3,9},{4,14},{5,15},{6,12},{7,13},{8,2},{9,3},... | collective-permute-start | bytes 245768 | tf_op jit(solution)/shard_map/ppermute | solution.py:615
  112.5 1.6 %collective-permute-start.19 = (bf16[8,160,128]{2,1,0:T(8,128)(2,1)S(1)}, bf16[8,160,128]{2,1,0:T(8,128)(2,1)S(1)}, u32[]{:S(2)}, u32[]{:S(2)}) collective-permute-start(bf16[8,160,128]{2,1,0:T(8,128)(2,1)S(1)} %get-tuple-element.58), channel_id=1, source_target_pairs={{0,1},{1,0},{2,3},{3,2},{4,5},{5,4},{6,7},{7,6},{8,9},{9,8},{10,11... | collective-permute-start | bytes 983048 | tf_op jit(solution)/shard_map/ppermute | solution.py:615
  114.2 30.8 %copy-start.2 = (bf16[8,160,128]{2,1,0:T(8,128)(2,1)}, bf16[8,160,128]{2,1,0:T(8,128)(2,1)S(1)}, u32[]{:S(2)}) copy-start(bf16[8,160,128]{2,1,0:T(8,128)(2,1)S(1)} %collective-permute-done.19.other) | copy-start | bytes 983044
  114.2 8.8 %collective-permute-start.31 = (bf16[2,160,128]{2,1,0:T(8,128)(2,1)S(1)}, bf16[2,160,128]{2,1,0:T(8,128)(2,1)S(1)}, u32[]{:S(2)}, u32[]{:S(2)}) collective-permute-start(bf16[2,160,128]{2,1,0:T(8,128)(2,1)S(1)} %pad_maximum_fusion.31), channel_id=1, source_target_pairs={{0,12},{1,13},{2,14},{3,15},{4,8},{5,9},{6,10},{7,11},{8,4},{9,5},... | collective-permute-start | bytes 245768 | tf_op jit(solution)/shard_map/ppermute | solution.py:615
  116.5 23.3 %copy-start.8 = (bf16[2,160,128]{2,1,0:T(8,128)(2,1)}, bf16[2,160,128]{2,1,0:T(8,128)(2,1)S(1)}, u32[]{:S(2)}) copy-start(bf16[2,160,128]{2,1,0:T(8,128)(2,1)S(1)} %collective-permute-done.27.rest_1_) | copy-start | bytes 245764
  116.5 9.4 %collective-permute-start.32 = (bf16[2,160,128]{2,1,0:T(8,128)(2,1)S(1)}, bf16[2,160,128]{2,1,0:T(8,128)(2,1)S(1)}, u32[]{:S(2)}, u32[]{:S(2)}) collective-permute-start(bf16[2,160,128]{2,1,0:T(8,128)(2,1)S(1)} %pad_maximum_fusion.32), channel_id=1, source_target_pairs={{0,14},{1,15},{2,12},{3,13},{4,10},{5,11},{6,8},{7,9},{8,6},{9,7},... | collective-permute-start | bytes 245768 | tf_op jit(solution)/shard_map/ppermute | solution.py:615
  119.1 20.7 %copy-start.9 = (bf16[2,160,128]{2,1,0:T(8,128)(2,1)}, bf16[2,160,128]{2,1,0:T(8,128)(2,1)S(1)}, u32[]{:S(2)}) copy-start(bf16[2,160,128]{2,1,0:T(8,128)(2,1)S(1)} %collective-permute-done.28.rest_2_) | copy-start | bytes 245764
  119.1 9.7 %collective-permute-start.20 = (bf16[2,160,128]{2,1,0:T(8,128)(2,1)S(1)}, bf16[2,160,128]{2,1,0:T(8,128)(2,1)S(1)}, u32[]{:S(2)}, u32[]{:S(2)}) collective-permute-start(bf16[2,160,128]{2,1,0:T(8,128)(2,1)S(1)} %pad_maximum_fusion.20), channel_id=1, source_target_pairs={{0,2},{1,3},{2,0},{3,1},{4,6},{5,7},{6,4},{7,5},{8,10},{9,11},{10,... | collective-permute-start | bytes 245768 | tf_op jit(solution)/shard_map/ppermute | solution.py:615
  119.7 20.1 %copy-start.10 = (bf16[2,160,128]{2,1,0:T(8,128)(2,1)}, bf16[2,160,128]{2,1,0:T(8,128)(2,1)S(1)}, u32[]{:S(2)}) copy-start(bf16[2,160,128]{2,1,0:T(8,128)(2,1)S(1)} %collective-permute-done.29.rest_3_) | copy-start | bytes 245764
  119.7 10.9 %collective-permute-start.21 = (bf16[2,160,128]{2,1,0:T(8,128)(2,1)S(1)}, bf16[2,160,128]{2,1,0:T(8,128)(2,1)S(1)}, u32[]{:S(2)}, u32[]{:S(2)}) collective-permute-start(bf16[2,160,128]{2,1,0:T(8,128)(2,1)S(1)} %pad_maximum_fusion.21), channel_id=1, source_target_pairs={{0,4},{1,5},{2,6},{3,7},{4,0},{5,1},{6,2},{7,3},{8,12},{9,13},{10,... | collective-permute-start | bytes 245768 | tf_op jit(solution)/shard_map/ppermute | solution.py:615
  122.1 17.7 %copy-start.11 = (bf16[2,160,128]{2,1,0:T(8,128)(2,1)}, bf16[2,160,128]{2,1,0:T(8,128)(2,1)S(1)}, u32[]{:S(2)}) copy-start(bf16[2,160,128]{2,1,0:T(8,128)(2,1)S(1)} %collective-permute-done.30.rest_4_) | copy-start | bytes 245764
  122.1 23.0 %collective-permute-start.22 = (bf16[2,160,128]{2,1,0:T(8,128)(2,1)S(1)}, bf16[2,160,128]{2,1,0:T(8,128)(2,1)S(1)}, u32[]{:S(2)}, u32[]{:S(2)}) collective-permute-start(bf16[2,160,128]{2,1,0:T(8,128)(2,1)S(1)} %pad_maximum_fusion.22), channel_id=1, source_target_pairs={{0,6},{1,7},{2,4},{3,5},{4,2},{5,3},{6,0},{7,1},{8,14},{9,15},{10,... | collective-permute-start | bytes 245768 | tf_op jit(solution)/shard_map/ppermute | solution.py:615
  123.0 16.8 %copy-start.12 = (bf16[2,160,128]{2,1,0:T(8,128)(2,1)}, bf16[2,160,128]{2,1,0:T(8,128)(2,1)S(1)}, u32[]{:S(2)}) copy-start(bf16[2,160,128]{2,1,0:T(8,128)(2,1)S(1)} %collective-permute-done.31.rest_5_) | copy-start | bytes 245764
  123.0 22.1 %collective-permute-start.23 = (bf16[2,160,128]{2,1,0:T(8,128)(2,1)S(1)}, bf16[2,160,128]{2,1,0:T(8,128)(2,1)S(1)}, u32[]{:S(2)}, u32[]{:S(2)}) collective-permute-start(bf16[2,160,128]{2,1,0:T(8,128)(2,1)S(1)} %pad_maximum_fusion.23), channel_id=1, source_target_pairs={{0,8},{1,9},{2,10},{3,11},{4,12},{5,13},{6,14},{7,15},{8,0},{9,1},... | collective-permute-start | bytes 245768 | tf_op jit(solution)/shard_map/ppermute | solution.py:615
  125.9 13.9 %copy-start.16 = (bf16[2,160,128]{2,1,0:T(8,128)(2,1)}, bf16[2,160,128]{2,1,0:T(8,128)(2,1)S(1)}, u32[]{:S(2)}) copy-start(bf16[2,160,128]{2,1,0:T(8,128)(2,1)S(1)} %collective-permute-done.32.rest_6_) | copy-start | bytes 245764
  125.9 19.2 %collective-permute-start.24 = (bf16[2,160,128]{2,1,0:T(8,128)(2,1)S(1)}, bf16[2,160,128]{2,1,0:T(8,128)(2,1)S(1)}, u32[]{:S(2)}, u32[]{:S(2)}) collective-permute-start(bf16[2,160,128]{2,1,0:T(8,128)(2,1)S(1)} %pad_maximum_fusion.24), channel_id=1, source_target_pairs={{0,10},{1,11},{2,8},{3,9},{4,14},{5,15},{6,12},{7,13},{8,2},{9,3},... | collective-permute-start | bytes 245768 | tf_op jit(solution)/shard_map/ppermute | solution.py:615
  128.8 16.2 %copy-start.13 = (bf16[2,160,128]{2,1,0:T(8,128)(2,1)}, bf16[2,160,128]{2,1,0:T(8,128)(2,1)S(1)}, u32[]{:S(2)}) copy-start(bf16[2,160,128]{2,1,0:T(8,128)(2,1)S(1)} %collective-permute-done.20.rest_0_) | copy-start | bytes 245764
  128.8 16.3 %collective-permute-start.25 = (bf16[2,160,128]{2,1,0:T(8,128)(2,1)S(1)}, bf16[2,160,128]{2,1,0:T(8,128)(2,1)S(1)}, u32[]{:S(2)}, u32[]{:S(2)}) collective-permute-start(bf16[2,160,128]{2,1,0:T(8,128)(2,1)S(1)} %pad_maximum_fusion.25), channel_id=1, source_target_pairs={{0,12},{1,13},{2,14},{3,15},{4,8},{5,9},{6,10},{7,11},{8,4},{9,5},... | collective-permute-start | bytes 245768 | tf_op jit(solution)/shard_map/ppermute | solution.py:615
  130.6 14.5 %copy-start.14 = (bf16[2,160,128]{2,1,0:T(8,128)(2,1)}, bf16[2,160,128]{2,1,0:T(8,128)(2,1)S(1)}, u32[]{:S(2)}) copy-start(bf16[2,160,128]{2,1,0:T(8,128)(2,1)S(1)} %collective-permute-done.21.rest_1_) | copy-start | bytes 245764
  130.6 14.5 %collective-permute-start.26 = (bf16[2,160,128]{2,1,0:T(8,128)(2,1)S(1)}, bf16[2,160,128]{2,1,0:T(8,128)(2,1)S(1)}, u32[]{:S(2)}, u32[]{:S(2)}) collective-permute-start(bf16[2,160,128]{2,1,0:T(8,128)(2,1)S(1)} %pad_maximum_fusion.26), channel_id=1, source_target_pairs={{0,14},{1,15},{2,12},{3,13},{4,10},{5,11},{6,8},{7,9},{8,6},{9,7},... | collective-permute-start | bytes 245768 | tf_op jit(solution)/shard_map/ppermute | solution.py:615
  145.1 0.7 copy-start.18
  145.1 0.7 copy-start.20
  (5 other events, 3.2 us)

commit v3 on v2

--- a/solution.py
+++ b/solution.py
@@ -13,9 +13,9 @@
 HALO = 8
 FINE_PRODUCT = 256
 UNROLL = 8
-CHIP_GROUP = 4
-FINISH_GROUP = 4
-CHIP_ORDER = (4, 1, 5, 2, 6, 3, 7)
+STRIP = 32
+PLANE = 4
+PAIR = 2
 SINE = (1.0, -1.0 / 6, 1.0 / 120, -1.0 / 5040, 1.0 / 362880, -1.0 / 39916800, 1.0 / 6227020800)
 
 
@@ -179,17 +179,12 @@
     return (high, low)
 
 
-def split_outside(value):
-    high = lax.reduce_precision(value, 8, 7)
-    return (high.astype(jnp.bfloat16), (value - high).astype(jnp.bfloat16))
-
-
 def dot32(left, right):
     return jnp.dot(left, right, preferred_element_type=jnp.float32)
 
 
 def cosines(turns, whole):
-    folded = jnp.bitwise_and(turns + whole // 2, whole - 1) - whole // 2
+    folded = ((turns + whole // 2) & (whole - 1)) - whole // 2
     angle = (2.0 * math.pi / whole) * (whole // 4 - jnp.abs(folded)).astype(jnp.float32)
     square = angle * angle
     series = jnp.full_like(angle, SINE[-1])
@@ -198,91 +193,121 @@
     return angle * series
 
 
-def grid_of(height, width, zero):
-    shape = (height, width)
-    return (
-        lax.broadcasted_iota(jnp.int32, shape, 0) + zero,
-        lax.broadcasted_iota(jnp.int32, shape, 1) + zero,
-    )
-
-
-def spectral_tables(devices, rows, zero):
+def table_body(devices, rows, forward, backward, outer_forward, outer_backward, twist):
     fine = FINE_PRODUCT // devices
-    line, lane = grid_of(2 * rows, 2 * rows, zero)
-    quarter = (line // rows - lane // rows) * (rows // 4)
-    base = cosines((line % rows) * (lane % rows) + quarter, rows)
-    base_back = cosines((line % rows) * (lane % rows) - quarter, rows)
-    line, lane = grid_of(2 * FINE_PRODUCT, FINE_PRODUCT, zero)
-    coarse = line % FINE_PRODUCT // fine
-    outer = jnp.where(
-        line % fine == lane % fine,
-        cosines((2 * coarse + 1) * (lane // fine) + line // FINE_PRODUCT * devices, 4 * devices),
-        0.0,
-    )
-    line, lane = grid_of(FINE_PRODUCT, 2 * FINE_PRODUCT, zero)
-    coarse = lane % FINE_PRODUCT // fine
-    outer_back = jnp.where(
-        line % fine == lane % fine,
-        cosines((2 * coarse + 1) * (line // fine) + lane // FINE_PRODUCT * devices, 4 * devices)
-        * (1.0 / (devices * rows)),
-        0.0,
-    )
-    line, lane = grid_of(FINE_PRODUCT, LANES, zero)
-    odd = 2 * (line // fine) + 1
+    log_rows, log_fine = rows.bit_length() - 1, fine.bit_length() - 1
+    log_product = FINE_PRODUCT.bit_length() - 1
     length = devices * rows
-    first = odd * (line % fine)
-    twist = jnp.stack(
-        [
-            cosines(first, 4 * length),
-            cosines(first - length, 4 * length),
-            cosines(odd * fine, 4 * length),
-            cosines(odd * fine - length, 4 * length),
-        ]
-    )
-    packed = [
-        jnp.concatenate(split_outside(table), axis=0)
-        for table in (base, base_back, outer, outer_back)
+
+    def fill(out, height, width, value):
+        for start in range(0, height, STRIP):
+            line = lax.broadcasted_iota(jnp.int32, (STRIP, width), 0) + start
+            lane = lax.broadcasted_iota(jnp.int32, (STRIP, width), 1)
+            high, low = split_pair(value(line, lane))
+            out[start : start + STRIP, :] = high
+            out[height + start : height + start + STRIP, :] = low
+
+    def base(sign):
+        def value(line, lane):
+            quarter = ((line >> log_rows) - (lane >> log_rows)) * (sign * (rows // 4))
+            return cosines((line & (rows - 1)) * (lane & (rows - 1)) + quarter, rows)
+
+        return value
+
+    def outer(line, lane):
+        coarse = (line & (FINE_PRODUCT - 1)) >> log_fine
+        turns = (2 * coarse + 1) * (lane >> log_fine) + (line >> log_product) * devices
+        same = (line & (fine - 1)) == (lane & (fine - 1))
+        return jnp.where(same, cosines(turns, 4 * devices), 0.0)
+
+    def outer_back(line, lane):
+        coarse = (lane & (FINE_PRODUCT - 1)) >> log_fine
+        position = line >> log_fine
+        turns = (2 * coarse + 1) * position + (lane >> log_product) * devices
+        same = (line & (fine - 1)) == (lane & (fine - 1))
+        return jnp.where(same, cosines(turns, 4 * devices) * (1.0 / length), 0.0)
+
+    fill(forward, 2 * rows, 2 * rows, base(1))
+    fill(backward, 2 * rows, 2 * rows, base(-1))
+    fill(outer_forward, 2 * FINE_PRODUCT, FINE_PRODUCT, outer)
+    fill(outer_backward, FINE_PRODUCT, 2 * FINE_PRODUCT, outer_back)
+    for start in range(0, FINE_PRODUCT, STRIP):
+        line = lax.broadcasted_iota(jnp.int32, (STRIP, LANES), 0) + start
+        odd = 2 * (line >> log_fine) + 1
+        for index, turns in enumerate((odd * (line & (fine - 1)), odd * fine)):
+            twist[2 * index, start : start + STRIP, :] = cosines(turns, 4 * length)
+            twist[2 * index + 1, start : start + STRIP, :] = cosines(turns - length, 4 * length)
+
+
+def spectral_tables(devices, rows, earlier):
+    whole = lambda shape: pl.BlockSpec(shape, lambda g: (0,) * len(shape))
+    shapes = [
+        jax.ShapeDtypeStruct((4 * rows, 2 * rows), jnp.bfloat16),
+        jax.ShapeDtypeStruct((4 * rows, 2 * rows), jnp.bfloat16),
+        jax.ShapeDtypeStruct((4 * FINE_PRODUCT, FINE_PRODUCT), jnp.bfloat16),
+        jax.ShapeDtypeStruct((2 * FINE_PRODUCT, 2 * FINE_PRODUCT), jnp.bfloat16),
+        jax.ShapeDtypeStruct((4, FINE_PRODUCT, LANES), jnp.float32),
     ]
-    return (*packed, twist)
-
-
-def mix_body(where, query_in, key_in, value_in, before_q, before_k, before_v, weight_q, weight_k, weight_v, cot, kept, given, query_out, mixed_out, padded):
+    return pl.pallas_call(
+        lambda earlier, *outs: table_body(devices, rows, *outs),
+        grid=(1,),
+        in_specs=[pl.BlockSpec(memory_space=pl.ANY)],
+        out_specs=[whole(one.shape) for one in shapes],
+        out_shape=shapes,
+        cost_estimate=pl.CostEstimate(
+            flops=1000, transcendentals=0, bytes_accessed=1000
+        ),
+        name="tables",
+    )(earlier)
+
+
+def mix_body(
+    plain, where, query_in, key_in, value_in, before_q, before_k, before_v,
+    weight_q, weight_k, weight_v, cot, *outputs
+):
+    *sends, query_out, mixed_out, padded = outputs
     taps = weight_q.shape[0]
     rows = query_in.shape[0]
     tail = before_q.shape[0]
-    chip, core = where[0], where[1]
+    plane, rank = where[0], where[1]
     streams = ((query_in, before_q, weight_q), (key_in, before_k, weight_k), (value_in, before_v, weight_v))
     for index, (block, before, _) in enumerate(streams):
         padded[index, :tail, :] = before[...].astype(jnp.float32)
         padded[index, tail:, :] = block[...].astype(jnp.float32)
-    group = kept.shape[0]
-    for index in range(group):
-        slot = index ^ (chip % group)
-        for side, sent in enumerate((kept, given)):
-            piece = 2 * index + (core ^ side)
+
+    def work(piece, sent, slot):
+        if isinstance(piece, int):
+            lanes = slice(piece * LANES, (piece + 1) * LANES)
+        else:
             lanes = pl.ds(pl.multiple_of(piece * LANES, LANES), LANES)
-            filtered = []
-            for stream, (_, _, weight) in enumerate(streams):
-                total = None
-                for tap in range(taps):
-                    term = weight[tap : tap + 1, lanes] * padded[stream, tail - tap : tail - tap + rows, lanes]
-                    total = term if total is None else total + term
-                filtered.append(total)
-            mixed = (filtered[1] * filtered[2]).astype(jnp.bfloat16)
-            scaled = (filtered[0] * cot[:, lanes].astype(jnp.float32)).astype(jnp.bfloat16)
-            query_out[:, lanes] = filtered[0]
-            mixed_out[:, lanes] = mixed
-            sent[slot, :, :LANES] = mixed
-            sent[slot, :, LANES:] = scaled
-
-
-def mix_streams(where, proj, before, short_weight, grad_out, chunk, chunks, devices):
+        filtered = []
+        for stream, (_, _, weight) in enumerate(streams):
+            total = None
+            for tap in range(taps):
+                term = weight[tap : tap + 1, lanes] * padded[stream, tail - tap : tail - tap + rows, lanes]
+                total = term if total is None else total + term
+            filtered.append(total)
+        mixed = (filtered[1] * filtered[2]).astype(jnp.bfloat16)
+        scaled = (filtered[0] * cot[:, lanes].astype(jnp.float32)).astype(jnp.bfloat16)
+        query_out[:, lanes] = filtered[0]
+        mixed_out[:, lanes] = mixed
+        sent[slot, :, :LANES] = mixed
+        sent[slot, :, LANES:] = scaled
+
+    if plain:
+        for piece in range(sends[0].shape[0]):
+            work(piece, sends[0], piece)
+    else:
+        for index in range(PAIR):
+            for side in range(PLANE):
+                work(PLANE * index + (rank ^ side), sends[side], index ^ (plane % PAIR))
+
+
+def mix_streams(where, proj, before, short_weight, grad_out, chunk, chunks, devices, plain):
     rows, channels = grad_out.shape
     taps = short_weight.shape[0]
     tail = before.shape[0]
-    chips = devices // 2
-    group = CHIP_GROUP
-    step = 2 * group * LANES
+    step = PAIR * PLANE * LANES
     steps = channels // chunks // step
     base = chunk * steps
     stride = channels // step
@@ -290,8 +315,18 @@
     def stream_spec(height, stream):
         return pl.BlockSpec((height, step), lambda g, w, s=stream: (0, s * stride + base + g))
 
-    return pl.pallas_call(
-        mix_body,
+    if plain:
+        send_specs = [pl.BlockSpec((PAIR * PLANE, rows, 2 * LANES), lambda g, w: (g, 0, 0))]
+        send_shapes = [jax.ShapeDtypeStruct((devices, rows, 2 * LANES), jnp.bfloat16)]
+    else:
+        send_specs = [
+            pl.BlockSpec((PAIR, rows, 2 * LANES), lambda g, w: (g ^ (w[0] // PAIR), 0, 0))
+        ] * PLANE
+        send_shapes = [
+            jax.ShapeDtypeStruct((devices // PLANE, rows, 2 * LANES), jnp.bfloat16)
+        ] * PLANE
+    *sends, query, mixed = pl.pallas_call(
+        functools.partial(mix_body, plain),
         grid_spec=pltpu.PrefetchScalarGridSpec(
             num_scalar_prefetch=1,
             grid=(steps,),
@@ -299,17 +334,15 @@
             + [stream_spec(tail, s) for s in range(3)]
             + [stream_spec(taps, s) for s in range(3)]
             + [pl.BlockSpec((rows, step), lambda g, w: (0, base + g))],
-            out_specs=[
-                pl.BlockSpec((group, rows, 2 * LANES), lambda g, w: (g ^ (w[0] // group), 0, 0)),
-                pl.BlockSpec((group, rows, 2 * LANES), lambda g, w: (g ^ (w[0] // group), 0, 0)),
+            out_specs=send_specs
+            + [
                 pl.BlockSpec((rows, step), lambda g, w: (0, g)),
                 pl.BlockSpec((rows, step), lambda g, w: (0, g)),
             ],
             scratch_shapes=[pltpu.VMEM((3, tail + rows, step), jnp.float32)],
         ),
-        out_shape=[
-            jax.ShapeDtypeStruct((chips, rows, 2 * LANES), jnp.bfloat16),
-            jax.ShapeDtypeStruct((chips, rows, 2 * LANES), jnp.bfloat16),
+        out_shape=send_shapes
+        + [
             jax.ShapeDtypeStruct((rows, channels // chunks), jnp.float32),
             jax.ShapeDtypeStruct((rows, channels // chunks), jnp.bfloat16),
         ],
@@ -318,6 +351,7 @@
         ),
         name="mix",
     )(where, *[proj] * 3, *[before] * 3, *[short_weight] * 3, grad_out)
+    return (sends, query, mixed)
 
 
 def near_body(mixed, decay, gain, skip, near_out, spread, answer):
@@ -354,42 +388,56 @@
         near_out[:, lanes] = answer[pl.ds(piece, rows, stride=tiles), :]
 
 
-def near_part(mixed, decay, gain, skip):
+def near_part(mixed, decay, gain, skip, chunk):
     rows, width = mixed.shape
-    tiles = width // LANES
+    modes, tiles = decay.shape[0], width // LANES
     return pl.pallas_call(
         near_body,
+        grid=(1,),
+        in_specs=[
+            pl.BlockSpec((rows, width), lambda g: (0, 0)),
+            pl.BlockSpec((modes, tiles, LANES), lambda g: (0, chunk, 0)),
+            pl.BlockSpec((modes, tiles, LANES), lambda g: (0, chunk, 0)),
+            pl.BlockSpec((tiles, LANES), lambda g: (chunk, 0)),
+        ],
+        out_specs=pl.BlockSpec((rows, width), lambda g: (0, 0)),
         out_shape=jax.ShapeDtypeStruct((rows, width), jnp.float32),
         scratch_shapes=[
             pltpu.VMEM((rows * tiles, LANES), jnp.float32),
             pltpu.VMEM((rows * tiles, LANES), jnp.float32),
         ],
-        cost_estimate=pl.CostEstimate(
-            flops=4_000_000, transcendentals=0, bytes_accessed=8_000_000
-        ),
+        cost_estimate=pl.CostEstimate(flops=1000, transcendentals=0, bytes_accessed=1000),
         name="near",
     )(mixed, decay, gain, skip)
 
 
-def lag_body(chips, where, own, other, *rest):
-    sources = rest[: chips - 1]
-    (rate, amplitude, forward, backward, outer_forward, outer_backward, twist, out,
-     stacked, lined, high, low, back, turns) = rest[chips - 1 :]
-    chip, core = where[0], where[1]
-    devices = 2 * chips
-    rows = own.shape[-2]
+def lag_body(count, where, *refs):
+    sources = refs[:count]
+    (rate, amplitude, forward, backward, outer_forward, outer_backward, twist) = refs[count : count + 7]
+    (out, stacked, lined, high, low, back, turns, leads) = refs[count + 7 :]
+    plane, rank = where[0], where[1]
+    devices, rows = lined.shape[0], lined.shape[1]
     fine = FINE_PRODUCT // devices
     groups = rows // fine
     modes = rate.shape[0]
 
-    for turned in range(chips):
-        for side in range(2):
-            position = 2 * (turned ^ chip) + (side ^ core)
-            at = pl.ds(pl.multiple_of(position * fine, fine), fine)
-            whole = (own, other)[side][0] if turned == 0 else sources[turned - 1][side]
-            for group in range(groups):
-                stacked[group, at, :] = whole[group * fine : (group + 1) * fine, :]
-            lined[position] = whole[:, :LANES].astype(jnp.float32)
+    def place(position, whole):
+        at = pl.ds(pl.multiple_of(position * fine, fine), fine)
+        for group in range(groups):
+            stacked[group, at, :] = whole[group * fine : (group + 1) * fine, :]
+        lined[position] = whole[:, :LANES].astype(jnp.float32)
+
+    if count == 1:
+        for position in range(devices):
+            place(position, sources[0][position])
+    else:
+        for turned in range(devices // PLANE):
+            for side in range(PLANE):
+                whole = sources[side][0] if turned == 0 else sources[PLANE - 1 + turned][side]
+                place(PLANE * (turned ^ plane) + (side ^ rank), whole)
+
+    def store(line, at, value):
+        out[line, at, :] = value
 
     turns[0, 0] = twist[0]
     turns[0, 1] = twist[1]
@@ -459,12 +507,12 @@
     lead = amplitude[...] * decay
     carried = jnp.zeros((modes, LANES), jnp.float32)
     for p in range(devices):
-        turned = (p // 2) ^ chip
-        side = (p % 2) ^ core
         send_high, send_low = split_pair(lead * carried)
-        out[side, turned, rows : rows + modes, :] = send_high
-        out[side, turned, rows + modes : rows + 2 * modes, :] = send_low
+        leads[p, :modes, :] = send_high
+        leads[p, modes:, :] = send_low
         carried = far * carried + ends[p]
+    for line in range(devices):
+        store(line, slice(rows, rows + 2 * modes), leads[line])
 
     def last_step(group, carry):
         cos, sin = turns[group, 0], turns[group, 1]
@@ -477,31 +525,35 @@
             + dot32(outer_backward[FINE_PRODUCT:, :], back_high)
         ).astype(jnp.bfloat16)
         at = pl.ds(pl.multiple_of(group * fine, fine), fine)
-        for p in range(devices):
-            turned = (p // 2) ^ chip
-            side = (p % 2) ^ core
-            out[side, turned, at, :] = result[p * fine : (p + 1) * fine, :]
+        for line in range(devices):
+            store(line, at, result[line * fine : (line + 1) * fine, :])
         return carry
 
     lax.fori_loop(0, groups, last_step, 0, unroll=4)
 
 
-def lag_part(where, sent, received, moved, rate, amplitude, tables, devices):
-    rows = sent.shape[-2]
-    chips = devices // 2
+def lag_part(where, sources, rate, amplitude, tables, devices):
+    rows = sources[0].shape[-2]
     modes = rate.shape[0]
     groups = rows * devices // FINE_PRODUCT
-    whole = lambda shape: pl.BlockSpec(shape, lambda k, w: (0,) * len(shape))
+    height = rows + 2 * modes
+    count = len(sources)
+    whole = lambda shape: pl.BlockSpec(shape, lambda g, w: (0,) * len(shape))
+    if count == 1:
+        source_specs = [whole(sources[0].shape)]
+    else:
+        source_specs = [whole((1, rows, 2 * LANES))] * PLANE
+        source_specs += [whole(one.shape) for one in sources[PLANE:]]
+    out_shape = jax.ShapeDtypeStruct((devices, height, LANES), jnp.bfloat16)
     return pl.pallas_call(
-        functools.partial(lag_body, chips),
+        functools.partial(lag_body, count),
         grid_spec=pltpu.PrefetchScalarGridSpec(
             num_scalar_prefetch=1,
             grid=(1,),
-            in_specs=[whole((1, rows, 2 * LANES))] * 2
-            + [whole((2, rows, 2 * LANES))] * (chips - 1)
+            in_specs=source_specs
             + [whole((modes, LANES))] * 2
             + [whole(table.shape) for table in tables],
-            out_specs=[whole((2, chips, rows + 2 * modes, LANES))],
+            out_specs=whole(out_shape.shape),
             scratch_shapes=[
                 pltpu.VMEM((groups, FINE_PRODUCT, 2 * LANES), jnp.bfloat16),
                 pltpu.VMEM((devices, rows, LANES), jnp.float32),
@@ -509,29 +561,26 @@
                 pltpu.VMEM((devices, 2 * rows, 2 * LANES), jnp.bfloat16),
                 pltpu.VMEM((groups, 2 * FINE_PRODUCT, LANES), jnp.float32),
                 pltpu.VMEM((groups, 2, FINE_PRODUCT, LANES), jnp.float32),
+                pltpu.VMEM((devices, 2 * modes, LANES), jnp.bfloat16),
             ],
         ),
-        out_shape=[jax.ShapeDtypeStruct((2, chips, rows + 2 * modes, LANES), jnp.bfloat16)],
+        out_shape=out_shape,
         cost_estimate=pl.CostEstimate(
-            flops=5_000_000_000, transcendentals=0, bytes_accessed=12_000_000
+            flops=60_000_000_000, transcendentals=0, bytes_accessed=12_000_000
         ),
         name="lags",
-    )(where, sent, received, *moved, rate, amplitude, *tables)[0]
-
-
-def finish_body(chips, group, where, own, other, *rest):
-    sources = rest[: chips - 1]
-    near, query, decay = rest[chips - 1 : chips + 2]
-    gated_out, grad_out = rest[-2:]
-    chip, core = where[0], where[1]
+    )(where, *sources, rate, amplitude, *tables)
+
+
+def finish_body(arrived, near, query, decay, *refs):
+    gated_out, grad_out = refs[-2:]
     rows = near.shape[0]
     modes = decay.shape[0]
     line = lax.broadcasted_iota(jnp.int32, (8, LANES), 0)
 
-    def work(turned, side):
-        column = 2 * ((turned ^ chip) % group) + (side ^ core)
-        at = pl.ds(pl.multiple_of(column * LANES, LANES), LANES)
-        block = (own, other)[side].at[0] if turned == 0 else sources[turned - 1].at[side]
+    def work(column):
+        at = slice(column * LANES, (column + 1) * LANES)
+        block = arrived.at[column]
         grad_out[:, at] = block[:rows, :].astype(jnp.float32)
         lead = block[rows : rows + modes, :].astype(jnp.float32) + block[
             rows + modes : rows + 2 * modes, :
@@ -557,58 +606,41 @@
         conv = jnp.concatenate(total, axis=0).astype(jnp.bfloat16)
         gated_out[:, at] = (query[:, at] * conv.astype(jnp.float32)).astype(jnp.bfloat16)
 
-    for first in range(0, chips, group):
-
-        @pl.when(pl.program_id(0) == first // group)
-        def _(first=first):
-            for turned in range(first, first + group):
-                for side in range(2):
-                    work(turned, side)
-
-
-def finish_part(where, back, back_other, moved, near, query, decay, previous, chunk, chunks, devices):
+    for column in range(PAIR * PLANE):
+        work(column)
+
+
+def finish_part(arrived, near, query, decay, previous, chunk, chunks):
     rows, width = near.shape
-    chips = devices // 2
     modes = decay.shape[0]
-    height = back.shape[1]
-    group = FINISH_GROUP
-    step = 2 * group * LANES
+    step = PAIR * PLANE * LANES
     steps = width // step
-    whole = lambda shape: pl.BlockSpec(shape, lambda g, w: (0,) * len(shape))
-    column = lambda g, w: g ^ (w[0] // group)
-    in_specs = (
-        [whole((1, height, LANES))] * 2
-        + [whole((2, height, LANES))] * (chips - 1)
-        + [pl.BlockSpec((rows, step), lambda g, w: (0, column(g, w)))] * 2
-        + [pl.BlockSpec((modes, step), lambda g, w: (0, chunk * steps + column(g, w)))]
-    )
-    args = [back, back_other, *moved, near, query, decay]
+    here = lambda g: (0, chunk * steps + g)
+    in_specs = [
+        pl.BlockSpec((PAIR * PLANE, arrived.shape[1], LANES), lambda g: (g, 0, 0)),
+        pl.BlockSpec((rows, step), lambda g: (0, g)),
+        pl.BlockSpec((rows, step), lambda g: (0, g)),
+        pl.BlockSpec((modes, step), here),
+    ]
+    args = [arrived, near, query, decay]
     aliases = {}
     if previous is not None:
         in_specs += [pl.BlockSpec(memory_space=pl.ANY)] * 2
-        aliases = {len(args) + 1: 0, len(args) + 2: 1}
+        aliases = {len(args): 0, len(args) + 1: 1}
         args += list(previous)
     return pl.pallas_call(
-        functools.partial(finish_body, chips, group),
-        grid_spec=pltpu.PrefetchScalarGridSpec(
-            num_scalar_prefetch=1,
-            grid=(steps,),
-            in_specs=in_specs,
-            out_specs=[
-                pl.BlockSpec((rows, step), lambda g, w: (0, chunk * steps + column(g, w)))
-            ]
-            * 2,
-        ),
+        finish_body,
+        grid=(steps,),
+        in_specs=in_specs,
+        out_specs=[pl.BlockSpec((rows, step), here)] * 2,
         out_shape=[
             jax.ShapeDtypeStruct((rows, width * chunks), jnp.bfloat16),
             jax.ShapeDtypeStruct((rows, width * chunks), jnp.float32),
         ],
         input_output_aliases=aliases,
-        cost_estimate=pl.CostEstimate(
-            flops=4_000_000, transcendentals=0, bytes_accessed=5_000_000
-        ),
+        cost_estimate=pl.CostEstimate(flops=1000, transcendentals=0, bytes_accessed=1000),
         name="finish",
-    )(where, *args)
+    )(*args)
 
 
 def swap(value, mask, devices):
@@ -619,81 +651,59 @@
     return lax.optimization_barrier((value, earlier))[0]
 
 
-def hand_over(given, devices):
-    return swap(given, 1, devices)
-
-
-def spread_out(kept, received, devices):
-    chips = devices // 2
-    moved = {}
-    for k in CHIP_ORDER:
-        if k < chips:
-            block = jnp.concatenate([kept[k : k + 1], received[k : k + 1]], axis=0)
-            moved[k] = swap(block, 2 * k, devices)
-    return [moved[k] for k in range(1, chips)]
+def share(parts, devices):
+    return [parts[0]] + [swap(parts[side], side, devices) for side in range(1, PLANE)]
+
+
+def spread_out(shared, devices):
+    return [
+        swap(jnp.concatenate([one[k : k + 1] for one in shared], axis=0), PLANE * k, devices)
+        for k in range(1, devices // PLANE)
+    ]
+
+
+def all_to_all(sent):
+    return lax.all_to_all(sent, "seq", split_axis=0, concat_axis=0, tiled=True)
 
 
 def fast_on_device(proj, short_weight, residues, rates, skip, grad_out):
     devices = lax.axis_size("seq")
     rows, channels = grad_out.shape
     modes = rates.shape[0]
-    chunks = channels // (devices * LANES)
-    width = channels // chunks
+    width = channels // 2
     me = lax.axis_index("seq")
-    where = jnp.stack([me // 2, me % 2]).astype(jnp.int32)
+    where = jnp.stack([me // PLANE, me % PLANE]).astype(jnp.int32)
     before = lax.ppermute(
         proj[rows - HALO :], "seq", [(i, i + 1) for i in range(devices - 1)]
     )
-    shape = (modes, chunks, width // LANES, LANES)
-    mixes, ready = [], []
-    token = before
-    for chunk in range(chunks):
-        kept, given, query, mixed = mix_streams(
-            after(where, token), proj, before, short_weight, grad_out, chunk, chunks, devices
-        )
-        received = hand_over(given, devices)
-        moved = spread_out(kept, received, devices)
-        mixes.append((query, mixed))
-        ready.append((kept, received, moved))
-        token = moved[0]
-    last = ready[-1][1]
-    zero = after(jnp.zeros((), jnp.int32), last)
-    tables = spectral_tables(devices, rows, zero)
-    rates_late, residues_late, skip_late = after((rates, residues, skip), last)
-    decay = jnp.exp(-rates_late)
-    amplitude = residues_late * jnp.sqrt(rates_late)
-    decay_tiles = decay.reshape(shape)
-    gain_tiles = amplitude.reshape(shape)
-    skip_tiles = skip_late.reshape(shape[1:])
-    result = None
-    nears, returns = [], []
-    token = None
-    for chunk in range(chunks):
-        kept, received, moved = ready[chunk]
-        near = near_part(
-            after(mixes[chunk][1], tables if token is None else token),
-            decay_tiles[:, chunk],
-            gain_tiles[:, chunk],
-            skip_tiles[chunk],
-        )
+    streams = (proj, before, short_weight, grad_out)
+    (sent,), query_a, mixed_a = mix_streams(where, *streams, 0, 2, devices, True)
+    arrived = all_to_all(sent)
+    parts, query_b, mixed_b = mix_streams(after(where, sent), *streams, 1, 2, devices, False)
+    shared = share(parts, devices)
+    tables = spectral_tables(devices, rows, parts[0])
+    rates, residues, skip = after((rates, residues, skip), parts)
+    decay = jnp.exp(-rates)
+    amplitude = residues * jnp.sqrt(rates)
+    tiles = (modes, channels // LANES, LANES)
+    params = (decay.reshape(tiles), amplitude.reshape(tiles), skip.reshape(tiles[1:]))
+    near_a = near_part(mixed_a, *params, 0)
+    shared = after(shared, near_a, tables)
+    moved = spread_out(shared, devices)
+
+    def lags(guard, sources, chunk):
         start = chunk * width + me * LANES
-        rate_local = lax.dynamic_slice_in_dim(rates_late, start, LANES, 1)
-        amplitude_local = lax.dynamic_slice_in_dim(amplitude, start, LANES, 1)
-        guard = (token,) if chunk else (near, *[one[2][0] for one in ready[1:2]])
-        back = lag_part(
-            after(where, *guard), kept, received, moved, rate_local, amplitude_local, tables, devices
-        )
-        back_received = hand_over(back[1], devices)
-        back_moved = spread_out(back[0], back_received, devices)
-        nears.append(near)
-        returns.append((back[0], back_received, back_moved))
-        token = back_moved[0]
-    for chunk in range(chunks):
-        back_kept, back_received, back_moved = returns[chunk]
-        result = finish_part(
-            where, back_kept, back_received, back_moved, nears[chunk], mixes[chunk][0], decay,
-            result, chunk, chunks, devices,
-        )
+        rate = lax.dynamic_slice_in_dim(rates, start, LANES, 1)
+        lead = lax.dynamic_slice_in_dim(amplitude, start, LANES, 1)
+        return lag_part(after(where, guard), sources, rate, lead, tables, devices)
+
+    back_a = lags(shared[0], [arrived], 0)
+    arrived_a = all_to_all(back_a)
+    back_b = lags(back_a, [*shared, *moved], 1)
+    arrived_b = all_to_all(back_b)
+    near_b = near_part(after(mixed_b, back_b), *params, 1)
+    result = finish_part(arrived_a, near_a, query_a, decay, None, 0, 2)
+    result = finish_part(arrived_b, near_b, query_b, decay, result, 1, 2)
     return tuple(result)
 
 
@@ -702,9 +712,9 @@
         devices = lax.axis_size("seq")
         rows, channels = grad_out.shape
         fits = (
-            devices in (4, 8, 16)
+            devices in (8, 16)
             and rows % LANES == 0
-            and channels % (devices * LANES) == 0
+            and channels == 2 * devices * LANES
             and residues.shape[0] == 16
             and short_weight.shape[0] <= HALO + 1
         )

time: 152 us -> 118 us (0.78)
  starting transfers between devices: 60.7 us -> 30.4 us
  waiting for transfers between devices: 3.5 us -> 15.7 us
  other arithmetic: 9.16 us -> 1.49 us
  local copies, waits for them, and re-layouts: 13.5 us -> 6.5 us
    ppermute x32 -> x6, starting transfers between devices: 58.3 us -> 7.76 us  [swap(): return lax.ppermute(value, 'seq', [(i, i ^ mask) for i in range(devices)])]
    all_to_all x0 -> x3, starting transfers between devices: none -> 20.2 us  [all_to_all(): return lax.all_to_all(sent, 'seq', split_axis=0, concat_axis=0, tiled=True)]
    all_to_all x0 -> x3, waiting for transfers between devices: none -> 8.81 us  [all_to_all(): return lax.all_to_all(sent, 'seq', split_axis=0, concat_axis=0, tiled=True)]
    slice x9 -> x2, local copies, waits for them, and re-layouts: 4.68 us -> 0.06 us  [spread_out(): one[k:k + 1]]
    squeeze x3 -> x0, local copies, waits for them, and re-layouts: 4.47 us -> none  [the longest x1 1.86 us: fast_on_device(): back_received = hand_over(back[1], devices)]
    ppermute x32 -> x6, waiting for transfers between devices: 3.03 us -> 6.5 us  [swap(): return lax.ppermute(value, 'seq', [(i, i ^ mask) for i in range(devices)])]
    concatenate x32 -> x3, other arithmetic: 3.48 us -> 0.11 us  [spread_out(): jnp.concatenate([one[k:k + 1] for one in shared], axis=0)]
    convert_element_type x3 -> x0, other arithmetic: 2.82 us -> none  [split_outside(): return (high.astype(jnp.bfloat16), (value - high).astype(jnp.bfloat16))]
  transfers between devices with their start and end apart: 33 -> 10, of which waited for: 6 -> 4; matrix products, arithmetic and copies ran while one was open for 13% -> 3% of each run, Pallas kernels for 34% -> 45%
where the time goes in v3:
time: 118 us; the launch traced here: 117 us
  Pallas kernels  62.4 us (53%)
  starting transfers between devices  30.4 us (26%)
  waiting for transfers between devices  15.7 us (13%)
  local copies, waits for them, and re-layouts  6.5 us (6%)
  other arithmetic  1.49 us (1%)
    pallas_call x2, Pallas kernels, lag_part(): pl.pallas_call(functools.partial(lag_body, count), grid_spec=pltpu.Prefet...  28.5 us
    all_to_all x3, starting transfers between devices, all_to_all(): return lax.all_to_all(sent, 'seq', split_axis=0, concat_axis=0, tiled=True)  20.2 us
    pallas_call x2, Pallas kernels, mix_streams(): pl.pallas_call(functools.partial(mix_body, plain), grid_spec=pltpu.Prefet...  12.7 us
    pallas_call x2, Pallas kernels, near_part(): pl.pallas_call(near_body, grid=(1,), in_specs=[pl.BlockSpec((rows, width)...  10.9 us
    all_to_all x3, waiting for transfers between devices, all_to_all(): return lax.all_to_all(sent, 'seq', split_axis=0, concat_axis=0, tiled=True)  8.81 us
    ppermute x6, starting transfers between devices, swap(): return lax.ppermute(value, 'seq', [(i, i ^ mask) for i in range(devices)])  7.76 us
    pallas_call x2, Pallas kernels, finish_part(): pl.pallas_call(finish_body, grid=(steps,), in_specs=in_specs, out_specs=[...  7.45 us
    ppermute x6, waiting for transfers between devices, swap(): return lax.ppermute(value, 'seq', [(i, i ^ mask) for i in range(devices)])  6.5 us
  transfers between devices with their start and end apart: 10, of which 4 were waited for; matrix products, arithmetic and copies ran while one was open for 3% of the time, Pallas kernels for 45%

profile of v3, /device:TPU:0, one launch (start us, length us, event | category | flops | bytes accessed | tf_op | source)
XLA Modules:
  0.0 117.3 jit_solution(1765227609946766930)
XLA Ops:
  0.6 0.9 slice.39
  1.6 2.4 %collective-permute-start = (bf16[8,12288]{1,0:T(8,128)(2,1)S(1)}, bf16[8,12288]{1,0:T(8,128)(2,1)S(1)}, u32[]{:S(2)}, u32[]{:S(2)}) collective-permute-start(bf16[8,12288]{1,0:T(8,128)(2,1)S(1)} %slice.39), channel_id=1, source_target_pairs={{0,1},{1,2},{2,3},{3,4},{4,5},{5,6},{6,7},{7,8},{8,9},{9,10},{10,1... | collective-permute-start | bytes 589832 | tf_op jit(solution)/shard_map/ppermute | solution.py:676
  4.0 0.6 pad_add_fusion.where
  4.6 0.4 collective-permute-done.before_q.before_k.before_v
  5.0 0.0 copy-start
  5.0 0.7 copy-done
  5.7 6.2 %mix.2 = (bf16[16,128,256]{2,1,0:T(8,128)(2,1)}, f32[128,2048]{1,0:T(8,128)}, bf16[128,2048]{1,0:T(8,128)(2,1)}) custom-call(s32[2]{0:T(128)} %pad_add_fusion.where, bf16[128,12288]{1,0:T(8,128)(2,1)} %value_in.3, bf16[128,12288]{1,0:T(8,128)(2,1)} %value_in.3, bf16[128,12288]{1,0:T(8,128)(2,1)} %value_in.3, bf16[8,12288]{1,0:T(8,128)(2,1)} %copy-done, ...), custom_call_target="tpu_custom_call" | custom-call | flops 3000000 | bytes 5000000 | tf_op jit(solution)/shard_map/mix/pallas_call | solution.py:328
  11.9 11.0 %all-to-all-start = ((bf16[16,128,256]{2,1,0:T(8,128)(2,1)}), bf16[16,128,256]{2,1,0:T(8,128)(2,1)S(1)}, u32[]{:S(2)}, u32[]{:S(2)}) async-start(bf16[16,128,256]{2,1,0:T(8,128)(2,1)} %get-tuple-element.29), calls=%async_computation | async-start | bytes 2097152 | tf_op jit(solution)/shard_map/all_to_all | solution.py:666
  22.9 0.0 copy-start.5
  22.9 0.0 copy-start.6
  22.9 6.5 %mix.3 = (bf16[4,128,256]{2,1,0:T(8,128)(2,1)}, bf16[4,128,256]{2,1,0:T(8,128)(2,1)}, bf16[4,128,256]{2,1,0:T(8,128)(2,1)}, bf16[4,128,256]{2,1,0:T(8,128)(2,1)}...) custom-call(s32[2]{0:T(128)} %pad_add_fusion.where, bf16[128,12288]{1,0:T(8,128)(2,1)} %value_in.3, ...), custom_call_target="tpu_custom_call" | custom-call | flops 3000000 | bytes 5000000 | tf_op jit(solution)/shard_map/mix/pallas_call | solution.py:328
  29.4 0.5 collective-permute-start.1
  29.8 1.6 %collective-permute-start.2 = (bf16[4,128,256]{2,1,0:T(8,128)(2,1)}, bf16[4,128,256]{2,1,0:T(8,128)(2,1)S(1)}, u32[]{:S(2)}, u32[]{:S(2)}) collective-permute-start(bf16[4,128,256]{2,1,0:T(8,128)(2,1)} %get-tuple-element.33), channel_id=1, source_target_pairs={{0,2},{1,3},{2,0},{3,1},{4,6},{5,7},{6,4},{7,5},{8,10},{9,11},{10,... | collective-permute-start | bytes 786440 | tf_op jit(solution)/shard_map/ppermute | solution.py:647
  31.5 0.0 collective-permute-start.3
  31.5 0.0 copy-done.5
  31.5 0.0 copy-done.6
  31.5 0.0 copy-start.4
  31.5 0.8 negate_exponential_fusion
  32.3 2.9 %tables.1 = (bf16[512,256]{1,0:T(8,128)(2,1)}, bf16[512,256]{1,0:T(8,128)(2,1)}, bf16[1024,256]{1,0:T(8,128)(2,1)}, bf16[512,512]{1,0:T(8,128)(2,1)}, f32[4,256,128]{2,1,0:T(8,128)}) custom-call(bf16[4,128,256]{2,1,0:T(8,128)(2,1)} %get-tuple-element.44.earlier.refs_0_), custom_call_target="tpu_custom_call" | custom-call | flops 1000 | bytes 1000 | tf_op jit(solution)/shard_map/tables/pallas_call | solution.py:251
  35.1 0.8 copy.10
  35.9 0.8 copy.11
  36.7 5.5 %near.2 = f32[128,2048]{1,0:T(8,128)} custom-call(bf16[128,2048]{1,0:T(8,128)(2,1)} %get-tuple-element.35.mixed, f32[16,32,128]{2,1,0:T(8,128)} %bitcast.8, f32[16,32,128]{2,1,0:T(8,128)} %bitcast.10, f32[32,128]{1,0:T(8,128)} %bitcast.13), custom_call_target="tpu_custom_call" | custom-call | flops 1000 | bytes 1000 | tf_op jit(solution)/shard_map/near/pallas_call | solution.py:394
  42.2 0.6 constant_dynamic-slice_fusion
  42.8 0.0 collective-permute-done.1.refs_1_
  42.8 0.0 copy-start.7
  42.8 0.0 collective-permute-done.2.refs_2_
  42.8 0.0 copy-start.8
  42.8 6.5 %collective-permute-done.3.refs_3_ = bf16[4,128,256]{2,1,0:T(8,128)(2,1)S(1)} collective-permute-done((bf16[4,128,256]{2,1,0:T(8,128)(2,1)}, bf16[4,128,256]{2,1,0:T(8,128)(2,1)S(1)}, u32[]{:S(2)}, u32[]{:S(2)}) %collective-permute-start.3) | collective-permute-done | bytes 262176 | tf_op jit(solution)/shard_map/ppermute | solution.py:647
  49.3 0.0 copy-start.9
  49.3 0.0 copy-done.4
  49.4 3.1 %collective-permute-start.4 = (bf16[4,128,256]{2,1,0:T(8,128)(2,1)S(1)}, bf16[4,128,256]{2,1,0:T(8,128)(2,1)S(1)}, u32[]{:S(2)}, u32[]{:S(2)}) collective-permute-start(bf16[4,128,256]{2,1,0:T(8,128)(2,1)S(1)} %pad_maximum_fusion), channel_id=1, source_target_pairs={{0,4},{1,5},{2,6},{3,7},{4,0},{5,1},{6,2},{7,3},{8,12},{9,13},{10,... | collective-permute-start | bytes 786440 | tf_op jit(solution)/shard_map/ppermute | solution.py:647
  52.6 0.6 collective-permute-start.5
  53.3 1.9 %collective-permute-start.6 = (bf16[4,128,256]{2,1,0:T(8,128)(2,1)S(1)}, bf16[4,128,256]{2,1,0:T(8,128)(2,1)S(1)}, u32[]{:S(2)}, u32[]{:S(2)}) collective-permute-start(bf16[4,128,256]{2,1,0:T(8,128)(2,1)S(1)} %pad_maximum_fusion.2), channel_id=1, source_target_pairs={{0,12},{1,13},{2,14},{3,15},{4,8},{5,9},{6,10},{7,11},{8,4},{9,5},... | collective-permute-start | bytes 786440 | tf_op jit(solution)/shard_map/ppermute | solution.py:647
  55.2 0.0 all-to-all-done.refs_0_
  55.2 0.0 copy-start.3
  55.2 1.0 copy-done.3
  56.1 14.2 %lags.2 = bf16[16,160,128]{2,1,0:T(8,128)(2,1)} custom-call(s32[2]{0:T(128)} %pad_add_fusion.where, bf16[16,128,256]{2,1,0:T(8,128)(2,1)} %copy-done.3, f32[16,128]{1,0:T(8,128)} %get-tuple-element.81.refs_1_, f32[16,128]{1,0:T(8,128)} %get-tuple-element.60.refs_2_, bf16[512,256]{1,0:T(8,128)(2,1)} %get-tuple-element.39.refs_3_.refs_9_, ...), custom_call_target="tpu_custom_call" | custom-call | flops 60000002048 | bytes 12000000 | tf_op jit(solution)/shard_map/lags/pallas_call | solution.py:548
  70.3 0.0 copy-done.7
  70.3 0.0 copy-done.8
  70.3 0.0 copy-done.9
  70.3 4.3 %all-to-all-start.2 = ((bf16[16,160,128]{2,1,0:T(8,128)(2,1)}), bf16[16,160,128]{2,1,0:T(8,128)(2,1)S(1)}, u32[]{:S(2)}, u32[]{:S(2)}) async-start(bf16[16,160,128]{2,1,0:T(8,128)(2,1)} %lags.2), calls=%async_computation.2 | async-start | bytes 1310720 | tf_op jit(solution)/shard_map/all_to_all | solution.py:666
  74.6 0.0 collective-permute-done.4.refs_4_
  74.6 0.0 copy-start.10
  74.7 0.0 collective-permute-done.5.refs_5_
  74.7 0.0 copy-start.11
  74.7 0.0 collective-permute-done.6.refs_6_
  74.7 0.0 copy-start.12
  74.7 0.7 copy-done.10
  75.4 0.1 copy-done.11
  75.5 0.1 copy-done.12
  75.5 14.3 %lags.3 = bf16[16,160,128]{2,1,0:T(8,128)(2,1)} custom-call(s32[2]{0:T(128)} %pad_add_fusion.where, bf16[4,128,256]{2,1,0:T(8,128)(2,1)} %get-tuple-element.44.earlier.refs_0_, bf16[4,128,256]{2,1,0:T(8,128)(2,1)} %copy-done.7, bf16[4,128,256]{2,1,0:T(8,128)(2,1)} %copy-done.8, bf16[4,128,256]{2,1,0:T(8,128)(2,1)} %copy-done.9, ...), custom_call_target="tpu_custom_call" | custom-call | flops 60000002048 | bytes 12000000 | tf_op jit(solution)/shard_map/lags/pallas_call | solution.py:548
  89.8 1.4 %all-to-all-done.2.arrived = bf16[16,160,128]{2,1,0:T(8,128)(2,1)S(1)} async-done(((bf16[16,160,128]{2,1,0:T(8,128)(2,1)}), bf16[16,160,128]{2,1,0:T(8,128)(2,1)S(1)}, u32[]{:S(2)}, u32[]{:S(2)}) %all-to-all-start.2) | async-done | bytes 655392 | tf_op jit(solution)/shard_map/all_to_all | solution.py:666
  91.2 0.0 copy-start.2
  91.2 5.0 %all-to-all-start.1 = ((bf16[16,160,128]{2,1,0:T(8,128)(2,1)}), bf16[16,160,128]{2,1,0:T(8,128)(2,1)S(1)}, u32[]{:S(2)}, u32[]{:S(2)}) async-start(bf16[16,160,128]{2,1,0:T(8,128)(2,1)} %lags.3), calls=%async_computation.1 | async-start | bytes 1310720 | tf_op jit(solution)/shard_map/all_to_all | solution.py:666
  96.2 5.5 %near.3 = f32[128,2048]{1,0:T(8,128)} custom-call(bf16[128,2048]{1,0:T(8,128)(2,1)} %get-tuple-element.51.mixed, f32[16,32,128]{2,1,0:T(8,128)} %bitcast.9, f32[16,32,128]{2,1,0:T(8,128)} %bitcast.11, f32[32,128]{1,0:T(8,128)} %bitcast.14), custom_call_target="tpu_custom_call" | custom-call | flops 1000 | bytes 1000 | tf_op jit(solution)/shard_map/near/pallas_call | solution.py:394
  101.6 0.0 copy-done.2
  101.6 3.7 %finish.2 = (bf16[128,4096]{1,0:T(8,128)(2,1)}, f32[128,4096]{1,0:T(8,128)}) custom-call(bf16[16,160,128]{2,1,0:T(8,128)(2,1)} %copy-done.2, f32[128,2048]{1,0:T(8,128)} %near.2, f32[128,2048]{1,0:T(8,128)} %get-tuple-element.53.query, f32[16,4096]{1,0:T(8,128)} %get-tuple-element.56.decay), custom_call_target="tpu_custom_call" | custom-call | flops 1000 | bytes 1000 | tf_op jit(solution)/shard_map/finish/pallas_call | solution.py:631
  105.4 7.4 %all-to-all-done.1.arrived = bf16[16,160,128]{2,1,0:T(8,128)(2,1)S(1)} async-done(((bf16[16,160,128]{2,1,0:T(8,128)(2,1)}), bf16[16,160,128]{2,1,0:T(8,128)(2,1)S(1)}, u32[]{:S(2)}, u32[]{:S(2)}) %all-to-all-start.1) | async-done | bytes 655392 | tf_op jit(solution)/shard_map/all_to_all | solution.py:666
  112.7 0.0 copy-start.1
  112.7 0.8 copy-done.1
  113.6 3.7 %finish.3 = (bf16[128,4096]{1,0:T(8,128)(2,1)}, f32[128,4096]{1,0:T(8,128)}) custom-call(bf16[16,160,128]{2,1,0:T(8,128)(2,1)} %copy-done.1, f32[128,2048]{1,0:T(8,128)} %near.3, f32[128,2048]{1,0:T(8,128)} %get-tuple-element.52.query, f32[16,4096]{1,0:T(8,128)} %get-tuple-element.56.decay, ...), custom_call_target="tpu_custom_call", output_to_operand_aliasing={{0}: (4, {}), {1}: (5, {})} | custom-call | flops 1000 | bytes 1000 | tf_op jit(solution)/shard_map/finish/pallas_call | solution.py:631
  (5 shorter events, 0.2 us)
Async XLA Ops:
  1.6 3.5 %collective-permute-start = (bf16[8,12288]{1,0:T(8,128)(2,1)S(1)}, bf16[8,12288]{1,0:T(8,128)(2,1)S(1)}, u32[]{:S(2)}, u32[]{:S(2)}) collective-permute-start(bf16[8,12288]{1,0:T(8,128)(2,1)S(1)} %slice.39), channel_id=1, source_target_pairs={{0,1},{1,2},{2,3},{3,4},{4,5},{5,6},{6,7},{7,8},{8,9},{9,10},{10,1... | collective-permute-start | bytes 589832 | tf_op jit(solution)/shard_map/ppermute | solution.py:676
  5.0 0.7 copy-start
  11.9 43.2 %all-to-all-start = ((bf16[16,128,256]{2,1,0:T(8,128)(2,1)}), bf16[16,128,256]{2,1,0:T(8,128)(2,1)S(1)}, u32[]{:S(2)}, u32[]{:S(2)}) async-start(bf16[16,128,256]{2,1,0:T(8,128)(2,1)} %get-tuple-element.29), calls=%async_computation | async-start | bytes 2097152 | tf_op jit(solution)/shard_map/all_to_all | solution.py:666
  22.9 8.6 %copy-start.5 = (f32[16,4096]{1,0:T(8,128)S(1)}, f32[16,4096]{1,0:T(8,128)}, u32[]{:S(2)}) copy-start(f32[16,4096]{1,0:T(8,128)} %param.9) | copy-start | bytes 786436
  22.9 8.6 %copy-start.6 = (f32[16,4096]{1,0:T(8,128)S(1)}, f32[16,4096]{1,0:T(8,128)}, u32[]{:S(2)}) copy-start(f32[16,4096]{1,0:T(8,128)} %param.8) | copy-start | bytes 786436
  29.4 13.4 %collective-permute-start.1 = (bf16[4,128,256]{2,1,0:T(8,128)(2,1)}, bf16[4,128,256]{2,1,0:T(8,128)(2,1)S(1)}, u32[]{:S(2)}, u32[]{:S(2)}) collective-permute-start(bf16[4,128,256]{2,1,0:T(8,128)(2,1)} %get-tuple-element.32), channel_id=1, source_target_pairs={{0,1},{1,0},{2,3},{3,2},{4,5},{5,4},{6,7},{7,6},{8,9},{9,8},{10,11... | collective-permute-start | bytes 786440 | tf_op jit(solution)/shard_map/ppermute | solution.py:647
  29.8 13.0 %collective-permute-start.2 = (bf16[4,128,256]{2,1,0:T(8,128)(2,1)}, bf16[4,128,256]{2,1,0:T(8,128)(2,1)S(1)}, u32[]{:S(2)}, u32[]{:S(2)}) collective-permute-start(bf16[4,128,256]{2,1,0:T(8,128)(2,1)} %get-tuple-element.33), channel_id=1, source_target_pairs={{0,2},{1,3},{2,0},{3,1},{4,6},{5,7},{6,4},{7,5},{8,10},{9,11},{10,... | collective-permute-start | bytes 786440 | tf_op jit(solution)/shard_map/ppermute | solution.py:647
  31.5 17.8 %collective-permute-start.3 = (bf16[4,128,256]{2,1,0:T(8,128)(2,1)}, bf16[4,128,256]{2,1,0:T(8,128)(2,1)S(1)}, u32[]{:S(2)}, u32[]{:S(2)}) collective-permute-start(bf16[4,128,256]{2,1,0:T(8,128)(2,1)} %get-tuple-element.34), channel_id=1, source_target_pairs={{0,3},{1,2},{2,1},{3,0},{4,7},{5,6},{6,5},{7,4},{8,11},{9,10},{10,... | collective-permute-start | bytes 786440 | tf_op jit(solution)/shard_map/ppermute | solution.py:647
  31.5 17.8 %copy-start.4 = (bf16[4,128,256]{2,1,0:T(8,128)(2,1)S(1)}, bf16[4,128,256]{2,1,0:T(8,128)(2,1)}, u32[]{:S(2)}) copy-start(bf16[4,128,256]{2,1,0:T(8,128)(2,1)} %get-tuple-element.44.earlier.refs_0_) | copy-start | bytes 786436
  42.8 27.6 %copy-start.7 = (bf16[4,128,256]{2,1,0:T(8,128)(2,1)}, bf16[4,128,256]{2,1,0:T(8,128)(2,1)S(1)}, u32[]{:S(2)}) copy-start(bf16[4,128,256]{2,1,0:T(8,128)(2,1)S(1)} %collective-permute-done.1.refs_1_) | copy-start | bytes 786436
  42.8 27.5 %copy-start.8 = (bf16[4,128,256]{2,1,0:T(8,128)(2,1)}, bf16[4,128,256]{2,1,0:T(8,128)(2,1)S(1)}, u32[]{:S(2)}) copy-start(bf16[4,128,256]{2,1,0:T(8,128)(2,1)S(1)} %collective-permute-done.2.refs_2_) | copy-start | bytes 786436
  49.3 21.0 %copy-start.9 = (bf16[4,128,256]{2,1,0:T(8,128)(2,1)}, bf16[4,128,256]{2,1,0:T(8,128)(2,1)S(1)}, u32[]{:S(2)}) copy-start(bf16[4,128,256]{2,1,0:T(8,128)(2,1)S(1)} %collective-permute-done.3.refs_3_) | copy-start | bytes 786436
  49.4 25.2 %collective-permute-start.4 = (bf16[4,128,256]{2,1,0:T(8,128)(2,1)S(1)}, bf16[4,128,256]{2,1,0:T(8,128)(2,1)S(1)}, u32[]{:S(2)}, u32[]{:S(2)}) collective-permute-start(bf16[4,128,256]{2,1,0:T(8,128)(2,1)S(1)} %pad_maximum_fusion), channel_id=1, source_target_pairs={{0,4},{1,5},{2,6},{3,7},{4,0},{5,1},{6,2},{7,3},{8,12},{9,13},{10,... | collective-permute-start | bytes 786440 | tf_op jit(solution)/shard_map/ppermute | solution.py:647
  52.6 22.1 %collective-permute-start.5 = (bf16[4,128,256]{2,1,0:T(8,128)(2,1)S(1)}, bf16[4,128,256]{2,1,0:T(8,128)(2,1)S(1)}, u32[]{:S(2)}, u32[]{:S(2)}) collective-permute-start(bf16[4,128,256]{2,1,0:T(8,128)(2,1)S(1)} %pad_maximum_fusion.1), channel_id=1, source_target_pairs={{0,8},{1,9},{2,10},{3,11},{4,12},{5,13},{6,14},{7,15},{8,0},{9,1},... | collective-permute-start | bytes 786440 | tf_op jit(solution)/shard_map/ppermute | solution.py:647
  53.3 21.4 %collective-permute-start.6 = (bf16[4,128,256]{2,1,0:T(8,128)(2,1)S(1)}, bf16[4,128,256]{2,1,0:T(8,128)(2,1)S(1)}, u32[]{:S(2)}, u32[]{:S(2)}) collective-permute-start(bf16[4,128,256]{2,1,0:T(8,128)(2,1)S(1)} %pad_maximum_fusion.2), channel_id=1, source_target_pairs={{0,12},{1,13},{2,14},{3,15},{4,8},{5,9},{6,10},{7,11},{8,4},{9,5},... | collective-permute-start | bytes 786440 | tf_op jit(solution)/shard_map/ppermute | solution.py:647
  55.2 1.0 copy-start.3
  70.3 20.9 %all-to-all-start.2 = ((bf16[16,160,128]{2,1,0:T(8,128)(2,1)}), bf16[16,160,128]{2,1,0:T(8,128)(2,1)S(1)}, u32[]{:S(2)}, u32[]{:S(2)}) async-start(bf16[16,160,128]{2,1,0:T(8,128)(2,1)} %lags.2), calls=%async_computation.2 | async-start | bytes 1310720 | tf_op jit(solution)/shard_map/all_to_all | solution.py:666
  74.6 0.7 copy-start.10
  74.7 0.8 copy-start.11
  74.7 0.8 copy-start.12
  91.2 10.4 %copy-start.2 = (bf16[16,160,128]{2,1,0:T(8,128)(2,1)}, bf16[16,160,128]{2,1,0:T(8,128)(2,1)S(1)}, u32[]{:S(2)}) copy-start(bf16[16,160,128]{2,1,0:T(8,128)(2,1)S(1)} %all-to-all-done.2.arrived) | copy-start | bytes 1966084
  91.2 21.5 %all-to-all-start.1 = ((bf16[16,160,128]{2,1,0:T(8,128)(2,1)}), bf16[16,160,128]{2,1,0:T(8,128)(2,1)S(1)}, u32[]{:S(2)}, u32[]{:S(2)}) async-start(bf16[16,160,128]{2,1,0:T(8,128)(2,1)} %lags.3), calls=%async_computation.1 | async-start | bytes 1310720 | tf_op jit(solution)/shard_map/all_to_all | solution.py:666
  112.7 0.8 copy-start.1

commit v4 on v3

--- a/solution.py
+++ b/solution.py
@@ -11,8 +11,7 @@
 HIGH_PRECISION = lax.Precision.HIGH
 LANES = 128
 HALO = 8
-FINE_PRODUCT = 256
-UNROLL = 8
+UNROLL = 16
 STRIP = 32
 PLANE = 4
 PAIR = 2
@@ -193,10 +192,8 @@
     return angle * series
 
 
-def table_body(devices, rows, forward, backward, outer_forward, outer_backward, twist):
-    fine = FINE_PRODUCT // devices
-    log_rows, log_fine = rows.bit_length() - 1, fine.bit_length() - 1
-    log_product = FINE_PRODUCT.bit_length() - 1
+def table_body(devices, rows, forward, backward, twist):
+    log_rows = rows.bit_length() - 1
     length = devices * rows
 
     def fill(out, height, width, value):
@@ -214,29 +211,12 @@
 
         return value
 
-    def outer(line, lane):
-        coarse = (line & (FINE_PRODUCT - 1)) >> log_fine
-        turns = (2 * coarse + 1) * (lane >> log_fine) + (line >> log_product) * devices
-        same = (line & (fine - 1)) == (lane & (fine - 1))
-        return jnp.where(same, cosines(turns, 4 * devices), 0.0)
-
-    def outer_back(line, lane):
-        coarse = (lane & (FINE_PRODUCT - 1)) >> log_fine
-        position = line >> log_fine
-        turns = (2 * coarse + 1) * position + (lane >> log_product) * devices
-        same = (line & (fine - 1)) == (lane & (fine - 1))
-        return jnp.where(same, cosines(turns, 4 * devices) * (1.0 / length), 0.0)
-
     fill(forward, 2 * rows, 2 * rows, base(1))
     fill(backward, 2 * rows, 2 * rows, base(-1))
-    fill(outer_forward, 2 * FINE_PRODUCT, FINE_PRODUCT, outer)
-    fill(outer_backward, FINE_PRODUCT, 2 * FINE_PRODUCT, outer_back)
-    for start in range(0, FINE_PRODUCT, STRIP):
-        line = lax.broadcasted_iota(jnp.int32, (STRIP, LANES), 0) + start
-        odd = 2 * (line >> log_fine) + 1
-        for index, turns in enumerate((odd * (line & (fine - 1)), odd * fine)):
-            twist[2 * index, start : start + STRIP, :] = cosines(turns, 4 * length)
-            twist[2 * index + 1, start : start + STRIP, :] = cosines(turns - length, 4 * length)
+    line = lax.broadcasted_iota(jnp.int32, (8 * devices, LANES), 0)
+    turns = (4 * (line >> 3) + 1) * (line & 7)
+    twist[0] = cosines(turns, 4 * length)
+    twist[1] = cosines(turns - length, 4 * length)
 
 
 def spectral_tables(devices, rows, earlier):
@@ -244,9 +224,7 @@
     shapes = [
         jax.ShapeDtypeStruct((4 * rows, 2 * rows), jnp.bfloat16),
         jax.ShapeDtypeStruct((4 * rows, 2 * rows), jnp.bfloat16),
-        jax.ShapeDtypeStruct((4 * FINE_PRODUCT, FINE_PRODUCT), jnp.bfloat16),
-        jax.ShapeDtypeStruct((2 * FINE_PRODUCT, 2 * FINE_PRODUCT), jnp.bfloat16),
-        jax.ShapeDtypeStruct((4, FINE_PRODUCT, LANES), jnp.float32),
+        jax.ShapeDtypeStruct((2, 8 * devices, LANES), jnp.float32),
     ]
     return pl.pallas_call(
         lambda earlier, *outs: table_body(devices, rows, *outs),
@@ -262,10 +240,10 @@
 
 
 def mix_body(
-    plain, where, query_in, key_in, value_in, before_q, before_k, before_v,
+    plain, skipped, where, query_in, key_in, value_in, before_q, before_k, before_v,
     weight_q, weight_k, weight_v, cot, *outputs
 ):
-    *sends, query_out, mixed_out, padded = outputs
+    *sends, query_out, mixed_out, padded = outputs[skipped:]
     taps = weight_q.shape[0]
     rows = query_in.shape[0]
     tail = before_q.shape[0]
@@ -303,10 +281,13 @@
                 work(PLANE * index + (rank ^ side), sends[side], index ^ (plane % PAIR))
 
 
-def mix_streams(where, proj, before, short_weight, grad_out, chunk, chunks, devices, plain):
-    rows, channels = grad_out.shape
+def mix_streams(
+    where, proj, before, short_weight, grad_out, chunk, chunks, devices, plain, top=None, earlier=None
+):
+    full, channels = grad_out.shape
+    rows = full if top is None else top
     taps = short_weight.shape[0]
-    tail = before.shape[0]
+    tail = HALO
     step = PAIR * PLANE * LANES
     steps = channels // chunks // step
     base = chunk * steps
@@ -317,23 +298,26 @@
 
     if plain:
         send_specs = [pl.BlockSpec((PAIR * PLANE, rows, 2 * LANES), lambda g, w: (g, 0, 0))]
-        send_shapes = [jax.ShapeDtypeStruct((devices, rows, 2 * LANES), jnp.bfloat16)]
+        send_shapes = [jax.ShapeDtypeStruct((devices, full, 2 * LANES), jnp.bfloat16)]
     else:
         send_specs = [
             pl.BlockSpec((PAIR, rows, 2 * LANES), lambda g, w: (g ^ (w[0] // PAIR), 0, 0))
         ] * PLANE
         send_shapes = [
-            jax.ShapeDtypeStruct((devices // PLANE, rows, 2 * LANES), jnp.bfloat16)
+            jax.ShapeDtypeStruct((devices // PLANE, full, 2 * LANES), jnp.bfloat16)
         ] * PLANE
+    earlier = () if earlier is None else earlier
+    operands = (*[proj] * 3, *[before] * 3, *[short_weight] * 3, grad_out)
     *sends, query, mixed = pl.pallas_call(
-        functools.partial(mix_body, plain),
+        functools.partial(mix_body, plain, len(earlier)),
         grid_spec=pltpu.PrefetchScalarGridSpec(
             num_scalar_prefetch=1,
             grid=(steps,),
             in_specs=[stream_spec(rows, s) for s in range(3)]
             + [stream_spec(tail, s) for s in range(3)]
             + [stream_spec(taps, s) for s in range(3)]
-            + [pl.BlockSpec((rows, step), lambda g, w: (0, base + g))],
+            + [pl.BlockSpec((rows, step), lambda g, w: (0, base + g))]
+            + [pl.BlockSpec(memory_space=pl.ANY)] * len(earlier),
             out_specs=send_specs
             + [
                 pl.BlockSpec((rows, step), lambda g, w: (0, g)),
@@ -343,14 +327,15 @@
         ),
         out_shape=send_shapes
         + [
-            jax.ShapeDtypeStruct((rows, channels // chunks), jnp.float32),
-            jax.ShapeDtypeStruct((rows, channels // chunks), jnp.bfloat16),
+            jax.ShapeDtypeStruct((full, channels // chunks), jnp.float32),
+            jax.ShapeDtypeStruct((full, channels // chunks), jnp.bfloat16),
         ],
+        input_output_aliases={len(operands) + 1 + i: i for i in range(len(earlier))},
         cost_estimate=pl.CostEstimate(
             flops=3_000_000, transcendentals=0, bytes_accessed=5_000_000
         ),
         name="mix",
-    )(where, *[proj] * 3, *[before] * 3, *[short_weight] * 3, grad_out)
+    )(where, *operands, *earlier)
     return (sends, query, mixed)
 
 
@@ -411,21 +396,46 @@
     )(mixed, decay, gain, skip)
 
 
+def fourier(values, sign):
+    size = len(values)
+    if size == 1:
+        return values
+    evens, odds = fourier(values[::2], sign), fourier(values[1::2], sign)
+    result = [None] * size
+    for k in range(size // 2):
+        real, imag = odds[k]
+        if 4 * k == size:
+            real, imag, sums = imag, real, (-sign, sign)
+        else:
+            sums = (1, 1)
+            cos, sin = math.cos(2 * math.pi * k / size), sign * math.sin(2 * math.pi * k / size)
+            if 8 * k in (size, 3 * size):
+                root = math.sqrt(0.5)
+                up, down = (real + imag) * root, (imag - real) * root
+                turned = {(1, 1): (-down, up), (1, -1): (up, down), (-1, 1): (-up, -down), (-1, -1): (down, -up)}
+                real, imag = turned[(1 if cos > 0 else -1, 1 if sin > 0 else -1)]
+            elif k:
+                real, imag = real * cos - imag * sin, real * sin + imag * cos
+        even_real, even_imag = evens[k]
+        plus = lambda left, right, way: left + right if way > 0 else left - right
+        result[k] = (plus(even_real, real, sums[0]), plus(even_imag, imag, sums[1]))
+        result[k + size // 2] = (plus(even_real, real, -sums[0]), plus(even_imag, imag, -sums[1]))
+    return result
+
+
 def lag_body(count, where, *refs):
     sources = refs[:count]
-    (rate, amplitude, forward, backward, outer_forward, outer_backward, twist) = refs[count : count + 7]
-    (out, stacked, lined, high, low, back, turns, leads) = refs[count + 7 :]
+    (rate, amplitude, forward, backward, twist) = refs[count : count + 5]
+    (out, lined, data, back, plain, spin) = refs[count + 5 :]
     plane, rank = where[0], where[1]
-    devices, rows = lined.shape[0], lined.shape[1]
-    fine = FINE_PRODUCT // devices
-    groups = rows // fine
+    devices, rows = lined.shape[1], lined.shape[2]
+    tiles = rows // 8
     modes = rate.shape[0]
+    length = devices * rows
 
     def place(position, whole):
-        at = pl.ds(pl.multiple_of(position * fine, fine), fine)
-        for group in range(groups):
-            stacked[group, at, :] = whole[group * fine : (group + 1) * fine, :]
-        lined[position] = whole[:, :LANES].astype(jnp.float32)
+        for half in range(2):
+            lined[half, position] = whole[:, half * LANES : (half + 1) * LANES].astype(jnp.float32)
 
     if count == 1:
         for position in range(devices):
@@ -433,44 +443,47 @@
     else:
         for turned in range(devices // PLANE):
             for side in range(PLANE):
-                whole = sources[side][0] if turned == 0 else sources[PLANE - 1 + turned][side]
+                if turned == 0:
+                    whole = sources[side][0]
+                else:
+                    pair = (devices // PLANE - 1) * (side // 2) + turned - 1
+                    whole = sources[PLANE + pair][side % 2]
                 place(PLANE * (turned ^ plane) + (side ^ rank), whole)
 
-    def store(line, at, value):
-        out[line, at, :] = value
-
-    turns[0, 0] = twist[0]
-    turns[0, 1] = twist[1]
-    for group in range(1, groups):
-        cos, sin = turns[group - 1, 0], turns[group - 1, 1]
-        turns[group, 0] = cos * twist[2] - sin * twist[3]
-        turns[group, 1] = sin * twist[2] + cos * twist[3]
-
-    def outer_step(group, carry):
-        signal = stacked[group]
-        first = dot32(outer_forward[: 2 * FINE_PRODUCT, :], signal) + dot32(
-            outer_forward[2 * FINE_PRODUCT :, :], signal
-        )
-        cos, sin = turns[group, 0], turns[group, 1]
-        cos = jnp.concatenate([cos, cos], axis=1)
-        sin = jnp.concatenate([sin, sin], axis=1)
-        real, imag = first[:FINE_PRODUCT], first[FINE_PRODUCT:]
-        pairs = (split_pair(real * cos + imag * sin), split_pair(imag * cos - real * sin))
+    def advance_spin():
         for k in range(devices):
-            source = slice(k * fine, (k + 1) * fine)
-            for part in range(2):
-                at = pl.ds(pl.multiple_of(part * rows + group * fine, fine), fine)
-                high[k, at, :] = pairs[part][0][source, :]
-                low[k, at, :] = pairs[part][1][source, :]
+            line = slice(8 * k, 8 * k + 8)
+            angle = 2.0 * math.pi * 8 * (4 * k + 1) / (4 * length)
+            cos, sin = spin[0, line, :], spin[1, line, :]
+            spin[0, line, :] = cos * math.cos(angle) - sin * math.sin(angle)
+            spin[1, line, :] = sin * math.cos(angle) + cos * math.sin(angle)
+
+    def outer_step(tile, carry):
+        at = pl.ds(pl.multiple_of(tile * 8, 8), 8)
+        imag_at = pl.ds(pl.multiple_of(rows + tile * 8, 8), 8)
+        for half in range(2):
+            lanes = slice(half * LANES, (half + 1) * LANES)
+            values = []
+            for p in range(devices):
+                angle = math.pi * p / (2 * devices)
+                here = lined[half, p, at, :]
+                values.append((here * math.cos(angle), here * -math.sin(angle)))
+            for k, (real, imag) in enumerate(fourier(values, -1)):
+                cos, sin = spin[0, 8 * k : 8 * k + 8, :], spin[1, 8 * k : 8 * k + 8, :]
+                data[k, at, lanes] = real * cos + imag * sin
+                data[k, imag_at, lanes] = imag * cos - real * sin
+        advance_spin()
         return carry
 
-    lax.fori_loop(0, groups, outer_step, 0, unroll=4)
+    spin[...] = twist[...]
+    lax.fori_loop(0, tiles, outer_step, 0)
 
     def inner_step(k, carry):
+        high, low = split_pair(data[k])
         spectrum = (
-            dot32(forward[: 2 * rows], high[k])
-            + dot32(forward[: 2 * rows], low[k])
-            + dot32(forward[2 * rows :], high[k])
+            dot32(forward[: 2 * rows], high)
+            + dot32(forward[: 2 * rows], low)
+            + dot32(forward[2 * rows :], high)
         )
         real_m, imag_m = spectrum[:rows, :LANES], spectrum[rows:, :LANES]
         real_s, imag_s = spectrum[:rows, LANES:], spectrum[rows:, LANES:]
@@ -478,16 +491,11 @@
             [real_m * real_s + imag_m * imag_s, real_m * imag_s - imag_m * real_s], axis=0
         )
         prod_high, prod_low = split_pair(product)
-        lagged = (
+        back[k] = (
             dot32(backward[: 2 * rows], prod_high)
             + dot32(backward[: 2 * rows], prod_low)
             + dot32(backward[2 * rows :], prod_high)
         )
-        for group in range(groups):
-            for part in range(2):
-                source = slice(part * rows + group * fine, part * rows + (group + 1) * fine)
-                at = pl.ds(pl.multiple_of(part * FINE_PRODUCT + k * fine, fine), fine)
-                back[group, at, :] = lagged[source, :]
         return carry
 
     lax.fori_loop(0, devices, inner_step, 0, unroll=UNROLL)
@@ -497,7 +505,7 @@
     def advance(t, states):
         result = []
         for p in range(devices):
-            here = jnp.broadcast_to(lined[p, pl.ds(t, 1), :], (modes, LANES))
+            here = jnp.broadcast_to(lined[0, p, pl.ds(t, 1), :], (modes, LANES))
             result.append(decay * states[p] + here)
         return tuple(result)
 
@@ -508,34 +516,33 @@
     carried = jnp.zeros((modes, LANES), jnp.float32)
     for p in range(devices):
         send_high, send_low = split_pair(lead * carried)
-        leads[p, :modes, :] = send_high
-        leads[p, modes:, :] = send_low
+        out[p, rows : rows + modes, :] = send_high
+        out[p, rows + modes : rows + 2 * modes, :] = send_low
         carried = far * carried + ends[p]
-    for line in range(devices):
-        store(line, slice(rows, rows + 2 * modes), leads[line])
-
-    def last_step(group, carry):
-        cos, sin = turns[group, 0], turns[group, 1]
-        real, imag = back[group, :FINE_PRODUCT, :], back[group, FINE_PRODUCT:, :]
-        turned_back = jnp.concatenate([real * cos - imag * sin, real * sin + imag * cos], axis=0)
-        back_high, back_low = split_pair(turned_back)
-        result = (
-            dot32(outer_backward[:FINE_PRODUCT, :], back_high)
-            + dot32(outer_backward[:FINE_PRODUCT, :], back_low)
-            + dot32(outer_backward[FINE_PRODUCT:, :], back_high)
-        ).astype(jnp.bfloat16)
-        at = pl.ds(pl.multiple_of(group * fine, fine), fine)
-        for line in range(devices):
-            store(line, at, result[line * fine : (line + 1) * fine, :])
+
+    def last_step(tile, carry):
+        at = pl.ds(pl.multiple_of(tile * 8, 8), 8)
+        imag_at = pl.ds(pl.multiple_of(rows + tile * 8, 8), 8)
+        values = []
+        for k in range(devices):
+            real, imag = back[k, at, :], back[k, imag_at, :]
+            cos, sin = spin[0, 8 * k : 8 * k + 8, :], spin[1, 8 * k : 8 * k + 8, :]
+            values.append((real * cos - imag * sin, real * sin + imag * cos))
+        for p, (real, imag) in enumerate(fourier(values, 1)):
+            angle = math.pi * p / (2 * devices)
+            plain[p, at, :] = real * (math.cos(angle) / length) - imag * (math.sin(angle) / length)
+        advance_spin()
         return carry
 
-    lax.fori_loop(0, groups, last_step, 0, unroll=4)
+    spin[...] = twist[...]
+    lax.fori_loop(0, tiles, last_step, 0)
+    for p in range(devices):
+        out[p, :rows, :] = plain[p].astype(jnp.bfloat16)
 
 
 def lag_part(where, sources, rate, amplitude, tables, devices):
     rows = sources[0].shape[-2]
     modes = rate.shape[0]
-    groups = rows * devices // FINE_PRODUCT
     height = rows + 2 * modes
     count = len(sources)
     whole = lambda shape: pl.BlockSpec(shape, lambda g, w: (0,) * len(shape))
@@ -555,13 +562,11 @@
             + [whole(table.shape) for table in tables],
             out_specs=whole(out_shape.shape),
             scratch_shapes=[
-                pltpu.VMEM((groups, FINE_PRODUCT, 2 * LANES), jnp.bfloat16),
+                pltpu.VMEM((2, devices, rows, LANES), jnp.float32),
+                pltpu.VMEM((devices, 2 * rows, 2 * LANES), jnp.float32),
+                pltpu.VMEM((devices, 2 * rows, LANES), jnp.float32),
                 pltpu.VMEM((devices, rows, LANES), jnp.float32),
-                pltpu.VMEM((devices, 2 * rows, 2 * LANES), jnp.bfloat16),
-                pltpu.VMEM((devices, 2 * rows, 2 * LANES), jnp.bfloat16),
-                pltpu.VMEM((groups, 2 * FINE_PRODUCT, LANES), jnp.float32),
-                pltpu.VMEM((groups, 2, FINE_PRODUCT, LANES), jnp.float32),
-                pltpu.VMEM((devices, 2 * modes, LANES), jnp.bfloat16),
+                pltpu.VMEM((2, 8 * devices, LANES), jnp.float32),
             ],
         ),
         out_shape=out_shape,
@@ -677,7 +682,10 @@
         proj[rows - HALO :], "seq", [(i, i + 1) for i in range(devices - 1)]
     )
     streams = (proj, before, short_weight, grad_out)
-    (sent,), query_a, mixed_a = mix_streams(where, *streams, 0, 2, devices, True)
+    partly = mix_streams(where, proj, proj, short_weight, grad_out, 0, 2, devices, True)
+    (sent,), query_a, mixed_a = mix_streams(
+        where, *streams, 0, 2, devices, True, top=2 * HALO, earlier=(*partly[0], *partly[1:])
+    )
     arrived = all_to_all(sent)
     parts, query_b, mixed_b = mix_streams(after(where, sent), *streams, 1, 2, devices, False)
     shared = share(parts, devices)
@@ -687,9 +695,11 @@
     amplitude = residues * jnp.sqrt(rates)
     tiles = (modes, channels // LANES, LANES)
     params = (decay.reshape(tiles), amplitude.reshape(tiles), skip.reshape(tiles[1:]))
-    near_a = near_part(mixed_a, *params, 0)
-    shared = after(shared, near_a, tables)
-    moved = spread_out(shared, devices)
+    near_a = near_part(after(mixed_a, tables), *params, 0)
+    close = after(shared[:2], near_a)
+    moved = spread_out(close, devices)
+    distant = after(shared[2:], moved[0])
+    moved += spread_out(distant, devices)
 
     def lags(guard, sources, chunk):
         start = chunk * width + me * LANES
@@ -697,7 +707,7 @@
         lead = lax.dynamic_slice_in_dim(amplitude, start, LANES, 1)
         return lag_part(after(where, guard), sources, rate, lead, tables, devices)
 
-    back_a = lags(shared[0], [arrived], 0)
+    back_a = lags(distant[0], [arrived], 0)
     arrived_a = all_to_all(back_a)
     back_b = lags(back_a, [*shared, *moved], 1)
     arrived_b = all_to_all(back_b)

time: 118 us -> 114 us (0.966)
  Pallas kernels: 62.4 us -> 57.9 us
    pallas_call x2, Pallas kernels: 28.5 us -> 22.8 us  [lag_part(): pl.pallas_call(functools.partial(lag_body, count), grid_spec=pltpu.Prefet...]
    ppermute x6 -> x9, starting transfers between devices: 7.76 us -> 12 us  [swap(): return lax.ppermute(value, 'seq', [(i, i ^ mask) for i in range(devices)])]
    all_to_all x3, starting transfers between devices: 20.2 us -> 16.7 us  [all_to_all(): return lax.all_to_all(sent, 'seq', split_axis=0, concat_axis=0, tiled=True)]
    ppermute x6 -> x9, waiting for transfers between devices: 6.5 us -> 3.42 us  [swap(): return lax.ppermute(value, 'seq', [(i, i ^ mask) for i in range(devices)])]
    all_to_all x3, waiting for transfers between devices: 8.81 us -> 11.7 us  [all_to_all(): return lax.all_to_all(sent, 'seq', split_axis=0, concat_axis=0, tiled=True)]
    pallas_call x2 -> x3, Pallas kernels: 12.7 us -> 15.5 us  [mix_streams(): pl.pallas_call(functools.partial(mix_body, plain, len(earlier)), grid_spe...]
    pallas_call x1, Pallas kernels: 2.86 us -> 1.29 us  [spectral_tables(): pl.pallas_call(lambda earlier, *outs: table_body(devices, rows, *outs), g...]
    unnamed x28 -> x34, local copies, waits for them, and re-layouts: 4.89 us -> 4.81 us
  transfers between devices with their start and end apart: 10 -> 13, of which waited for: 4 -> 4; matrix products, arithmetic and copies ran while one was open for 3% -> 3% of each run, Pallas kernels for 45% -> 46%
where the time goes in v4:
time: 114 us; the launch traced here: 113 us
  Pallas kernels  57.9 us (51%)
  starting transfers between devices  31 us (27%)
  waiting for transfers between devices  15.1 us (13%)
  local copies, waits for them, and re-layouts  6.43 us (6%)
  other arithmetic  1.49 us (1%)
    pallas_call x2, Pallas kernels, lag_part(): pl.pallas_call(functools.partial(lag_body, count), grid_spec=pltpu.Prefet...  22.8 us
    all_to_all x3, starting transfers between devices, all_to_all(): return lax.all_to_all(sent, 'seq', split_axis=0, concat_axis=0, tiled=True)  16.7 us
    pallas_call x3, Pallas kernels, mix_streams(): pl.pallas_call(functools.partial(mix_body, plain, len(earlier)), grid_spe...  15.5 us
    ppermute x9, starting transfers between devices, swap(): return lax.ppermute(value, 'seq', [(i, i ^ mask) for i in range(devices)])  12 us
    all_to_all x3, waiting for transfers between devices, all_to_all(): return lax.all_to_all(sent, 'seq', split_axis=0, concat_axis=0, tiled=True)  11.7 us
    pallas_call x2, Pallas kernels, near_part(): pl.pallas_call(near_body, grid=(1,), in_specs=[pl.BlockSpec((rows, width)...  10.9 us
    pallas_call x2, Pallas kernels, finish_part(): pl.pallas_call(finish_body, grid=(steps,), in_specs=in_specs, out_specs=[...  7.45 us
    unnamed x34, local copies, waits for them, and re-layouts  4.81 us
  transfers between devices with their start and end apart: 13, of which 4 were waited for; matrix products, arithmetic and copies ran while one was open for 3% of the time, Pallas kernels for 46%

profile of v4, /device:TPU:0, one launch (start us, length us, event | category | flops | bytes accessed | tf_op | source)
XLA Modules:
  0.0 112.8 jit_solution(16701317446252990162)
XLA Ops:
  0.6 0.9 slice.39
  1.6 2.4 %collective-permute-start = (bf16[8,12288]{1,0:T(8,128)(2,1)S(1)}, bf16[8,12288]{1,0:T(8,128)(2,1)S(1)}, u32[]{:S(2)}, u32[]{:S(2)}) collective-permute-start(bf16[8,12288]{1,0:T(8,128)(2,1)S(1)} %slice.39), channel_id=1, source_target_pairs={{0,1},{1,2},{2,3},{3,4},{4,5},{5,6},{6,7},{7,8},{8,9},{9,10},{10,1... | collective-permute-start | bytes 589832 | tf_op jit(solution)/shard_map/ppermute | solution.py:681
  4.0 0.6 pad_add_fusion.where
  4.6 6.2 %mix.3 = (bf16[16,128,256]{2,1,0:T(8,128)(2,1)}, f32[128,2048]{1,0:T(8,128)}, bf16[128,2048]{1,0:T(8,128)(2,1)}) custom-call(s32[2]{0:T(128)} %pad_add_fusion.where, bf16[128,12288]{1,0:T(8,128)(2,1)} %value_in.5, bf16[128,12288]{1,0:T(8,128)(2,1)} %value_in.5, bf16[128,12288]{1,0:T(8,128)(2,1)} %value_in.5, bf16[128,12288]{1,0:T(8,128)(2,1)} %value_in.5, ...), custom_call_target="tpu_custom_call" | custom-call | flops 3000000 | bytes 5000000 | tf_op jit(solution)/shard_map/mix/pallas_call | solution.py:311
  10.8 0.0 collective-permute-done.before_q.before_k.before_v
  10.8 0.0 copy-start
  10.9 0.7 copy-done
  11.5 2.8 %mix.4 = (bf16[16,128,256]{2,1,0:T(8,128)(2,1)}, f32[128,2048]{1,0:T(8,128)}, bf16[128,2048]{1,0:T(8,128)(2,1)}) custom-call(s32[2]{0:T(128)} %pad_add_fusion.where, bf16[128,12288]{1,0:T(8,128)(2,1)} %value_in.5, bf16[128,12288]{1,0:T(8,128)(2,1)} %value_in.5, ...), custom_call_target="tpu_custom_call", output_to_operand_aliasing={{0}: (11, {}), {1}: (12, {}), {2}: (13, {})} | custom-call | flops 3000000 | bytes 5000000 | tf_op jit(solution)/shard_map/mix/pallas_call | solution.py:311
  14.3 7.2 %all-to-all-start = ((bf16[16,128,256]{2,1,0:T(8,128)(2,1)}), bf16[16,128,256]{2,1,0:T(8,128)(2,1)S(1)}, u32[]{:S(2)}, u32[]{:S(2)}) async-start(bf16[16,128,256]{2,1,0:T(8,128)(2,1)} %get-tuple-element.34), calls=%async_computation | async-start | bytes 2097152 | tf_op jit(solution)/shard_map/all_to_all | solution.py:671
  21.5 0.0 copy-start.5
  21.6 0.0 copy-start.6
  21.6 6.5 %mix.5 = (bf16[4,128,256]{2,1,0:T(8,128)(2,1)}, bf16[4,128,256]{2,1,0:T(8,128)(2,1)}, bf16[4,128,256]{2,1,0:T(8,128)(2,1)}, bf16[4,128,256]{2,1,0:T(8,128)(2,1)}...) custom-call(s32[2]{0:T(128)} %pad_add_fusion.where, bf16[128,12288]{1,0:T(8,128)(2,1)} %value_in.5, ...), custom_call_target="tpu_custom_call" | custom-call | flops 3000000 | bytes 5000000 | tf_op jit(solution)/shard_map/mix/pallas_call | solution.py:311
  28.0 2.0 %collective-permute-start.1 = (bf16[4,128,256]{2,1,0:T(8,128)(2,1)}, bf16[4,128,256]{2,1,0:T(8,128)(2,1)S(1)}, u32[]{:S(2)}, u32[]{:S(2)}) collective-permute-start(bf16[4,128,256]{2,1,0:T(8,128)(2,1)} %get-tuple-element.36), channel_id=1, source_target_pairs={{0,2},{1,3},{2,0},{3,1},{4,6},{5,7},{6,4},{7,5},{8,10},{9,11},{10,... | collective-permute-start | bytes 786440 | tf_op jit(solution)/shard_map/ppermute | solution.py:652
  30.0 0.0 collective-permute-start.2
  30.0 0.2 collective-permute-start.3
  30.2 0.0 copy-done.5
  30.2 0.0 copy-done.6
  30.2 0.8 negate_exponential_fusion
  31.0 1.3 %tables.1 = (bf16[512,256]{1,0:T(8,128)(2,1)}, bf16[512,256]{1,0:T(8,128)(2,1)}, f32[2,128,128]{2,1,0:T(8,128)}) custom-call(bf16[4,128,256]{2,1,0:T(8,128)(2,1)} %get-tuple-element.48.earlier.refs_0_), custom_call_target="tpu_custom_call" | custom-call | flops 1000 | bytes 1000 | tf_op jit(solution)/shard_map/tables/pallas_call | solution.py:229
  32.3 0.8 copy.13
  33.1 0.8 copy.14
  33.9 5.5 %near.2 = f32[128,2048]{1,0:T(8,128)} custom-call(bf16[128,2048]{1,0:T(8,128)(2,1)} %get-tuple-element.44.mixed, f32[16,32,128]{2,1,0:T(8,128)} %bitcast.8, f32[16,32,128]{2,1,0:T(8,128)} %bitcast.10, f32[32,128]{1,0:T(8,128)} %bitcast.13), custom_call_target="tpu_custom_call" | custom-call | flops 1000 | bytes 1000 | tf_op jit(solution)/shard_map/near/pallas_call | solution.py:379
  39.3 0.6 constant_dynamic-slice_fusion
  39.9 0.0 collective-permute-done.3.refs_1_
  39.9 0.0 copy-done.4
  39.9 0.0 copy-start.9
  40.0 2.0 %collective-permute-start.4 = (bf16[2,128,256]{2,1,0:T(8,128)(2,1)S(1)}, bf16[2,128,256]{2,1,0:T(8,128)(2,1)S(1)}, u32[]{:S(2)}, u32[]{:S(2)}) collective-permute-start(bf16[2,128,256]{2,1,0:T(8,128)(2,1)S(1)} %pad_maximum_fusion), channel_id=1, source_target_pairs={{0,4},{1,5},{2,6},{3,7},{4,0},{5,1},{6,2},{7,3},{8,12},{9,13},{10,... | collective-permute-start | bytes 393224 | tf_op jit(solution)/shard_map/ppermute | solution.py:652
  42.0 2.4 %collective-permute-start.5 = (bf16[2,128,256]{2,1,0:T(8,128)(2,1)S(1)}, bf16[2,128,256]{2,1,0:T(8,128)(2,1)S(1)}, u32[]{:S(2)}, u32[]{:S(2)}) collective-permute-start(bf16[2,128,256]{2,1,0:T(8,128)(2,1)S(1)} %pad_maximum_fusion.1), channel_id=1, source_target_pairs={{0,8},{1,9},{2,10},{3,11},{4,12},{5,13},{6,14},{7,15},{8,0},{9,1},... | collective-permute-start | bytes 393224 | tf_op jit(solution)/shard_map/ppermute | solution.py:652
  44.5 0.2 collective-permute-start.6
  44.6 0.0 collective-permute-done.1.refs_2_
  44.6 3.3 %collective-permute-done.2.refs_3_ = bf16[4,128,256]{2,1,0:T(8,128)(2,1)S(1)} collective-permute-done((bf16[4,128,256]{2,1,0:T(8,128)(2,1)}, bf16[4,128,256]{2,1,0:T(8,128)(2,1)S(1)}, u32[]{:S(2)}, u32[]{:S(2)}) %collective-permute-start.2) | collective-permute-done | bytes 262176 | tf_op jit(solution)/shard_map/ppermute | solution.py:652
  47.9 0.1 collective-permute-done.4.refs_4_
  48.1 2.7 %collective-permute-start.7 = (bf16[2,128,256]{2,1,0:T(8,128)(2,1)S(1)}, bf16[2,128,256]{2,1,0:T(8,128)(2,1)S(1)}, u32[]{:S(2)}, u32[]{:S(2)}) collective-permute-start(bf16[2,128,256]{2,1,0:T(8,128)(2,1)S(1)} %pad_maximum_fusion.3), channel_id=1, source_target_pairs={{0,4},{1,5},{2,6},{3,7},{4,0},{5,1},{6,2},{7,3},{8,12},{9,13},{10,... | collective-permute-start | bytes 393224 | tf_op jit(solution)/shard_map/ppermute | solution.py:652
  50.8 1.8 %collective-permute-start.8 = (bf16[2,128,256]{2,1,0:T(8,128)(2,1)S(1)}, bf16[2,128,256]{2,1,0:T(8,128)(2,1)S(1)}, u32[]{:S(2)}, u32[]{:S(2)}) collective-permute-start(bf16[2,128,256]{2,1,0:T(8,128)(2,1)S(1)} %pad_maximum_fusion.4), channel_id=1, source_target_pairs={{0,8},{1,9},{2,10},{3,11},{4,12},{5,13},{6,14},{7,15},{8,0},{9,1},... | collective-permute-start | bytes 393224 | tf_op jit(solution)/shard_map/ppermute | solution.py:652
  52.6 0.7 collective-permute-start.9
  53.3 0.0 all-to-all-done.refs_0_
  53.3 1.0 copy-done.3
  54.3 11.3 %lags.2 = bf16[16,160,128]{2,1,0:T(8,128)(2,1)} custom-call(s32[2]{0:T(128)} %pad_add_fusion.where, bf16[16,128,256]{2,1,0:T(8,128)(2,1)} %copy-done.3, f32[16,128]{1,0:T(8,128)} %get-tuple-element.82.refs_1_, f32[16,128]{1,0:T(8,128)} %get-tuple-element.64.refs_2_, bf16[512,256]{1,0:T(8,128)(2,1)} %get-tuple-element.41.refs_3_.refs_12_, ...), custom_call_target="tpu_custom_call" | custom-call | flops 60000002048 | bytes 12000000 | tf_op jit(solution)/shard_map/lags/pallas_call | solution.py:555
  65.6 0.0 copy-done.9
  65.6 0.0 copy-done.7
  65.6 0.0 copy-done.8
  65.6 4.8 %all-to-all-start.2 = ((bf16[16,160,128]{2,1,0:T(8,128)(2,1)}), bf16[16,160,128]{2,1,0:T(8,128)(2,1)S(1)}, u32[]{:S(2)}, u32[]{:S(2)}) async-start(bf16[16,160,128]{2,1,0:T(8,128)(2,1)} %lags.2), calls=%async_computation.2 | async-start | bytes 1310720 | tf_op jit(solution)/shard_map/all_to_all | solution.py:671
  70.4 0.0 collective-permute-done.5.refs_5_
  70.4 0.0 copy-start.11
  70.4 0.0 collective-permute-done.6.refs_6_
  70.5 0.0 copy-start.12
  70.5 0.0 collective-permute-done.7.refs_7_
  70.5 0.0 collective-permute-done.8.refs_8_
  70.5 0.0 collective-permute-done.9.refs_9_
  70.5 0.0 copy-start.15
  70.5 0.6 copy-done.11
  71.1 0.0 copy-done.12
  71.1 0.0 copy-done.13
  71.2 0.0 copy-done.14
  71.2 0.0 copy-done.15
  71.3 11.4 %lags.3 = bf16[16,160,128]{2,1,0:T(8,128)(2,1)} custom-call(s32[2]{0:T(128)} %pad_add_fusion.where, bf16[4,128,256]{2,1,0:T(8,128)(2,1)} %get-tuple-element.48.earlier.refs_0_, bf16[4,128,256]{2,1,0:T(8,128)(2,1)} %copy-done.9, bf16[4,128,256]{2,1,0:T(8,128)(2,1)} %copy-done.7, bf16[4,128,256]{2,1,0:T(8,128)(2,1)} %copy-done.8, ...), custom_call_target="tpu_custom_call" | custom-call | flops 60000002048 | bytes 12000000 | tf_op jit(solution)/shard_map/lags/pallas_call | solution.py:555
  82.7 4.3 %all-to-all-done.2.arrived = bf16[16,160,128]{2,1,0:T(8,128)(2,1)S(1)} async-done(((bf16[16,160,128]{2,1,0:T(8,128)(2,1)}), bf16[16,160,128]{2,1,0:T(8,128)(2,1)S(1)}, u32[]{:S(2)}, u32[]{:S(2)}) %all-to-all-start.2) | async-done | bytes 655392 | tf_op jit(solution)/shard_map/all_to_all | solution.py:671
  87.0 4.7 %all-to-all-start.1 = ((bf16[16,160,128]{2,1,0:T(8,128)(2,1)}), bf16[16,160,128]{2,1,0:T(8,128)(2,1)S(1)}, u32[]{:S(2)}, u32[]{:S(2)}) async-start(bf16[16,160,128]{2,1,0:T(8,128)(2,1)} %lags.3), calls=%async_computation.1 | async-start | bytes 1310720 | tf_op jit(solution)/shard_map/all_to_all | solution.py:671
  91.7 5.5 %near.3 = f32[128,2048]{1,0:T(8,128)} custom-call(bf16[128,2048]{1,0:T(8,128)(2,1)} %get-tuple-element.55.mixed, f32[16,32,128]{2,1,0:T(8,128)} %bitcast.9, f32[16,32,128]{2,1,0:T(8,128)} %bitcast.11, f32[32,128]{1,0:T(8,128)} %bitcast.14), custom_call_target="tpu_custom_call" | custom-call | flops 1000 | bytes 1000 | tf_op jit(solution)/shard_map/near/pallas_call | solution.py:379
  97.1 0.0 copy-done.2
  97.2 3.7 %finish.2 = (bf16[128,4096]{1,0:T(8,128)(2,1)}, f32[128,4096]{1,0:T(8,128)}) custom-call(bf16[16,160,128]{2,1,0:T(8,128)(2,1)} %copy-done.2, f32[128,2048]{1,0:T(8,128)} %near.2, f32[128,2048]{1,0:T(8,128)} %get-tuple-element.57.query, f32[16,4096]{1,0:T(8,128)} %get-tuple-element.60.decay), custom_call_target="tpu_custom_call" | custom-call | flops 1000 | bytes 1000 | tf_op jit(solution)/shard_map/finish/pallas_call | solution.py:636
  100.9 7.4 %all-to-all-done.1.arrived = bf16[16,160,128]{2,1,0:T(8,128)(2,1)S(1)} async-done(((bf16[16,160,128]{2,1,0:T(8,128)(2,1)}), bf16[16,160,128]{2,1,0:T(8,128)(2,1)S(1)}, u32[]{:S(2)}, u32[]{:S(2)}) %all-to-all-start.1) | async-done | bytes 655392 | tf_op jit(solution)/shard_map/all_to_all | solution.py:671
  108.2 0.9 copy-done.1
  109.1 3.7 %finish.3 = (bf16[128,4096]{1,0:T(8,128)(2,1)}, f32[128,4096]{1,0:T(8,128)}) custom-call(bf16[16,160,128]{2,1,0:T(8,128)(2,1)} %copy-done.1, f32[128,2048]{1,0:T(8,128)} %near.3, f32[128,2048]{1,0:T(8,128)} %get-tuple-element.56.query, f32[16,4096]{1,0:T(8,128)} %get-tuple-element.60.decay, ...), custom_call_target="tpu_custom_call", output_to_operand_aliasing={{0}: (4, {}), {1}: (5, {})} | custom-call | flops 1000 | bytes 1000 | tf_op jit(solution)/shard_map/finish/pallas_call | solution.py:636
  (19 shorter events, 0.2 us)
Async XLA Ops:
  1.6 9.3 %collective-permute-start = (bf16[8,12288]{1,0:T(8,128)(2,1)S(1)}, bf16[8,12288]{1,0:T(8,128)(2,1)S(1)}, u32[]{:S(2)}, u32[]{:S(2)}) collective-permute-start(bf16[8,12288]{1,0:T(8,128)(2,1)S(1)} %slice.39), channel_id=1, source_target_pairs={{0,1},{1,2},{2,3},{3,4},{4,5},{5,6},{6,7},{7,8},{8,9},{9,10},{10,1... | collective-permute-start | bytes 589832 | tf_op jit(solution)/shard_map/ppermute | solution.py:681
  10.8 0.7 copy-start
  14.3 39.0 %all-to-all-start = ((bf16[16,128,256]{2,1,0:T(8,128)(2,1)}), bf16[16,128,256]{2,1,0:T(8,128)(2,1)S(1)}, u32[]{:S(2)}, u32[]{:S(2)}) async-start(bf16[16,128,256]{2,1,0:T(8,128)(2,1)} %get-tuple-element.34), calls=%async_computation | async-start | bytes 2097152 | tf_op jit(solution)/shard_map/all_to_all | solution.py:671
  21.5 8.7 %copy-start.5 = (f32[16,4096]{1,0:T(8,128)S(1)}, f32[16,4096]{1,0:T(8,128)}, u32[]{:S(2)}) copy-start(f32[16,4096]{1,0:T(8,128)} %param.9) | copy-start | bytes 786436
  21.6 8.7 %copy-start.6 = (f32[16,4096]{1,0:T(8,128)S(1)}, f32[16,4096]{1,0:T(8,128)}, u32[]{:S(2)}) copy-start(f32[16,4096]{1,0:T(8,128)} %param.8) | copy-start | bytes 786436
  28.0 16.6 %collective-permute-start.1 = (bf16[4,128,256]{2,1,0:T(8,128)(2,1)}, bf16[4,128,256]{2,1,0:T(8,128)(2,1)S(1)}, u32[]{:S(2)}, u32[]{:S(2)}) collective-permute-start(bf16[4,128,256]{2,1,0:T(8,128)(2,1)} %get-tuple-element.36), channel_id=1, source_target_pairs={{0,2},{1,3},{2,0},{3,1},{4,6},{5,7},{6,4},{7,5},{8,10},{9,11},{10,... | collective-permute-start | bytes 786440 | tf_op jit(solution)/shard_map/ppermute | solution.py:652
  30.0 17.9 %collective-permute-start.2 = (bf16[4,128,256]{2,1,0:T(8,128)(2,1)}, bf16[4,128,256]{2,1,0:T(8,128)(2,1)S(1)}, u32[]{:S(2)}, u32[]{:S(2)}) collective-permute-start(bf16[4,128,256]{2,1,0:T(8,128)(2,1)} %get-tuple-element.37), channel_id=1, source_target_pairs={{0,3},{1,2},{2,1},{3,0},{4,7},{5,6},{6,5},{7,4},{8,11},{9,10},{10,... | collective-permute-start | bytes 786440 | tf_op jit(solution)/shard_map/ppermute | solution.py:652
  30.0 9.9 %collective-permute-start.3 = (bf16[4,128,256]{2,1,0:T(8,128)(2,1)}, bf16[4,128,256]{2,1,0:T(8,128)(2,1)S(1)}, u32[]{:S(2)}, u32[]{:S(2)}) collective-permute-start(bf16[4,128,256]{2,1,0:T(8,128)(2,1)} %get-tuple-element.39), channel_id=1, source_target_pairs={{0,1},{1,0},{2,3},{3,2},{4,5},{5,4},{6,7},{7,6},{8,9},{9,8},{10,11... | collective-permute-start | bytes 786440 | tf_op jit(solution)/shard_map/ppermute | solution.py:652
  30.2 9.7 %copy-start.4 = (bf16[4,128,256]{2,1,0:T(8,128)(2,1)S(1)}, bf16[4,128,256]{2,1,0:T(8,128)(2,1)}, u32[]{:S(2)}) copy-start(bf16[4,128,256]{2,1,0:T(8,128)(2,1)} %get-tuple-element.48.earlier.refs_0_) | copy-start | bytes 786436
  39.9 25.7 %copy-start.9 = (bf16[4,128,256]{2,1,0:T(8,128)(2,1)}, bf16[4,128,256]{2,1,0:T(8,128)(2,1)S(1)}, u32[]{:S(2)}) copy-start(bf16[4,128,256]{2,1,0:T(8,128)(2,1)S(1)} %collective-permute-done.3.refs_1_) | copy-start | bytes 786436
  40.0 8.0 %collective-permute-start.4 = (bf16[2,128,256]{2,1,0:T(8,128)(2,1)S(1)}, bf16[2,128,256]{2,1,0:T(8,128)(2,1)S(1)}, u32[]{:S(2)}, u32[]{:S(2)}) collective-permute-start(bf16[2,128,256]{2,1,0:T(8,128)(2,1)S(1)} %pad_maximum_fusion), channel_id=1, source_target_pairs={{0,4},{1,5},{2,6},{3,7},{4,0},{5,1},{6,2},{7,3},{8,12},{9,13},{10,... | collective-permute-start | bytes 393224 | tf_op jit(solution)/shard_map/ppermute | solution.py:652
  42.0 28.4 %collective-permute-start.5 = (bf16[2,128,256]{2,1,0:T(8,128)(2,1)S(1)}, bf16[2,128,256]{2,1,0:T(8,128)(2,1)S(1)}, u32[]{:S(2)}, u32[]{:S(2)}) collective-permute-start(bf16[2,128,256]{2,1,0:T(8,128)(2,1)S(1)} %pad_maximum_fusion.1), channel_id=1, source_target_pairs={{0,8},{1,9},{2,10},{3,11},{4,12},{5,13},{6,14},{7,15},{8,0},{9,1},... | collective-permute-start | bytes 393224 | tf_op jit(solution)/shard_map/ppermute | solution.py:652
  44.5 26.0 %collective-permute-start.6 = (bf16[2,128,256]{2,1,0:T(8,128)(2,1)S(1)}, bf16[2,128,256]{2,1,0:T(8,128)(2,1)S(1)}, u32[]{:S(2)}, u32[]{:S(2)}) collective-permute-start(bf16[2,128,256]{2,1,0:T(8,128)(2,1)S(1)} %pad_maximum_fusion.2), channel_id=1, source_target_pairs={{0,12},{1,13},{2,14},{3,15},{4,8},{5,9},{6,10},{7,11},{8,4},{9,5},... | collective-permute-start | bytes 393224 | tf_op jit(solution)/shard_map/ppermute | solution.py:652
  44.6 21.0 %copy-start.7 = (bf16[4,128,256]{2,1,0:T(8,128)(2,1)}, bf16[4,128,256]{2,1,0:T(8,128)(2,1)S(1)}, u32[]{:S(2)}) copy-start(bf16[4,128,256]{2,1,0:T(8,128)(2,1)S(1)} %collective-permute-done.1.refs_2_) | copy-start | bytes 786436
  47.9 17.7 %copy-start.8 = (bf16[4,128,256]{2,1,0:T(8,128)(2,1)}, bf16[4,128,256]{2,1,0:T(8,128)(2,1)S(1)}, u32[]{:S(2)}) copy-start(bf16[4,128,256]{2,1,0:T(8,128)(2,1)S(1)} %collective-permute-done.2.refs_3_) | copy-start | bytes 786436
  48.0 17.6 %copy-start.10 = (bf16[2,128,256]{2,1,0:T(8,128)(2,1)}, bf16[2,128,256]{2,1,0:T(8,128)(2,1)S(1)}, u32[]{:S(2)}) copy-start(bf16[2,128,256]{2,1,0:T(8,128)(2,1)S(1)} %collective-permute-done.4.refs_4_) | copy-start | bytes 393220
  48.1 22.4 %collective-permute-start.7 = (bf16[2,128,256]{2,1,0:T(8,128)(2,1)S(1)}, bf16[2,128,256]{2,1,0:T(8,128)(2,1)S(1)}, u32[]{:S(2)}, u32[]{:S(2)}) collective-permute-start(bf16[2,128,256]{2,1,0:T(8,128)(2,1)S(1)} %pad_maximum_fusion.3), channel_id=1, source_target_pairs={{0,4},{1,5},{2,6},{3,7},{4,0},{5,1},{6,2},{7,3},{8,12},{9,13},{10,... | collective-permute-start | bytes 393224 | tf_op jit(solution)/shard_map/ppermute | solution.py:652
  50.8 19.7 %collective-permute-start.8 = (bf16[2,128,256]{2,1,0:T(8,128)(2,1)S(1)}, bf16[2,128,256]{2,1,0:T(8,128)(2,1)S(1)}, u32[]{:S(2)}, u32[]{:S(2)}) collective-permute-start(bf16[2,128,256]{2,1,0:T(8,128)(2,1)S(1)} %pad_maximum_fusion.4), channel_id=1, source_target_pairs={{0,8},{1,9},{2,10},{3,11},{4,12},{5,13},{6,14},{7,15},{8,0},{9,1},... | collective-permute-start | bytes 393224 | tf_op jit(solution)/shard_map/ppermute | solution.py:652
  52.6 17.9 %collective-permute-start.9 = (bf16[2,128,256]{2,1,0:T(8,128)(2,1)S(1)}, bf16[2,128,256]{2,1,0:T(8,128)(2,1)S(1)}, u32[]{:S(2)}, u32[]{:S(2)}) collective-permute-start(bf16[2,128,256]{2,1,0:T(8,128)(2,1)S(1)} %pad_maximum_fusion.5), channel_id=1, source_target_pairs={{0,12},{1,13},{2,14},{3,15},{4,8},{5,9},{6,10},{7,11},{8,4},{9,5},... | collective-permute-start | bytes 393224 | tf_op jit(solution)/shard_map/ppermute | solution.py:652
  53.3 1.0 copy-start.3
  65.6 21.3 %all-to-all-start.2 = ((bf16[16,160,128]{2,1,0:T(8,128)(2,1)}), bf16[16,160,128]{2,1,0:T(8,128)(2,1)S(1)}, u32[]{:S(2)}, u32[]{:S(2)}) async-start(bf16[16,160,128]{2,1,0:T(8,128)(2,1)} %lags.2), calls=%async_computation.2 | async-start | bytes 1310720 | tf_op jit(solution)/shard_map/all_to_all | solution.py:671
  70.4 0.7 copy-start.11
  70.5 0.7 copy-start.12
  70.5 0.7 copy-start.13
  70.5 0.7 copy-start.14
  70.5 0.7 copy-start.15
  87.0 10.2 %copy-start.2 = (bf16[16,160,128]{2,1,0:T(8,128)(2,1)}, bf16[16,160,128]{2,1,0:T(8,128)(2,1)S(1)}, u32[]{:S(2)}) copy-start(bf16[16,160,128]{2,1,0:T(8,128)(2,1)S(1)} %all-to-all-done.2.arrived) | copy-start | bytes 1966084
  87.0 21.3 %all-to-all-start.1 = ((bf16[16,160,128]{2,1,0:T(8,128)(2,1)}), bf16[16,160,128]{2,1,0:T(8,128)(2,1)S(1)}, u32[]{:S(2)}, u32[]{:S(2)}) async-start(bf16[16,160,128]{2,1,0:T(8,128)(2,1)} %lags.3), calls=%async_computation.1 | async-start | bytes 1310720 | tf_op jit(solution)/shard_map/all_to_all | solution.py:671
  108.2 0.9 copy-start.1
